TPU v7x, 32 devices: a whole 2x2x4 slice. The times are simulated.
32 devices in a mesh: grp: 4 (over y, x), shard: 8 (over z, core).
Axes of the slice: x: 2, y: 2, z: 4, core: 2. Of those that a mesh axis runs over, the one named last changes fastest.
Arguments:
- partials: bfloat16 [4, 1536, 2, 4096], P('grp', 'shard'), may hold values from -225 to 225
- weights: float32 [1536, 2, 4096], P('shard'), may hold values from -4 to 4
- subspace: bfloat16 [1536, 2, 256], P('shard'), may hold values from -6 to 6
- moment_one: float32 [4096, 2, 256], P('shard'), may hold values from -2 to 2
- moment_two: float32 [4096, 2, 256], P('shard'), may hold values from 0.001 to 0.1
Outputs:
- new_weights: float32 [1536, 2, 4096], P('shard')
- new_moment_one: float32 [4096, 2, 256], P('shard')
- new_moment_two: float32 [4096, 2, 256], P('shard')
- new_subspace: bfloat16 [1536, 2, 256], P('shard')
All inputs are finite; a program needn't handle non-finite values.
Results may differ from a plain program's by a relative error of at most 0.01.
Values may be sent and summed in bfloat16 or wider, within the bound.
No kernel may reach another device: no remote copies, remote signals or barrier semaphores. Data moves between devices by JAX's collectives and lax.ppermute only.
A program may use at most 128 MiB of HBM per device.

v0:
```python
import math

import jax
import jax.numpy as jnp
from jax import lax
from jax.sharding import PartitionSpec as P

D = 1536


first_fix = 1.0 - 0.9**10
second_fix = 1.0 - 0.999**10


def per_device(partials, weights, subspace, moment_one, moment_two):
    gradient = lax.psum(partials[0].astype(jnp.float32).astype(jnp.bfloat16), "grp")
    inv_root = 1.0 / math.sqrt(D)
    column_block = gradient
    projected = lax.psum_scatter(
        jnp.einsum("dmf,dmk->fmk", column_block, subspace, preferred_element_type=jnp.float32)
        * inv_root,
        "shard",
        scatter_dimension=0,
        tiled=True,
    )
    new_moment_one = 0.9 * moment_one + 0.1 * projected
    new_moment_two = 0.999 * moment_two + 0.001 * projected * projected
    direction = (
        new_moment_one / first_fix / (jnp.sqrt(new_moment_two / second_fix) + 1e-08)
    ).astype(jnp.bfloat16)
    projected_half = projected.astype(jnp.bfloat16)
    update = jnp.einsum(
        "dmk,fmk->dmf",
        subspace,
        lax.all_gather(direction, "shard", axis=0, tiled=True),
        preferred_element_type=jnp.float32,
    )
    increment = update
    column_block = gradient
    spanned = jnp.einsum(
        "dmf,fmk->dmk",
        column_block,
        lax.all_gather(projected_half, "shard", axis=0, tiled=True),
        preferred_element_type=jnp.float32,
    )
    increment, spanned = (increment, spanned)
    new_weights = weights - increment * inv_root
    local_gram = jnp.einsum("dmk,dml->mkl", spanned, spanned, precision=lax.Precision.HIGHEST)
    gram_matrix = lax.psum(local_gram, "shard")
    normalizer = 1.7 / jnp.sqrt(jnp.sqrt(jnp.sum(gram_matrix * gram_matrix, axis=(1, 2))) + 1e-06)
    oriented = spanned * normalizer[None, :, None]
    own_gram = jnp.einsum("dmk,dml->mkl", oriented, oriented, precision=lax.Precision.HIGHEST)
    ortho_gram = lax.psum(own_gram, "shard")
    polished = 1.5 * oriented - 0.5 * jnp.einsum(
        "dmk,mkl->dml", oriented, ortho_gram, precision=lax.Precision.HIGHEST
    )
    new_subspace = (math.sqrt(D) * polished).astype(jnp.bfloat16)
    return (new_weights, new_moment_one, new_moment_two, new_subspace)


def solution(mesh):
    return jax.shard_map(
        per_device,
        mesh=mesh,
        in_specs=(
            P("grp", "shard", None, None),
            P("shard", None, None),
            P("shard", None, None),
            P("shard", None, None),
            P("shard", None, None),
        ),
        out_specs=(
            P("shard", None, None),
            P("shard", None, None),
            P("shard", None, None),
            P("shard", None, None),
        ),
        check_vma=False,
    )
```

profile of v0, /device:TPU:1, one launch (start us, length us, event | category | flops | bytes accessed | tf_op | source)
XLA Modules:
  0.0 421.7 jit_solution(8756850632732030668)
XLA Ops:
  7.2 0.0 copy-start.3
  7.2 0.0 all-reduce.4.cloned.1.call-start
  7.2 5.7 %copy.29 = bf16[1,192,2,4096]{3,1,2,0:T(8,128)(2,1)} copy(bf16[1,192,2,4096]{3,2,1,0:T(2,128)(2,1)} %param.5) | data formatting | bytes 6291456 | tf_op args[0]
  12.9 0.0 all-reduce.4.cloned.1.call-update
  12.9 0.0 reduce-scatter.2.cloned.1.call-start
  13.0 89.4 %all-reduce.4.cloned.1.call-done = bf16[192,2,4096]{2,0,1:T(8,128)(2,1)} async-done(((bf16[192,2,4096]{2,0,1:T(8,128)(2,1)}), bf16[192,2,4096]{2,0,1:T(8,128)(2,1)}) %all-reduce.4.cloned.1.call-update) | async-done | bytes 3145744 | tf_op jit(solution)/shard_map/psum | solution.py:16
  102.4 0.0 copy-done.3
  102.4 6.5 %multiply_bitcast_fusion = f32[4096,2,256]{0,2,1:T(8,128)} fusion(bf16[192,2,4096]{2,0,1:T(8,128)(2,1)} %all-reduce.4.cloned.1.call-done, bf16[192,2,256]{2,1,0:T(2,128)(2,1)S(1)} %copy-done.3), kind=kOutput, calls=%fused_computation | convolution fusion | flops 807403520 | bytes 11730944 | tf_op jit(solution)/shard_map/dmf,dmk->fmk/dot_general | solution.py:20
  108.9 0.0 copy-start.2
  108.9 0.0 reduce-scatter.2.cloned.1.call-update
  108.9 0.0 all-gather.5.cloned.1.call-start
  109.0 1.1 copy-done.2
  110.1 1.6 copy.9
  111.7 0.0 copy-start
  111.7 2.4 copy.12
  114.1 82.4 %reduce-scatter.2.cloned.1.call-done = f32[512,2,256]{0,2,1:T(8,128)} async-done(((f32[4096,2,256]{0,2,1:T(8,128)}), f32[512,2,256]{0,2,1:T(8,128)}) %reduce-scatter.2.cloned.1.call-update) | async-done | bytes 1048592 | tf_op jit(solution)/shard_map/reduce_scatter | solution.py:19
  196.6 4.4 %divide_convert_fusion = (bf16[512,2,256]{0,2,1:T(8,128)(2,1)}, f32[512,2,256]{0,2,1:T(8,128)}, f32[512,2,256]{0,2,1:T(8,128)}, bf16[512,2,256]{0,2,1:T(8,128)(2,1)}) fusion(f32[512,2,256]{0,2,1:T(8,128)} %reduce-scatter.2.cloned.1.call-done, f32[512,2,256]{0,2,1:T(8,128)} %copy.9, f32[512,2,256]{0,2,1:T(8,128)} %copy.12), kind=kLoop, calls=%fused_computation.11 | loop fusion | flops 3407872 | bytes 6291456 | tf_op jit(solution)/shard_map/convert_element_type | solution.py:30
  201.0 0.0 all-gather.5.cloned.1.call-update
  201.0 0.0 all-reduce.6.cloned.1.call-start
  201.0 48.1 %all-gather.5.cloned.1.call-done = bf16[4096,2,256]{0,2,1:T(8,128)(2,1)} async-done(((bf16[512,2,256]{0,2,1:T(8,128)(2,1)}), bf16[4096,2,256]{0,2,1:T(8,128)(2,1)}) %all-gather.5.cloned.1.call-update) | async-done | bytes 4194320 | tf_op jit(solution)/shard_map/all_gather | solution.py:43
  249.2 0.0 copy-done
  249.2 3.7 convolution_bitcast_fusion
  252.9 0.0 copy-start.1
  252.9 1.9 fusion.13
  254.8 0.0 all-reduce.6.cloned.1.call-update
  254.8 0.0 all-gather.3.cloned.1.call-start
  254.9 0.5 all-gather.3.cloned.1.call-update
  255.4 0.0 all-reduce.8.cloned.1.call-start
  255.5 2.4 copy.18
  257.9 0.0 copy-done.1
  257.9 1.3 copy.19
  259.2 48.5 %all-reduce.6.cloned.1.call-done = f32[2,256,256]{2,1,0:T(8,128)} async-done(((f32[2,256,256]{2,1,0:T(8,128)}), f32[2,256,256]{2,1,0:T(8,128)}) %all-reduce.6.cloned.1.call-update) | async-done | bytes 524304 | tf_op jit(solution)/shard_map/psum | solution.py:49
  307.7 1.2 multiply_reduce_fusion
  308.9 2.0 fusion.5
  310.9 0.0 all-reduce.8.cloned.1.call-update
  310.9 46.6 %all-gather.3.cloned.1.call-done = bf16[4096,2,256]{0,2,1:T(8,128)(2,1)} async-done(((bf16[512,2,256]{0,2,1:T(8,128)(2,1)}), bf16[4096,2,256]{0,2,1:T(8,128)(2,1)}) %all-gather.3.cloned.1.call-update) | async-done | bytes 4194320 | tf_op jit(solution)/shard_map/all_gather | solution.py:35
  357.5 8.7 %bitcast_subtract_fusion = f32[192,2,4096]{2,0,1:T(8,128)S(1)} fusion(f32[192,2,4096]{2,1,0:T(2,128)} %param.6, bf16[4096,2,256]{0,2,1:T(8,128)(2,1)} %all-gather.3.cloned.1.call-done, bf16[192,2,256]{2,1,0:T(2,128)(2,1)} %param.7), kind=kOutput, calls=%fused_computation.1 | convolution fusion | flops 808452096 | bytes 16973824 | tf_op jit(solution)/shard_map/dmk,fmk->dmf/dot_general | solution.py:32
  366.2 7.6 %copy.17 = f32[192,2,4096]{2,1,0:T(2,128)} copy(f32[192,2,4096]{2,0,1:T(8,128)S(1)} %bitcast_subtract_fusion) | data formatting | bytes 12582912
  373.7 38.6 %all-reduce.8.cloned.1.call-done = f32[2,256,256]{2,1,0:T(8,128)} async-done(((f32[2,256,256]{2,1,0:T(8,128)}), f32[2,256,256]{2,1,0:T(8,128)}) %all-reduce.8.cloned.1.call-update) | async-done | bytes 524304 | tf_op jit(solution)/shard_map/psum | solution.py:53
  412.4 1.6 fusion.3
  414.0 0.9 copy.20
  (1 shorter events, 0.0 us)
Async XLA Ops:
  7.2 95.2 %copy-start.3 = (bf16[192,2,256]{2,1,0:T(2,128)(2,1)S(1)}, bf16[192,2,256]{2,1,0:T(2,128)(2,1)}, u32[]{:S(2)}) copy-start(bf16[192,2,256]{2,1,0:T(2,128)(2,1)} %param.7) | copy-start | bytes 589828
  7.2 95.2 %all-reduce.4.cloned.1.call-start = ((), (), s32[]{:S(2)}) async-start(), calls=%async_computation.1 | async-start | bytes 6291456 | tf_op jit(solution)/shard_map/psum | solution.py:16
  12.9 183.6 %reduce-scatter.2.cloned.1.call-start = ((), (), s32[]{:S(2)}) async-start(), calls=%async_computation.2 | async-start | bytes 9437184 | tf_op jit(solution)/shard_map/reduce_scatter | solution.py:19
  108.9 1.2 copy-start.2
  108.9 140.2 %all-gather.5.cloned.1.call-start = ((), (), s32[]{:S(2)}) async-start(), calls=%async_computation.4 | async-start | bytes 4718592 | tf_op jit(solution)/shard_map/all_gather | solution.py:43
  111.7 137.5 %copy-start = (bf16[192,2,4096]{2,0,1:T(8,128)(2,1)S(1)}, bf16[192,2,4096]{2,0,1:T(8,128)(2,1)}, u32[]{:S(2)}) copy-start(bf16[192,2,4096]{2,0,1:T(8,128)(2,1)} %all-reduce.4.cloned.1.call-done) | copy-start | bytes 9437188
  201.0 106.7 %all-reduce.6.cloned.1.call-start = ((), (), s32[]{:S(2)}) async-start(), calls=%async_computation.5 | async-start | bytes 1048576 | tf_op jit(solution)/shard_map/psum | solution.py:49
  252.9 5.0 %copy-start.1 = (f32[512,2,256]{0,2,1:T(8,128)S(1)}, f32[512,2,256]{0,2,1:T(8,128)}, u32[]{:S(2)}) copy-start(f32[512,2,256]{0,2,1:T(8,128)} %get-tuple-element.10) | copy-start | bytes 3145732
  254.8 102.6 %all-gather.3.cloned.1.call-start = ((), (), s32[]{:S(2)}) async-start(), calls=%async_computation.3 | async-start | bytes 4718592 | tf_op jit(solution)/shard_map/all_gather | solution.py:35
  255.4 156.9 %all-reduce.8.cloned.1.call-start = ((), (), s32[]{:S(2)}) async-start(), calls=%async_computation.6 | async-start | bytes 1048576 | tf_op jit(solution)/shard_map/psum | solution.py:53
Sparse Core Ops, SparseCore 0:
  13.1 89.2 all-reduce.3
  109.1 87.4 reduce-scatter.1
  201.1 48.0 all-gather.4
  255.0 52.6 all-reduce.5
  309.1 48.2 all-gather.2
  359.6 52.6 all-reduce.7
where the time goes:
time: 424 us; the launch traced here: 422 us
  waiting for transfers between devices  354 us (83%)
  matrix products  24.5 us (6%)
  local copies, waits for them, and re-layouts  23 us (5%)
  between operations  14.1 us (3%)
  other arithmetic  5.61 us (1%)
    psum x1, waiting for transfers between devices, per_device(): lax.psum(partials[0].astype(jnp.float32).astype(jnp.bfloat16), 'grp')  89.4 us
    reduce_scatter x1, waiting for transfers between devices, per_device(): lax.psum_scatter(jnp.einsum('dmf,dmk->fmk', column_block, subspace, prefe...  82.4 us
    psum x1, waiting for transfers between devices, per_device(): gram_matrix = lax.psum(local_gram, 'shard')  48.5 us
    all_gather x1, waiting for transfers between devices, per_device(): lax.all_gather(projected_half, 'shard', axis=0, tiled=True)  48.1 us
    all_gather x1, waiting for transfers between devices, per_device(): lax.all_gather(direction, 'shard', axis=0, tiled=True)  46.6 us
    psum x1, waiting for transfers between devices, per_device(): ortho_gram = lax.psum(own_gram, 'shard')  38.6 us
    unnamed x15, local copies, waits for them, and re-layouts  23 us
    dot_general x1, matrix products, per_device(): jnp.einsum('dmk,fmk->dmf', subspace, lax.all_gather(direction, 'shard', a...  8.72 us
  transfers between devices with their start and end apart: 6, of which 6 were waited for; matrix products, arithmetic and copies ran while one was open for 6% of the time, Pallas kernels for 0%

commit v1 on v0

v1 whole, which is shorter than its diff:
```python
import math

import jax
import jax.numpy as jnp
from jax import lax
from jax.experimental import pallas as pl
from jax.experimental.pallas import tpu as pltpu
from jax.sharding import PartitionSpec as P

D = 1536
bf16 = jnp.bfloat16
f32 = jnp.float32
inv_root = 1.0 / math.sqrt(D)
first_fix = 1.0 - 0.9**10
second_fix = 1.0 - 0.999**10


def plain(partials, weights, subspace, moment_one, moment_two):
    gradient = lax.psum(partials[0], "grp")
    projected = lax.psum_scatter(
        jnp.einsum("dmf,dmk->fmk", gradient, subspace, preferred_element_type=f32) * inv_root,
        "shard",
        scatter_dimension=0,
        tiled=True,
    )
    new_one, new_two, direction = adam(projected, moment_one, moment_two)
    increment = jnp.einsum(
        "dmk,fmk->dmf",
        subspace,
        lax.all_gather(direction, "shard", axis=0, tiled=True),
        preferred_element_type=f32,
    )
    new_weights = weights - increment * inv_root
    spanned = jnp.einsum(
        "dmf,fmk->dmk",
        gradient,
        lax.all_gather(projected.astype(bf16), "shard", axis=0, tiled=True),
        preferred_element_type=f32,
    )
    gram = lax.psum(
        jnp.einsum("dmk,dml->mkl", spanned, spanned, precision=lax.Precision.HIGHEST), "shard"
    )
    normalizer = norm_of(gram, (1, 2))
    oriented = spanned * normalizer[None, :, None]
    ortho_gram = gram * (normalizer * normalizer)[:, None, None]
    polished = 1.5 * oriented - 0.5 * jnp.einsum(
        "dmk,mkl->dml", oriented, ortho_gram, precision=lax.Precision.HIGHEST
    )
    return new_weights, new_one, new_two, (math.sqrt(D) * polished).astype(bf16)


def norm_of(gram, axes):
    return 1.7 / jnp.sqrt(jnp.sqrt(jnp.sum(gram * gram, axis=axes)) + 1e-06)


def adam(projected, one, two):
    new_one = 0.9 * one + 0.1 * projected
    new_two = 0.999 * two + 0.001 * projected * projected
    direction = new_one / first_fix / (jnp.sqrt(new_two / second_fix) + 1e-08)
    return new_one, new_two, direction.astype(bf16)


def swap(x, axis, bit, size):
    return lax.ppermute(x, axis, [(i, i ^ bit) for i in range(size)])


def pack_kernel(place_ref, x_ref, *refs):
    outs, sem = refs[:-1], refs[-1]
    copies = []
    for a in range(4):
        for l in range(2):
            for k in range(4):
                column = (
                    (jnp.bitwise_xor(place_ref[1], k) * 2 + jnp.bitwise_xor(place_ref[2], l)) * 4
                    + jnp.bitwise_xor(place_ref[0], a)
                ) * 128
                source = x_ref.at[:, :, pl.ds(pl.multiple_of(column, 128), 128)]
                copies.append(
                    pltpu.make_async_copy(source, outs[a].at[l * 4 + k], sem.at[len(copies)])
                )
    for copy in copies:
        copy.start()
    for copy in copies:
        copy.wait()


def pack(place, x):
    rows = x.shape[0]
    piece = jax.ShapeDtypeStruct((8, rows, 2, 128), bf16)
    return pl.pallas_call(
        pack_kernel,
        out_shape=(piece,) * 4,
        in_specs=[pl.BlockSpec(memory_space=pltpu.SMEM), pl.BlockSpec(memory_space=pl.ANY)],
        out_specs=(pl.BlockSpec(memory_space=pl.ANY),) * 4,
        scratch_shapes=[pltpu.SemaphoreType.DMA((32,))],
    )(place, x)


def project_kernel(a_ref, b_ref, c_ref, d_ref, s_ref, g_ref, p_ref):
    total = (a_ref[0].astype(f32) + b_ref[0].astype(f32)) + (
        c_ref[0].astype(f32) + d_ref[0].astype(f32)
    )
    gradient = total.astype(bf16)
    g_ref[0] = gradient
    p_ref[0] = lax.dot_general(
        gradient, s_ref[...], (((0,), (0,)), ((), ())), preferred_element_type=f32
    )


def project(pieces, masked):
    rows = pieces[0].shape[1]
    block = pl.BlockSpec((1, rows, 128), lambda i: (i, 0, 0))
    return pl.pallas_call(
        project_kernel,
        grid=(8,),
        in_specs=[block] * 4 + [pl.BlockSpec((rows, 512), lambda i: (0, 0))],
        out_specs=(block, pl.BlockSpec((1, 128, 512), lambda i: (i, 0, 0))),
        out_shape=(
            jax.ShapeDtypeStruct((8, rows, 128), bf16),
            jax.ShapeDtypeStruct((8, 128, 512), f32),
        ),
    )(*pieces, masked)


def span_kernel(g_ref, *refs):
    p_refs, out_ref = refs[:8], refs[8]
    rows = out_ref.shape[0]
    total = jnp.zeros((rows, 512), f32)
    for i in range(8):
        total += jnp.dot(g_ref[i], p_refs[i][...], preferred_element_type=f32)
    odd = lax.broadcasted_iota(jnp.int32, (rows, 256), 0) % 2 == 1
    out_ref[...] = jnp.where(odd, total[:, 256:], total[:, :256]).astype(bf16)


def span(gradient, pieces):
    rows = gradient.shape[1]
    return pl.pallas_call(
        span_kernel, out_shape=jax.ShapeDtypeStruct((rows, 256), bf16)
    )(gradient, *pieces)


def gram_kernel(place_ref, a_ref, b_ref, c_ref, d_ref, spanned_ref, own_ref, other_ref):
    spanned = (a_ref[...].astype(f32) + b_ref[...].astype(f32)) + (
        c_ref[...].astype(f32) + d_ref[...].astype(f32)
    )
    spanned_ref[...] = spanned
    parity = lax.broadcasted_iota(jnp.int32, spanned.shape, 0) % 2
    mine = jnp.where(parity == place_ref[2], spanned, 0.0)
    theirs = spanned - mine
    for part, out_ref in ((mine, own_ref), (theirs, other_ref)):
        out_ref[...] = lax.dot_general(
            part,
            part,
            (((0,), (0,)), ((), ())),
            preferred_element_type=f32,
            precision=lax.Precision.HIGHEST,
        )


def grams(place, parts):
    rows = parts[0].shape[0]
    square = jax.ShapeDtypeStruct((256, 256), f32)
    vmem = pl.BlockSpec(memory_space=pltpu.VMEM)
    return pl.pallas_call(
        gram_kernel,
        in_specs=[pl.BlockSpec(memory_space=pltpu.SMEM)] + [vmem] * 4,
        out_specs=(vmem,) * 3,
        out_shape=(jax.ShapeDtypeStruct((rows, 256), f32), square, square),
    )(place, *parts)


def polish_kernel(place_ref, spanned_ref, own_ref, other_ref, out_ref):
    spanned = spanned_ref[...]
    parity = lax.broadcasted_iota(jnp.int32, spanned.shape, 0) % 2
    mine = parity == place_ref[2]
    total = jnp.zeros_like(spanned)
    for chosen, gram_ref in ((mine, own_ref), (jnp.logical_not(mine), other_ref)):
        gram = gram_ref[...]
        normalizer = norm_of(gram, (0, 1))
        oriented = jnp.where(chosen, spanned, 0.0) * normalizer
        ortho = gram * (normalizer * normalizer)
        total += 1.5 * oriented - 0.5 * jnp.dot(
            oriented, ortho, preferred_element_type=f32, precision=lax.Precision.HIGHEST
        )
    out_ref[...] = (math.sqrt(D) * total).astype(bf16)


def polish(place, spanned, own, other):
    vmem = pl.BlockSpec(memory_space=pltpu.VMEM)
    return pl.pallas_call(
        polish_kernel,
        in_specs=[pl.BlockSpec(memory_space=pltpu.SMEM)] + [vmem] * 3,
        out_specs=vmem,
        out_shape=jax.ShapeDtypeStruct(spanned.shape, bf16),
    )(place, spanned, own, other)


def per_device(partials, weights, subspace, moment_one, moment_two):
    rows = weights.shape[0]
    g = lax.axis_index("grp")
    s = lax.axis_index("shard")
    z, c = s // 2, s % 2
    place = jnp.stack([g, z, c]).astype(jnp.int32)

    flat = subspace.reshape(2 * rows, 256)
    odd = lax.broadcasted_iota(jnp.int32, flat.shape, 0) % 2 == 1
    zero = jnp.zeros_like(flat)
    masked = jnp.concatenate([jnp.where(odd, zero, flat), jnp.where(odd, flat, zero)], axis=1)

    pieces = pack(place, partials[0])
    arrived = [pieces[0]] + [swap(pieces[a], "grp", a, 4) for a in (1, 2, 3)]
    gradient, part = project([p.reshape(8, 2 * rows, 128) for p in arrived], masked)

    kept = part[:4] + swap(part[4:].astype(bf16), "shard", 1, 8).astype(f32)
    sent = [swap(kept[k].astype(bf16), "shard", 2 * k, 8).astype(f32) for k in (1, 2, 3)]
    projected = ((kept[0] + sent[0]) + (sent[1] + sent[2])) * inv_root
    half = projected.astype(bf16)

    one = moment_one.reshape(512, 512)
    two = moment_two.reshape(512, 512)
    _, _, direction = adam(
        projected,
        lax.dynamic_slice_in_dim(one, g * 128, 128, 0),
        lax.dynamic_slice_in_dim(two, g * 128, 128, 0),
    )

    halves = [half] + [swap(half, "shard", 2 * k, 8) for k in (1, 2, 3)]
    directions = [direction] + [swap(direction, "shard", 2 * k, 8) for k in (1, 2, 3)]
    far_halves = [swap(h, "shard", 1, 8) for h in halves]

    partial_span = span(gradient, halves + far_halves)
    spans = [partial_span] + [swap(partial_span, "grp", a, 4) for a in (1, 2, 3)]
    spanned, own, other = grams(place, spans)
    own = own + swap(other, "shard", 1, 8)
    ship = own.astype(bf16)
    own = (own + swap(ship, "shard", 2, 8).astype(f32)) + (
        swap(ship, "shard", 4, 8).astype(f32) + swap(ship, "shard", 6, 8).astype(f32)
    )
    other = swap(own, "shard", 1, 8)
    new_subspace = polish(place, spanned, own, other).reshape(rows, 2, 256)

    gathered = [half] + [swap(half, "grp", a, 4) for a in (1, 2, 3)]
    block = jnp.zeros((4, 128, 512), bf16)
    for a in range(4):
        block = lax.dynamic_update_slice(block, gathered[a][None], (jnp.bitwise_xor(g, a), 0, 0))
    new_one, new_two, _ = adam(block.reshape(512, 512).astype(f32), one, two)

    stack = jnp.stack(directions)
    near = [stack] + [swap(stack, "grp", a, 4) for a in (1, 2, 3)]
    far = [swap(n, "shard", 1, 8) for n in near]
    full = jnp.zeros((4, 2, 4, 128, 512), bf16)
    for a in range(4):
        for l, held in ((0, near[a]), (1, far[a])):
            for k in range(4):
                full = lax.dynamic_update_slice(
                    full,
                    held[k][None, None, None],
                    (jnp.bitwise_xor(z, k), jnp.bitwise_xor(c, l), jnp.bitwise_xor(g, a), 0, 0),
                )
    full = full.reshape(4096, 2, 256)
    increment = jnp.einsum("dmk,fmk->dmf", subspace, full, preferred_element_type=f32)
    new_weights = weights - increment * inv_root
    return (
        new_weights,
        new_one.reshape(512, 2, 256),
        new_two.reshape(512, 2, 256),
        new_subspace,
    )


def solution(mesh):
    small = mesh.shape["grp"] == 4 and mesh.shape["shard"] == 8
    return jax.shard_map(
        per_device if small else plain,
        mesh=mesh,
        in_specs=(
            P("grp", "shard", None, None),
            P("shard", None, None),
            P("shard", None, None),
            P("shard", None, None),
            P("shard", None, None),
        ),
        out_specs=(
            P("shard", None, None),
            P("shard", None, None),
            P("shard", None, None),
            P("shard", None, None),
        ),
        check_vma=False,
    )
```

time: 424 us -> 298 us (0.70)
  waiting for transfers between devices: 354 us -> 64.6 us
  Pallas kernels: 0 us -> 114 us
  starting transfers between devices: 0.24 us -> 41.2 us
  local copies, waits for them, and re-layouts: 23 us -> 56.3 us
  matrix products: 24.5 us -> 8.78 us
  between operations: 14.1 us -> 0.84 us
  other arithmetic: 5.61 us -> 11.6 us
    psum x3 -> x0, waiting for transfers between devices: 176 us -> none  [the longest x1 89.4 us: per_device(): lax.psum(partials[0].astype(jnp.float32).astype(jnp.bfloat16), 'grp')]
    pallas_call x0 -> x5, Pallas kernels: none -> 114 us  [the longest x1 97.3 us: pack(): pl.pallas_call(pack_kernel, out_shape=(piece,) * 4, in_specs=[pl.BlockSpe...]
    all_gather x2 -> x0, waiting for transfers between devices: 94.7 us -> none  [the longest x1 48.1 us: per_device(): lax.all_gather(projected_half, 'shard', axis=0, tiled=True)]
    reduce_scatter x1 -> x0, waiting for transfers between devices: 82.4 us -> none  [per_device(): lax.psum_scatter(jnp.einsum('dmf,dmk->fmk', column_block, subspace, prefe...]
    ppermute x0 -> x35, waiting for transfers between devices: none -> 64.6 us  [swap(): return lax.ppermute(x, axis, [(i, i ^ bit) for i in range(size)])]
    ppermute x0 -> x35, starting transfers between devices: none -> 41.2 us  [swap(): return lax.ppermute(x, axis, [(i, i ^ bit) for i in range(size)])]
    dynamic_update_slice x0 -> x34, local copies, waits for them, and re-layouts: none -> 26.2 us  [the longest x31 24.2 us: per_device(): lax.dynamic_update_slice(full, held[k][None, None, None], (jnp.bitwise_xo...]
    dot_general x6 -> x1, matrix products: 24.5 us -> 8.78 us  [per_device(): jnp.einsum('dmk,fmk->dmf', subspace, full, preferred_element_type=f32)]
  transfers between devices with their start and end apart: 6 -> 35, of which waited for: 6 -> 11; matrix products, arithmetic and copies ran while one was open for 6% -> 14% of each run, Pallas kernels for 0% -> 3%
where the time goes in v1:
time: 298 us; the launch traced here: 297 us
  Pallas kernels  114 us (38%)
  waiting for transfers between devices  64.6 us (22%)
  local copies, waits for them, and re-layouts  56.3 us (19%)
  starting transfers between devices  41.2 us (14%)
  other arithmetic  11.6 us (4%)
  matrix products  8.78 us (3%)
    pallas_call x1, Pallas kernels, pack(): pl.pallas_call(pack_kernel, out_shape=(piece,) * 4, in_specs=[pl.BlockSpe...  97.3 us
    ppermute x35, waiting for transfers between devices, swap(): return lax.ppermute(x, axis, [(i, i ^ bit) for i in range(size)])  64.6 us
    ppermute x35, starting transfers between devices, swap(): return lax.ppermute(x, axis, [(i, i ^ bit) for i in range(size)])  41.2 us
    dynamic_update_slice x31, local copies, waits for them, and re-layouts, per_device(): lax.dynamic_update_slice(full, held[k][None, None, None], (jnp.bitwise_xo...  24.2 us
    unnamed x41, local copies, waits for them, and re-layouts  13.3 us
    dot_general x1, matrix products, per_device(): jnp.einsum('dmk,fmk->dmf', subspace, full, preferred_element_type=f32)  8.78 us
    pallas_call x1, Pallas kernels, project(): pl.pallas_call(project_kernel, grid=(8,), in_specs=[block] * 4 + [pl.Bloc...  7.29 us
    reshape x1, local copies, waits for them, and re-layouts, per_device(): full = full.reshape(4096, 2, 256)  6.95 us
  transfers between devices with their start and end apart: 35, of which 11 were waited for; matrix products, arithmetic and copies ran while one was open for 14% of the time, Pallas kernels for 3%

profile of v1, /device:TPU:1, one launch (start us, length us, event | category | flops | bytes accessed | tf_op | source)
XLA Modules:
  0.0 297.4 jit_solution(6068016083375691859)
XLA Ops:
  1.3 97.3 %shard_map.84 = (bf16[8,192,2,128]{3,2,1,0:T(2,128)(2,1)}, bf16[8,192,2,128]{3,2,1,0:T(2,128)(2,1)}, bf16[8,192,2,128]{3,2,1,0:T(2,128)(2,1)}, bf16[8,192,2,128]{3,2,1,0:T(2,128)(2,1)}) custom-call(s32[3]{0:T(128)} %pad_add_fusion.place_ref, bf16[192,2,4096]{2,1,0:T(2,128)(2,1)} %bitcast.168), custom_call_target="tpu_custom_call" | custom-call | tf_op jit(solution)/shard_map/pallas_call | solution.py:90
  98.6 2.1 collective-permute-start
  100.7 1.2 collective-permute-start.1
  102.0 1.0 reshape.50
  104.0 14.2 %collective-permute-done = bf16[8,192,2,128]{3,2,1,0:T(2,128)(2,1)S(1)} collective-permute-done((bf16[8,192,2,128]{3,2,1,0:T(2,128)(2,1)}, bf16[8,192,2,128]{3,2,1,0:T(2,128)(2,1)S(1)}, u32[]{:S(2)}, u32[]{:S(2)}) %collective-permute-start) | collective-permute-done | bytes 786464 | tf_op jit(solution)/shard_map/ppermute | solution.py:64
  119.0 17.0 %collective-permute-done.2 = bf16[8,192,2,128]{3,2,1,0:T(2,128)(2,1)S(1)} collective-permute-done((bf16[8,192,2,128]{3,2,1,0:T(2,128)(2,1)}, bf16[8,192,2,128]{3,2,1,0:T(2,128)(2,1)S(1)}, u32[]{:S(2)}, u32[]{:S(2)}) %collective-permute-start.2) | collective-permute-done | bytes 786464 | tf_op jit(solution)/shard_map/ppermute | solution.py:64
  136.9 7.3 %shard_map.85 = (bf16[8,384,128]{2,1,0:T(8,128)(2,1)}, f32[8,128,512]{2,1,0:T(8,128)}) custom-call(bf16[8,384,128]{2,1,0:T(8,128)(2,1)} %bitcast.171, bf16[8,384,128]{2,1,0:T(8,128)(2,1)} %bitcast.172, bf16[8,384,128]{2,1,0:T(8,128)(2,1)} %bitcast.173, bf16[8,384,128]{2,1,0:T(8,128)(2,1)} %bitcast.174, bf16[384,512]{1,0:T(8,128)(2,1)} %pad_maximum_fusion.1.s_ref), custom_call_target="tpu_custom_call" | custom-call | tf_op jit(solution)/shard_map/pallas_call | solution.py:113
  144.2 1.4 slice.271
  145.6 2.1 collective-permute-start.3
  147.6 1.5 collective-permute-done.3
  149.2 1.4 fusion.40
  151.4 3.3 %collective-permute-start.6 = (bf16[128,512]{1,0:T(8,128)(2,1)}, bf16[128,512]{1,0:T(8,128)(2,1)S(1)}, u32[]{:S(2)}, u32[]{:S(2)}) collective-permute-start(bf16[128,512]{1,0:T(8,128)(2,1)} %get-tuple-element.41), channel_id=1, source_target_pairs={{0,6},{1,7},{2,4},{3,5},{4,2},{5,3},{6,0},{7,1},{8,14},{9,15},{10,... | collective-permute-start | bytes 393224 | tf_op jit(solution)/shard_map/ppermute | solution.py:64
  155.0 1.0 copy.17
  156.0 1.0 copy.16
  157.1 1.2 collective-permute-done.6
  158.3 7.5 %collective-permute-done.5 = bf16[128,512]{1,0:T(8,128)(2,1)S(1)} collective-permute-done((bf16[128,512]{1,0:T(8,128)(2,1)}, bf16[128,512]{1,0:T(8,128)(2,1)S(1)}, u32[]{:S(2)}, u32[]{:S(2)}) %collective-permute-start.5) | collective-permute-done | bytes 131104 | tf_op jit(solution)/shard_map/ppermute | solution.py:64
  167.2 1.7 bitcast_dynamic-update-slice_fusion.3
  169.7 2.5 broadcast_in_dim.21
  172.1 1.9 bitcast_dynamic-update-slice_fusion.7
  174.1 2.5 collective-permute-start.8
  176.6 1.0 collective-permute-start.9
  178.4 1.1 collective-permute-start.19
  180.2 1.5 collective-permute-done.18
  182.4 2.5 collective-permute-start.21
  184.9 1.0 collective-permute-start.22
  185.9 5.6 %collective-permute-start.23 = (bf16[128,512]{1,0:T(8,128)(2,1)S(1)}, bf16[128,512]{1,0:T(8,128)(2,1)}, u32[]{:S(2)}, u32[]{:S(2)}) collective-permute-start(bf16[128,512]{1,0:T(8,128)(2,1)S(1)} %get-tuple-element.33.refs_0_), channel_id=1, source_target_pairs={{0,1},{1,0},{2,3},{3,2},{4,5},{5,4},{6,7},{7,6},{8,9},{9,8},{10,11... | collective-permute-start | bytes 393224 | tf_op jit(solution)/shard_map/ppermute | solution.py:64
  193.2 1.7 reshape.54
  194.9 2.9 fusion.1
  198.3 1.1 collective-permute-start.25
  202.3 3.1 %shard_map.86.a_ref = bf16[384,256]{1,0:T(8,128)(2,1)} custom-call(bf16[8,384,128]{2,1,0:T(8,128)(2,1)} %get-tuple-element.18.g_ref, bf16[128,512]{1,0:T(8,128)(2,1)} %copy-done.7, bf16[128,512]{1,0:T(8,128)(2,1)} %collective-permute-done.20.refs_1_, bf16[128,512]{1,0:T(8,128)(2,1)} %collective-permute-done.21.refs_2_, ...), custom_call_target="tpu_custom_call" | custom-call | tf_op jit(solution)/shard_map/pallas_call | solution.py:137
  206.9 1.2 collective-permute-start.29
  208.7 9.4 %collective-permute-done.27.b_ref = bf16[384,256]{1,0:T(8,128)(2,1)S(1)} collective-permute-done((bf16[384,256]{1,0:T(8,128)(2,1)}, bf16[384,256]{1,0:T(8,128)(2,1)S(1)}, u32[]{:S(2)}, u32[]{:S(2)}) %collective-permute-start.27) | collective-permute-done | bytes 196640 | tf_op jit(solution)/shard_map/ppermute | solution.py:64
  218.9 1.2 collective-permute-start.15
  220.1 2.8 collective-permute-done.29.d_ref
  223.6 3.2 %shard_map.87 = (f32[384,256]{1,0:T(8,128)}, f32[256,256]{1,0:T(8,128)}, f32[256,256]{1,0:T(8,128)}) custom-call(s32[3]{0:T(128)} %pad_add_fusion.place_ref, bf16[384,256]{1,0:T(8,128)(2,1)} %shard_map.86.a_ref, bf16[384,256]{1,0:T(8,128)(2,1)} %copy-done.13, bf16[384,256]{1,0:T(8,128)(2,1)} %copy-done.14, bf16[384,256]{1,0:T(8,128)(2,1)} %copy-done.15), custom_call_target="tpu_custom_call" | custom-call | tf_op jit(solution)/shard_map/pallas_call | solution.py:164
  226.7 2.4 collective-permute-start.30
  229.1 1.6 fusion.34
  230.7 1.6 fusion.33
  232.3 1.6 fusion.32
  233.8 1.6 fusion.31
  237.1 2.2 collective-permute-start.33
  239.2 3.2 %collective-permute-start.32 = (bf16[256,256]{1,0:T(8,128)(2,1)S(1)}, bf16[256,256]{1,0:T(8,128)(2,1)S(1)}, u32[]{:S(2)}, u32[]{:S(2)}) collective-permute-start(bf16[256,256]{1,0:T(8,128)(2,1)S(1)} %get-tuple-element.30), channel_id=1, source_target_pairs={{0,4},{1,5},{2,6},{3,7},{4,0},{5,1},{6,2},{7,3},{8,12},{9,13},{10,... | collective-permute-start | bytes 393224 | tf_op jit(solution)/shard_map/ppermute | solution.py:64
  244.9 7.9 %collective-permute-done.32 = bf16[256,256]{1,0:T(8,128)(2,1)S(1)} collective-permute-done((bf16[256,256]{1,0:T(8,128)(2,1)S(1)}, bf16[256,256]{1,0:T(8,128)(2,1)S(1)}, u32[]{:S(2)}, u32[]{:S(2)}) %collective-permute-start.32) | collective-permute-done | bytes 131104 | tf_op jit(solution)/shard_map/ppermute | solution.py:64
  256.0 3.1 %shard_map.88 = bf16[384,256]{1,0:T(8,128)(2,1)} custom-call(s32[3]{0:T(128)} %pad_add_fusion.place_ref, f32[384,256]{1,0:T(8,128)} %get-tuple-element.19.spanned_ref, f32[256,256]{1,0:T(8,128)} %copy-done.2, f32[256,256]{1,0:T(8,128)} %copy-done.12), custom_call_target="tpu_custom_call" | custom-call | tf_op jit(solution)/shard_map/pallas_call | solution.py:190
  259.1 1.7 reshape.53
  274.1 6.9 %reshape.52 = bf16[4096,2,256]{2,1,0:T(2,128)(2,1)} reshape(bf16[4,2,4,128,512]{4,3,2,1,0:T(8,128)(2,1)} %fusion.7) | data formatting | bytes 8388608 | tf_op jit(solution)/shard_map/reshape | solution.py:260
  281.0 8.8 %bitcast_subtract_fusion = f32[192,2,4096]{2,0,1:T(8,128)S(1)} fusion(f32[192,2,4096]{2,1,0:T(2,128)} %param.6, bf16[4096,2,256]{2,1,0:T(2,128)(2,1)} %reshape.52, bf16[192,2,256]{2,1,0:T(2,128)(2,1)S(1)} %copy-done.3), kind=kOutput, calls=%fused_computation | convolution fusion | flops 808452096 | bytes 16973824 | tf_op jit(solution)/shard_map/dmk,fmk->dmf/dot_general | solution.py:261
  289.8 7.6 %copy.15 = f32[192,2,4096]{2,1,0:T(2,128)} copy(f32[192,2,4096]{2,0,1:T(8,128)S(1)} %bitcast_subtract_fusion) | data formatting | bytes 12582912
  (123 shorter events, 37.8 us)
Async XLA Ops:
  98.6 19.6 %collective-permute-start = (bf16[8,192,2,128]{3,2,1,0:T(2,128)(2,1)}, bf16[8,192,2,128]{3,2,1,0:T(2,128)(2,1)S(1)}, u32[]{:S(2)}, u32[]{:S(2)}) collective-permute-start(bf16[8,192,2,128]{3,2,1,0:T(2,128)(2,1)} %get-tuple-element.14), channel_id=1, source_target_pairs={{0,8},{8,0},{16,24},{24,16},{1,9},{9,1},{17,25},{25,17},{2,10},{10... | collective-permute-start | bytes 2359304 | tf_op jit(solution)/shard_map/ppermute | solution.py:64
  100.7 18.3 %collective-permute-start.1 = (bf16[8,192,2,128]{3,2,1,0:T(2,128)(2,1)}, bf16[8,192,2,128]{3,2,1,0:T(2,128)(2,1)S(1)}, u32[]{:S(2)}, u32[]{:S(2)}) collective-permute-start(bf16[8,192,2,128]{3,2,1,0:T(2,128)(2,1)} %get-tuple-element.15), channel_id=1, source_target_pairs={{0,16},{8,24},{16,0},{24,8},{1,17},{9,25},{17,1},{25,9},{2,18},{10... | collective-permute-start | bytes 2359304 | tf_op jit(solution)/shard_map/ppermute | solution.py:64
  102.0 34.0 %collective-permute-start.2 = (bf16[8,192,2,128]{3,2,1,0:T(2,128)(2,1)}, bf16[8,192,2,128]{3,2,1,0:T(2,128)(2,1)S(1)}, u32[]{:S(2)}, u32[]{:S(2)}) collective-permute-start(bf16[8,192,2,128]{3,2,1,0:T(2,128)(2,1)} %get-tuple-element.16), channel_id=1, source_target_pairs={{0,24},{8,16},{16,8},{24,0},{1,25},{9,17},{17,9},{25,1},{2,26},{10... | collective-permute-start | bytes 2359304 | tf_op jit(solution)/shard_map/ppermute | solution.py:64
  118.2 17.8 %copy-start.4 = (bf16[8,192,2,128]{3,2,1,0:T(2,128)(2,1)}, bf16[8,192,2,128]{3,2,1,0:T(2,128)(2,1)S(1)}, u32[]{:S(2)}) copy-start(bf16[8,192,2,128]{3,2,1,0:T(2,128)(2,1)S(1)} %collective-permute-done) | copy-start | bytes 2359300
  119.0 17.0 %copy-start.5 = (bf16[8,192,2,128]{3,2,1,0:T(2,128)(2,1)}, bf16[8,192,2,128]{3,2,1,0:T(2,128)(2,1)S(1)}, u32[]{:S(2)}) copy-start(bf16[8,192,2,128]{3,2,1,0:T(2,128)(2,1)S(1)} %collective-permute-done.1) | copy-start | bytes 2359300
  136.0 0.9 copy-start.6
  136.9 18.1 %copy-start = (f32[512,2,256]{2,1,0:T(2,128)S(1)}, f32[512,2,256]{2,1,0:T(2,128)}, u32[]{:S(2)}) copy-start(f32[512,2,256]{2,1,0:T(2,128)} %param.9) | copy-start | bytes 3145732
  144.2 11.9 %copy-start.1 = (f32[512,2,256]{2,1,0:T(2,128)S(1)}, f32[512,2,256]{2,1,0:T(2,128)}, u32[]{:S(2)}) copy-start(f32[512,2,256]{2,1,0:T(2,128)} %param.8) | copy-start | bytes 3145732
  145.6 3.6 %collective-permute-start.3 = (bf16[4,128,512]{2,1,0:T(8,128)(2,1)S(1)}, bf16[4,128,512]{2,1,0:T(8,128)(2,1)S(1)}, u32[]{:S(2)}, u32[]{:S(2)}) collective-permute-start(bf16[4,128,512]{2,1,0:T(8,128)(2,1)S(1)} %slice.271), channel_id=1, source_target_pairs={{0,1},{1,0},{2,3},{3,2},{4,5},{5,4},{6,7},{7,6},{8,9},{9,8},{10,11... | collective-permute-start | bytes 1572872 | tf_op jit(solution)/shard_map/ppermute | solution.py:64
  151.4 6.9 %collective-permute-start.6 = (bf16[128,512]{1,0:T(8,128)(2,1)}, bf16[128,512]{1,0:T(8,128)(2,1)S(1)}, u32[]{:S(2)}, u32[]{:S(2)}) collective-permute-start(bf16[128,512]{1,0:T(8,128)(2,1)} %get-tuple-element.41), channel_id=1, source_target_pairs={{0,6},{1,7},{2,4},{3,5},{4,2},{5,3},{6,0},{7,1},{8,14},{9,15},{10,... | collective-permute-start | bytes 393224 | tf_op jit(solution)/shard_map/ppermute | solution.py:64
  154.7 11.0 %collective-permute-start.5 = (bf16[128,512]{1,0:T(8,128)(2,1)}, bf16[128,512]{1,0:T(8,128)(2,1)S(1)}, u32[]{:S(2)}, u32[]{:S(2)}) collective-permute-start(bf16[128,512]{1,0:T(8,128)(2,1)} %get-tuple-element.42), channel_id=1, source_target_pairs={{0,4},{1,5},{2,6},{3,7},{4,0},{5,1},{6,2},{7,3},{8,12},{9,13},{10,... | collective-permute-start | bytes 393224 | tf_op jit(solution)/shard_map/ppermute | solution.py:64
  154.7 11.0 %collective-permute-start.4 = (bf16[128,512]{1,0:T(8,128)(2,1)}, bf16[128,512]{1,0:T(8,128)(2,1)S(1)}, u32[]{:S(2)}, u32[]{:S(2)}) collective-permute-start(bf16[128,512]{1,0:T(8,128)(2,1)} %get-tuple-element.40), channel_id=1, source_target_pairs={{0,2},{1,3},{2,0},{3,1},{4,6},{5,7},{6,4},{7,5},{8,10},{9,11},{10,... | collective-permute-start | bytes 393224 | tf_op jit(solution)/shard_map/ppermute | solution.py:64
  167.2 4.9 %copy-start.9 = (bf16[128,512]{1,0:T(8,128)(2,1)S(1)}, bf16[128,512]{1,0:T(8,128)(2,1)}, u32[]{:S(2)}) copy-start(bf16[128,512]{1,0:T(8,128)(2,1)} %copy-done.8) | copy-start | bytes 393220
  168.9 25.9 %copy-start.7 = (bf16[128,512]{1,0:T(8,128)(2,1)}, bf16[128,512]{1,0:T(8,128)(2,1)S(1)}, u32[]{:S(2)}) copy-start(bf16[128,512]{1,0:T(8,128)(2,1)S(1)} %get-tuple-element.33.refs_0_) | copy-start | bytes 393220
  168.9 9.5 %collective-permute-start.17 = (bf16[128,512]{1,0:T(8,128)(2,1)S(1)}, bf16[128,512]{1,0:T(8,128)(2,1)S(1)}, u32[]{:S(2)}, u32[]{:S(2)}) collective-permute-start(bf16[128,512]{1,0:T(8,128)(2,1)S(1)} %get-tuple-element.33.refs_0_), channel_id=1, source_target_pairs={{0,8},{8,0},{16,24},{24,16},{1,9},{9,1},{17,25},{25,17},{2,10},{10... | collective-permute-start | bytes 393224 | tf_op jit(solution)/shard_map/ppermute | solution.py:64
  174.1 8.3 %collective-permute-start.7 = (bf16[128,512]{1,0:T(8,128)(2,1)S(1)}, bf16[128,512]{1,0:T(8,128)(2,1)S(1)}, u32[]{:S(2)}, u32[]{:S(2)}) collective-permute-start(bf16[128,512]{1,0:T(8,128)(2,1)S(1)} %get-tuple-element.35), channel_id=1, source_target_pairs={{0,2},{1,3},{2,0},{3,1},{4,6},{5,7},{6,4},{7,5},{8,10},{9,11},{10,... | collective-permute-start | bytes 393224 | tf_op jit(solution)/shard_map/ppermute | solution.py:64
  174.1 10.8 %collective-permute-start.8 = (bf16[128,512]{1,0:T(8,128)(2,1)S(1)}, bf16[128,512]{1,0:T(8,128)(2,1)S(1)}, u32[]{:S(2)}, u32[]{:S(2)}) collective-permute-start(bf16[128,512]{1,0:T(8,128)(2,1)S(1)} %get-tuple-element.35), channel_id=1, source_target_pairs={{0,4},{1,5},{2,6},{3,7},{4,0},{5,1},{6,2},{7,3},{8,12},{9,13},{10,... | collective-permute-start | bytes 393224 | tf_op jit(solution)/shard_map/ppermute | solution.py:64
  176.6 9.4 %collective-permute-start.9 = (bf16[128,512]{1,0:T(8,128)(2,1)S(1)}, bf16[128,512]{1,0:T(8,128)(2,1)S(1)}, u32[]{:S(2)}, u32[]{:S(2)}) collective-permute-start(bf16[128,512]{1,0:T(8,128)(2,1)S(1)} %get-tuple-element.35), channel_id=1, source_target_pairs={{0,6},{1,7},{2,4},{3,5},{4,2},{5,3},{6,0},{7,1},{8,14},{9,15},{10,... | collective-permute-start | bytes 393224 | tf_op jit(solution)/shard_map/ppermute | solution.py:64
  177.6 4.1 %collective-permute-start.18 = (bf16[128,512]{1,0:T(8,128)(2,1)S(1)}, bf16[128,512]{1,0:T(8,128)(2,1)S(1)}, u32[]{:S(2)}, u32[]{:S(2)}) collective-permute-start(bf16[128,512]{1,0:T(8,128)(2,1)S(1)} %get-tuple-element.33.refs_0_), channel_id=1, source_target_pairs={{0,16},{8,24},{16,0},{24,8},{1,17},{9,25},{17,1},{25,9},{2,18},{10... | collective-permute-start | bytes 393224 | tf_op jit(solution)/shard_map/ppermute | solution.py:64
  178.4 14.1 %collective-permute-start.19 = (bf16[128,512]{1,0:T(8,128)(2,1)S(1)}, bf16[128,512]{1,0:T(8,128)(2,1)S(1)}, u32[]{:S(2)}, u32[]{:S(2)}) collective-permute-start(bf16[128,512]{1,0:T(8,128)(2,1)S(1)} %get-tuple-element.33.refs_0_), channel_id=1, source_target_pairs={{0,24},{8,16},{16,8},{24,0},{1,25},{9,17},{17,9},{25,1},{2,26},{10... | collective-permute-start | bytes 393224 | tf_op jit(solution)/shard_map/ppermute | solution.py:64
  181.7 16.1 %collective-permute-start.20 = (bf16[128,512]{1,0:T(8,128)(2,1)S(1)}, bf16[128,512]{1,0:T(8,128)(2,1)}, u32[]{:S(2)}, u32[]{:S(2)}) collective-permute-start(bf16[128,512]{1,0:T(8,128)(2,1)S(1)} %get-tuple-element.33.refs_0_), channel_id=1, source_target_pairs={{0,2},{1,3},{2,0},{3,1},{4,6},{5,7},{6,4},{7,5},{8,10},{9,11},{10,... | collective-permute-start | bytes 393224 | tf_op jit(solution)/shard_map/ppermute | solution.py:64
  182.4 15.9 %collective-permute-start.21 = (bf16[128,512]{1,0:T(8,128)(2,1)S(1)}, bf16[128,512]{1,0:T(8,128)(2,1)}, u32[]{:S(2)}, u32[]{:S(2)}) collective-permute-start(bf16[128,512]{1,0:T(8,128)(2,1)S(1)} %get-tuple-element.33.refs_0_), channel_id=1, source_target_pairs={{0,4},{1,5},{2,6},{3,7},{4,0},{5,1},{6,2},{7,3},{8,12},{9,13},{10,... | collective-permute-start | bytes 393224 | tf_op jit(solution)/shard_map/ppermute | solution.py:64
  184.9 7.6 %copy-start.10 = (bf16[128,512]{1,0:T(8,128)(2,1)}, bf16[128,512]{1,0:T(8,128)(2,1)S(1)}, u32[]{:S(2)}) copy-start(bf16[128,512]{1,0:T(8,128)(2,1)S(1)} %collective-permute-done.8) | copy-start | bytes 393220
  184.9 14.5 %collective-permute-start.22 = (bf16[128,512]{1,0:T(8,128)(2,1)S(1)}, bf16[128,512]{1,0:T(8,128)(2,1)}, u32[]{:S(2)}, u32[]{:S(2)}) collective-permute-start(bf16[128,512]{1,0:T(8,128)(2,1)S(1)} %get-tuple-element.33.refs_0_), channel_id=1, source_target_pairs={{0,6},{1,7},{2,4},{3,5},{4,2},{5,3},{6,0},{7,1},{8,14},{9,15},{10,... | collective-permute-start | bytes 393224 | tf_op jit(solution)/shard_map/ppermute | solution.py:64
  185.9 14.8 %collective-permute-start.23 = (bf16[128,512]{1,0:T(8,128)(2,1)S(1)}, bf16[128,512]{1,0:T(8,128)(2,1)}, u32[]{:S(2)}, u32[]{:S(2)}) collective-permute-start(bf16[128,512]{1,0:T(8,128)(2,1)S(1)} %get-tuple-element.33.refs_0_), channel_id=1, source_target_pairs={{0,1},{1,0},{2,3},{3,2},{4,5},{5,4},{6,7},{7,6},{8,9},{9,8},{10,11... | collective-permute-start | bytes 393224 | tf_op jit(solution)/shard_map/ppermute | solution.py:64
  192.5 36.6 %collective-permute-start.10 = (bf16[4,128,512]{2,1,0:T(8,128)(2,1)}, bf16[4,128,512]{2,1,0:T(8,128)(2,1)}, u32[]{:S(2)}, u32[]{:S(2)}) collective-permute-start(bf16[4,128,512]{2,1,0:T(8,128)(2,1)} %pad_maximum_fusion), channel_id=1, source_target_pairs={{0,1},{1,0},{2,3},{3,2},{4,5},{5,4},{6,7},{7,6},{8,9},{9,8},{10,11... | collective-permute-start | bytes 1572872 | tf_op jit(solution)/shard_map/ppermute | solution.py:64
  194.8 5.3 %copy-start.11 = (bf16[128,512]{1,0:T(8,128)(2,1)S(1)}, bf16[128,512]{1,0:T(8,128)(2,1)}, u32[]{:S(2)}) copy-start(bf16[128,512]{1,0:T(8,128)(2,1)} %copy-done.10) | copy-start | bytes 393220
  197.8 3.7 %collective-permute-start.24 = (bf16[128,512]{1,0:T(8,128)(2,1)}, bf16[128,512]{1,0:T(8,128)(2,1)S(1)}, u32[]{:S(2)}, u32[]{:S(2)}) collective-permute-start(bf16[128,512]{1,0:T(8,128)(2,1)} %collective-permute-done.20.refs_1_), channel_id=1, source_target_pairs={{0,1},{1,0},{2,3},{3,2},{4,5},{5,4},{6,7},{7,6},{8,9},{9,8},{10,11... | collective-permute-start | bytes 393224 | tf_op jit(solution)/shard_map/ppermute | solution.py:64
  198.3 3.2 %collective-permute-start.25 = (bf16[128,512]{1,0:T(8,128)(2,1)}, bf16[128,512]{1,0:T(8,128)(2,1)S(1)}, u32[]{:S(2)}, u32[]{:S(2)}) collective-permute-start(bf16[128,512]{1,0:T(8,128)(2,1)} %collective-permute-done.21.refs_2_), channel_id=1, source_target_pairs={{0,1},{1,0},{2,3},{3,2},{4,5},{5,4},{6,7},{7,6},{8,9},{9,8},{10,11... | collective-permute-start | bytes 393224 | tf_op jit(solution)/shard_map/ppermute | solution.py:64
  199.4 2.1 collective-permute-start.26
  200.8 34.6 %collective-permute-start.11 = (bf16[4,128,512]{2,1,0:T(8,128)(2,1)}, bf16[4,128,512]{2,1,0:T(8,128)(2,1)S(1)}, u32[]{:S(2)}, u32[]{:S(2)}) collective-permute-start(bf16[4,128,512]{2,1,0:T(8,128)(2,1)} %pad_maximum_fusion), channel_id=1, source_target_pairs={{0,8},{8,0},{16,24},{24,16},{1,9},{9,1},{17,25},{25,17},{2,10},{10... | collective-permute-start | bytes 1572872 | tf_op jit(solution)/shard_map/ppermute | solution.py:64
  205.4 12.8 %collective-permute-start.27 = (bf16[384,256]{1,0:T(8,128)(2,1)}, bf16[384,256]{1,0:T(8,128)(2,1)S(1)}, u32[]{:S(2)}, u32[]{:S(2)}) collective-permute-start(bf16[384,256]{1,0:T(8,128)(2,1)} %shard_map.86.a_ref), channel_id=1, source_target_pairs={{0,8},{8,0},{16,24},{24,16},{1,9},{9,1},{17,25},{25,17},{2,10},{10... | collective-permute-start | bytes 589832 | tf_op jit(solution)/shard_map/ppermute | solution.py:64
  206.1 12.8 %collective-permute-start.28 = (bf16[384,256]{1,0:T(8,128)(2,1)}, bf16[384,256]{1,0:T(8,128)(2,1)S(1)}, u32[]{:S(2)}, u32[]{:S(2)}) collective-permute-start(bf16[384,256]{1,0:T(8,128)(2,1)} %shard_map.86.a_ref), channel_id=1, source_target_pairs={{0,16},{8,24},{16,0},{24,8},{1,17},{9,25},{17,1},{25,9},{2,18},{10... | collective-permute-start | bytes 589832 | tf_op jit(solution)/shard_map/ppermute | solution.py:64
  206.9 16.0 %collective-permute-start.29 = (bf16[384,256]{1,0:T(8,128)(2,1)}, bf16[384,256]{1,0:T(8,128)(2,1)S(1)}, u32[]{:S(2)}, u32[]{:S(2)}) collective-permute-start(bf16[384,256]{1,0:T(8,128)(2,1)} %shard_map.86.a_ref), channel_id=1, source_target_pairs={{0,24},{8,16},{16,8},{24,0},{1,25},{9,17},{17,9},{25,1},{2,26},{10... | collective-permute-start | bytes 589832 | tf_op jit(solution)/shard_map/ppermute | solution.py:64
  218.2 4.7 %copy-start.13 = (bf16[384,256]{1,0:T(8,128)(2,1)}, bf16[384,256]{1,0:T(8,128)(2,1)S(1)}, u32[]{:S(2)}) copy-start(bf16[384,256]{1,0:T(8,128)(2,1)S(1)} %collective-permute-done.27.b_ref) | copy-start | bytes 589828
  218.2 35.9 %collective-permute-start.13 = (bf16[4,128,512]{2,1,0:T(8,128)(2,1)}, bf16[4,128,512]{2,1,0:T(8,128)(2,1)S(1)}, u32[]{:S(2)}, u32[]{:S(2)}) collective-permute-start(bf16[4,128,512]{2,1,0:T(8,128)(2,1)} %pad_maximum_fusion), channel_id=1, source_target_pairs={{0,16},{8,24},{16,0},{24,8},{1,17},{9,25},{17,1},{25,9},{2,18},{10... | collective-permute-start | bytes 1572872 | tf_op jit(solution)/shard_map/ppermute | solution.py:64
  218.9 4.0 %copy-start.14 = (bf16[384,256]{1,0:T(8,128)(2,1)}, bf16[384,256]{1,0:T(8,128)(2,1)S(1)}, u32[]{:S(2)}) copy-start(bf16[384,256]{1,0:T(8,128)(2,1)S(1)} %collective-permute-done.28.c_ref) | copy-start | bytes 589828
  218.9 35.2 %collective-permute-start.15 = (bf16[4,128,512]{2,1,0:T(8,128)(2,1)}, bf16[4,128,512]{2,1,0:T(8,128)(2,1)S(1)}, u32[]{:S(2)}, u32[]{:S(2)}) collective-permute-start(bf16[4,128,512]{2,1,0:T(8,128)(2,1)} %pad_maximum_fusion), channel_id=1, source_target_pairs={{0,24},{8,16},{16,8},{24,0},{1,25},{9,17},{17,9},{25,1},{2,26},{10... | collective-permute-start | bytes 1572872 | tf_op jit(solution)/shard_map/ppermute | solution.py:64
  226.7 9.3 %collective-permute-start.30 = (f32[256,256]{1,0:T(8,128)}, f32[256,256]{1,0:T(8,128)S(1)}, u32[]{:S(2)}, u32[]{:S(2)}) collective-permute-start(f32[256,256]{1,0:T(8,128)} %get-tuple-element.21), channel_id=1, source_target_pairs={{0,1},{1,0},{2,3},{3,2},{4,5},{5,4},{6,7},{7,6},{8,9},{9,8},{10,11... | collective-permute-start | bytes 786440 | tf_op jit(solution)/shard_map/ppermute | solution.py:64
  237.1 7.0 %collective-permute-start.33 = (bf16[256,256]{1,0:T(8,128)(2,1)S(1)}, bf16[256,256]{1,0:T(8,128)(2,1)S(1)}, u32[]{:S(2)}, u32[]{:S(2)}) collective-permute-start(bf16[256,256]{1,0:T(8,128)(2,1)S(1)} %get-tuple-element.30), channel_id=1, source_target_pairs={{0,6},{1,7},{2,4},{3,5},{4,2},{5,3},{6,0},{7,1},{8,14},{9,15},{10,... | collective-permute-start | bytes 393224 | tf_op jit(solution)/shard_map/ppermute | solution.py:64
  239.2 13.6 %collective-permute-start.32 = (bf16[256,256]{1,0:T(8,128)(2,1)S(1)}, bf16[256,256]{1,0:T(8,128)(2,1)S(1)}, u32[]{:S(2)}, u32[]{:S(2)}) collective-permute-start(bf16[256,256]{1,0:T(8,128)(2,1)S(1)} %get-tuple-element.30), channel_id=1, source_target_pairs={{0,4},{1,5},{2,6},{3,7},{4,0},{5,1},{6,2},{7,3},{8,12},{9,13},{10,... | collective-permute-start | bytes 393224 | tf_op jit(solution)/shard_map/ppermute | solution.py:64
  242.4 10.4 %collective-permute-start.31 = (bf16[256,256]{1,0:T(8,128)(2,1)S(1)}, bf16[256,256]{1,0:T(8,128)(2,1)S(1)}, u32[]{:S(2)}, u32[]{:S(2)}) collective-permute-start(bf16[256,256]{1,0:T(8,128)(2,1)S(1)} %get-tuple-element.30), channel_id=1, source_target_pairs={{0,2},{1,3},{2,0},{3,1},{4,6},{5,7},{6,4},{7,5},{8,10},{9,11},{10,... | collective-permute-start | bytes 393224 | tf_op jit(solution)/shard_map/ppermute | solution.py:64
  244.0 16.7 %collective-permute-start.12 = (bf16[4,128,512]{2,1,0:T(8,128)(2,1)S(1)}, bf16[4,128,512]{2,1,0:T(8,128)(2,1)S(1)}, u32[]{:S(2)}, u32[]{:S(2)}) collective-permute-start(bf16[4,128,512]{2,1,0:T(8,128)(2,1)S(1)} %collective-permute-done.11), channel_id=1, source_target_pairs={{0,1},{1,0},{2,3},{3,2},{4,5},{5,4},{6,7},{7,6},{8,9},{9,8},{10,11... | collective-permute-start | bytes 1572872 | tf_op jit(solution)/shard_map/ppermute | solution.py:64
  252.9 3.1 %copy-start.2 = (f32[256,256]{1,0:T(8,128)}, f32[256,256]{1,0:T(8,128)S(1)}, u32[]{:S(2)}) copy-start(f32[256,256]{1,0:T(8,128)S(1)} %add_add_fusion.own_ref) | copy-start | bytes 786436
  252.9 2.4 collective-permute-start.34
  254.1 12.0 %collective-permute-start.14 = (bf16[4,128,512]{2,1,0:T(8,128)(2,1)S(1)}, bf16[4,128,512]{2,1,0:T(8,128)(2,1)S(1)}, u32[]{:S(2)}, u32[]{:S(2)}) collective-permute-start(bf16[4,128,512]{2,1,0:T(8,128)(2,1)S(1)} %collective-permute-done.13), channel_id=1, source_target_pairs={{0,1},{1,0},{2,3},{3,2},{4,5},{5,4},{6,7},{7,6},{8,9},{9,8},{10,11... | collective-permute-start | bytes 1572872 | tf_op jit(solution)/shard_map/ppermute | solution.py:64
  254.2 17.2 %collective-permute-start.16 = (bf16[4,128,512]{2,1,0:T(8,128)(2,1)S(1)}, bf16[4,128,512]{2,1,0:T(8,128)(2,1)S(1)}, u32[]{:S(2)}, u32[]{:S(2)}) collective-permute-start(bf16[4,128,512]{2,1,0:T(8,128)(2,1)S(1)} %collective-permute-done.15), channel_id=1, source_target_pairs={{0,1},{1,0},{2,3},{3,2},{4,5},{5,4},{6,7},{7,6},{8,9},{9,8},{10,11... | collective-permute-start | bytes 1572872 | tf_op jit(solution)/shard_map/ppermute | solution.py:64
  274.1 7.0 %copy-start.3 = (bf16[192,2,256]{2,1,0:T(2,128)(2,1)S(1)}, bf16[192,2,256]{2,1,0:T(2,128)(2,1)}, u32[]{:S(2)}) copy-start(bf16[192,2,256]{2,1,0:T(2,128)(2,1)} %param.7) | copy-start | bytes 589828
  (6 other events, 4.1 us)

commit v2 on v0

v2 whole, which is shorter than its diff:
```python
import math

import jax
import jax.numpy as jnp
from jax import lax
from jax.experimental import pallas as pl
from jax.experimental.pallas import tpu as pltpu
from jax.sharding import PartitionSpec as P

D = 1536
bf16 = jnp.bfloat16
f32 = jnp.float32
inv_root = 1.0 / math.sqrt(D)
first_fix = 1.0 - 0.9**10
second_fix = 1.0 - 0.999**10


def plain(partials, weights, subspace, moment_one, moment_two):
    gradient = lax.psum(partials[0], "grp")
    projected = lax.psum_scatter(
        jnp.einsum("dmf,dmk->fmk", gradient, subspace, preferred_element_type=f32) * inv_root,
        "shard",
        scatter_dimension=0,
        tiled=True,
    )
    new_one, new_two, direction = adam(projected, moment_one, moment_two)
    increment = jnp.einsum(
        "dmk,fmk->dmf",
        subspace,
        lax.all_gather(direction, "shard", axis=0, tiled=True),
        preferred_element_type=f32,
    )
    new_weights = weights - increment * inv_root
    spanned = jnp.einsum(
        "dmf,fmk->dmk",
        gradient,
        lax.all_gather(projected.astype(bf16), "shard", axis=0, tiled=True),
        preferred_element_type=f32,
    )
    gram = lax.psum(
        jnp.einsum("dmk,dml->mkl", spanned, spanned, precision=lax.Precision.HIGHEST), "shard"
    )
    normalizer = norm_of(gram, (1, 2))
    oriented = spanned * normalizer[None, :, None]
    ortho_gram = gram * (normalizer * normalizer)[:, None, None]
    polished = 1.5 * oriented - 0.5 * jnp.einsum(
        "dmk,mkl->dml", oriented, ortho_gram, precision=lax.Precision.HIGHEST
    )
    return new_weights, new_one, new_two, (math.sqrt(D) * polished).astype(bf16)


def norm_of(gram, axes):
    return 1.7 / jnp.sqrt(jnp.sqrt(jnp.sum(gram * gram, axis=axes)) + 1e-06)


def adam(projected, one, two):
    new_one = 0.9 * one + 0.1 * projected
    new_two = 0.999 * two + 0.001 * projected * projected
    direction = new_one / first_fix / (jnp.sqrt(new_two / second_fix) + 1e-08)
    return new_one, new_two, direction.astype(bf16)


def swap(x, axis, bit, size):
    return lax.ppermute(x, axis, [(i, i ^ bit) for i in range(size)])


VMEM = pl.BlockSpec(memory_space=pltpu.VMEM)
SMEM = pl.BlockSpec(memory_space=pltpu.SMEM)
PARAMS = pltpu.CompilerParams(vmem_limit_bytes=24 * 2**20)
xor = jnp.bitwise_xor


def pin(x):
    return pltpu.with_memory_space_constraint(x, pltpu.VMEM)


def call(body, outs, *args, place=None):
    scalars = [] if place is None else [place]
    return pl.pallas_call(
        body,
        in_specs=[SMEM] * len(scalars) + [VMEM] * len(args),
        out_specs=(VMEM,) * len(outs),
        out_shape=tuple(pltpu.VMEM(shape, dtype) for shape, dtype in outs),
        compiler_params=PARAMS,
    )(*scalars, *[pin(a) for a in args])


def pack(place, x, a):
    rows = x.shape[0]

    def body(place_ref, x_ref, high_ref, low_ref):
        i = pl.program_id(0)
        piece = x_ref[...].reshape(2 * rows, 128)

        @pl.when(i < 4)
        def _():
            high_ref[i] = piece

        @pl.when(i >= 4)
        def _():
            low_ref[i - 4] = piece

    def where(i, place_ref):
        k, l = 2 * (1 - i // 4) + i % 2, i // 2 % 2
        shard = xor(place_ref[1], k) * 2 + xor(place_ref[2], l)
        return 0, 0, shard * 4 + xor(place_ref[0], a)

    half = pltpu.VMEM((4, 2 * rows, 128), bf16)
    whole = pl.BlockSpec(memory_space=pltpu.VMEM)
    return pl.pallas_call(
        body,
        grid_spec=pltpu.PrefetchScalarGridSpec(
            num_scalar_prefetch=1,
            grid=(8,),
            in_specs=[pl.BlockSpec((rows, 2, 128), where)],
            out_specs=(whole, whole),
        ),
        out_shape=(half, half),
        compiler_params=PARAMS,
    )(place, x)


def project(pieces, masked):
    rows = masked.shape[0]

    def body(a_ref, b_ref, c_ref, d_ref, s_ref, g_ref, keep_ref, send_ref):
        for i in (2, 3, 0, 1):
            total = (a_ref[i].astype(f32) + b_ref[i].astype(f32)) + (
                c_ref[i].astype(f32) + d_ref[i].astype(f32)
            )
            gradient = total.astype(bf16)
            g_ref[i] = gradient
            part = lax.dot_general(
                gradient, s_ref[...], (((0,), (0,)), ((), ())), preferred_element_type=f32
            )
            if i < 2:
                keep_ref[i] = part
            else:
                send_ref[i - 2] = part.astype(bf16)

    return call(
        body,
        [((4, rows, 128), bf16), ((2, 128, 512), f32), ((2, 128, 512), bf16)],
        *pieces,
        masked,
    )


def add_core(keep, came, first):
    def body(keep_ref, came_ref, a_ref, b_ref):
        a_ref[...] = (keep_ref[0] + came_ref[0].astype(f32)).astype(first)
        b_ref[...] = (keep_ref[1] + came_ref[1].astype(f32)).astype(bf16)

    return call(body, [((128, 512), first), ((128, 512), bf16)], keep, came)


def finish(parts):
    def body(a_ref, b_ref, c_ref, d_ref, half_ref):
        total = (a_ref[...] + b_ref[...].astype(f32)) + (
            c_ref[...].astype(f32) + d_ref[...].astype(f32)
        )
        half_ref[...] = (total * inv_root).astype(bf16)

    return call(body, [((128, 512), bf16)], *parts)[0]


def moments(place, gathered, one, two):
    def body(place_ref, a_ref, b_ref, c_ref, d_ref, one_ref, two_ref, new_one_ref, new_two_ref, own_ref, all_ref):
        for a, ref in enumerate((a_ref, b_ref, c_ref, d_ref)):
            at = pl.ds(pl.multiple_of(xor(place_ref[0], a) * 128, 128), 128)
            for m in range(2):
                lanes = slice(256 * m, 256 * (m + 1))
                projected = ref[:, lanes].astype(f32)
                new_one, new_two, direction = adam(projected, one_ref[at, m, :], two_ref[at, m, :])
                new_one_ref[at, m, :] = new_one
                new_two_ref[at, m, :] = new_two
                all_ref[a, :, lanes] = direction
                if a == 0:
                    own_ref[:, lanes] = direction

    return pl.pallas_call(
        body,
        in_specs=[SMEM] + [VMEM] * 6,
        out_specs=(VMEM,) * 4,
        out_shape=(
            jax.ShapeDtypeStruct(one.shape, f32),
            jax.ShapeDtypeStruct(one.shape, f32),
            pltpu.VMEM((128, 512), bf16),
            pltpu.VMEM((4, 128, 512), bf16),
        ),
        compiler_params=PARAMS,
    )(place, *[pin(x) for x in gathered], one, two)


def span(high, low, pieces):
    rows = high.shape[1]

    def body(high_ref, low_ref, *refs):
        p_refs, out_ref = refs[:8], refs[8]
        total = None
        for l in range(2):
            for k in range(4):
                g_ref = high_ref if k >= 2 else low_ref
                term = jnp.dot(
                    g_ref[l * 2 + k % 2], p_refs[l * 4 + k][...], preferred_element_type=f32
                )
                total = term if total is None else total + term
        odd = lax.broadcasted_iota(jnp.int32, (rows, 256), 0) % 2 == 1
        out_ref[...] = jnp.where(odd, total[:, 256:], total[:, :256]).astype(bf16)

    return call(body, [((rows, 256), bf16)], high, low, *pieces)[0]


def grams(place, parts):
    rows = parts[0].shape[0]

    def body(place_ref, a_ref, b_ref, c_ref, d_ref, spanned_ref, own_ref, other_ref):
        spanned = (a_ref[...].astype(f32) + b_ref[...].astype(f32)) + (
            c_ref[...].astype(f32) + d_ref[...].astype(f32)
        )
        spanned_ref[...] = spanned
        parity = lax.broadcasted_iota(jnp.int32, spanned.shape, 0) % 2
        mine = jnp.where(parity == place_ref[2], spanned, 0.0)
        theirs = jnp.where(parity == place_ref[2], 0.0, spanned)
        for part, out_ref in ((theirs, other_ref), (mine, own_ref)):
            out_ref[...] = lax.dot_general(
                part,
                part,
                (((0,), (0,)), ((), ())),
                preferred_element_type=f32,
                precision=lax.Precision.HIGHEST,
            )

    square = ((256, 256), f32)
    return call(body, [((rows, 256), f32), square, square], *parts, place=place)


def gram_core(own, came):
    def body(own_ref, came_ref, sum_ref, ship_ref):
        total = own_ref[...] + came_ref[...]
        sum_ref[...] = total
        ship_ref[...] = total.astype(bf16)

    return call(body, [((256, 256), f32), ((256, 256), bf16)], own, came)


def gram_chips(parts):
    def body(a_ref, b_ref, c_ref, d_ref, out_ref):
        out_ref[...] = (a_ref[...] + b_ref[...].astype(f32)) + (
            c_ref[...].astype(f32) + d_ref[...].astype(f32)
        )

    return call(body, [((256, 256), f32)], *parts)[0]


def polish(place, spanned, own, other):
    rows = spanned.shape[0]

    def body(place_ref, spanned_ref, own_ref, other_ref, out_ref):
        spanned = spanned_ref[...]
        parity = lax.broadcasted_iota(jnp.int32, spanned.shape, 0) % 2
        mine = parity == place_ref[2]
        total = jnp.zeros_like(spanned)
        for chosen, gram_ref in ((mine, own_ref), (jnp.logical_not(mine), other_ref)):
            gram = gram_ref[...]
            normalizer = norm_of(gram, (0, 1))
            oriented = jnp.where(chosen, spanned, 0.0) * normalizer
            ortho = gram * (normalizer * normalizer)
            total += 1.5 * oriented - 0.5 * jnp.dot(
                oriented, ortho, preferred_element_type=f32, precision=lax.Precision.HIGHEST
            )
        out_ref[...] = (math.sqrt(D) * total).astype(bf16)

    return call(body, [((rows, 256), bf16)], spanned, own, other, place=place)[0]


def update(place, weights, masked, held):
    rows = weights.shape[0]

    def body(place_ref, w_ref, s_ref, *refs):
        sides, out_ref = (refs[:7], refs[7:14]), refs[14]
        for i in range(8):
            l, k = i // 4, i % 4

            @pl.when(pl.program_id(0) == i)
            def _():
                side = sides[l]
                for a in range(4):
                    if k == 0:
                        piece = side[0][a]
                    elif a == 0:
                        piece = side[k][...]
                    else:
                        piece = side[3 + a][k - 1]
                    at = pl.ds(pl.multiple_of(xor(place_ref[0], a) * 128, 128), 128)
                    change = lax.dot_general(
                        s_ref[...], piece, (((1,), (1,)), ((), ())), preferred_element_type=f32
                    )
                    out_ref[:, :, at] = w_ref[:, :, at] - (change * inv_root).reshape(rows, 2, 128)

    def where(i, place_ref):
        return 0, 0, xor(place_ref[1], i % 4) * 2 + xor(place_ref[2], i // 4)

    block = pl.BlockSpec((rows, 2, 512), where)
    return pl.pallas_call(
        body,
        grid_spec=pltpu.PrefetchScalarGridSpec(
            num_scalar_prefetch=1,
            grid=(8,),
            in_specs=[block] + [VMEM] * 15,
            out_specs=block,
        ),
        out_shape=jax.ShapeDtypeStruct(weights.shape, f32),
        compiler_params=PARAMS,
    )(place, weights, pin(masked), *[pin(x) for x in held[0] + held[1]])


def per_device(partials, weights, subspace, moment_one, moment_two):
    rows = weights.shape[0]
    g = lax.axis_index("grp")
    s = lax.axis_index("shard")
    place = jnp.stack([g, s >> 1, s & 1]).astype(jnp.int32)

    def core(x):
        return swap(x, "shard", 1, 8)

    def chip(x, k):
        return swap(x, "shard", 2 * k, 8)

    def group(x, a):
        return swap(x, "grp", a, 4)

    flat = subspace.reshape(2 * rows, 256)
    odd = lax.broadcasted_iota(jnp.int32, flat.shape, 0) % 2 == 1
    zero = jnp.zeros_like(flat)
    masked = jnp.concatenate([jnp.where(odd, zero, flat), jnp.where(odd, flat, zero)], axis=1)

    packed = [pack(place, partials[0], a) for a in range(4)]
    high = [packed[0][0]] + [group(packed[a][0], a) for a in (1, 2, 3)]
    low = [packed[0][1]] + [group(packed[a][1], a) for a in (1, 2, 3)]

    gradient_high, keep, send = project(high, masked)
    q2, q3 = add_core(keep, core(send), bf16)
    r2, r3 = chip(q2, 2), chip(q3, 3)
    gradient_low, keep, send = project(low, masked)
    q0, q1 = add_core(keep, core(send), f32)
    half = finish([q0, chip(q1, 1), r2, r3])

    halves = [half] + [chip(half, k) for k in (1, 2, 3)]
    gathered = [half] + [group(half, a) for a in (1, 2, 3)]
    far_halves = [core(h) for h in halves]

    part = span(gradient_high, gradient_low, halves + far_halves)
    spanned, own, other = grams(place, [part] + [group(part, a) for a in (1, 2, 3)])
    own, ship = gram_core(own, core(other))
    own = gram_chips([own] + [chip(ship, k) for k in (1, 2, 3)])
    new_subspace = polish(place, spanned, own, core(own)).reshape(rows, 2, 256)

    new_one, new_two, mine, local = moments(place, gathered, moment_one, moment_two)
    along = [chip(mine, k) for k in (1, 2, 3)]
    stack = jnp.stack(along)
    near = [local] + along + [group(stack, a) for a in (1, 2, 3)]
    far = [core(x) for x in near]
    new_weights = update(place, weights, masked, (near, far))
    return new_weights, new_one, new_two, new_subspace


def solution(mesh):
    small = mesh.shape["grp"] == 4 and mesh.shape["shard"] == 8
    return jax.shard_map(
        per_device if small else plain,
        mesh=mesh,
        in_specs=(
            P("grp", "shard", None, None),
            P("shard", None, None),
            P("shard", None, None),
            P("shard", None, None),
            P("shard", None, None),
        ),
        out_specs=(
            P("shard", None, None),
            P("shard", None, None),
            P("shard", None, None),
            P("shard", None, None),
        ),
        check_vma=False,
    )
```

time: 424 us -> 150 us (0.35)
  waiting for transfers between devices: 354 us -> 63.5 us
  starting transfers between devices: 0.24 us -> 42.6 us
  Pallas kernels: 0 us -> 32.8 us
  matrix products: 24.5 us -> 0 us
  local copies, waits for them, and re-layouts: 23 us -> 9.32 us
  between operations: 14.1 us -> 0.88 us
  other arithmetic: 5.61 us -> 0.38 us
    psum x3 -> x0, waiting for transfers between devices: 176 us -> none  [the longest x1 89.4 us: per_device(): lax.psum(partials[0].astype(jnp.float32).astype(jnp.bfloat16), 'grp')]
    all_gather x2 -> x0, waiting for transfers between devices: 94.7 us -> none  [the longest x1 48.1 us: per_device(): lax.all_gather(projected_half, 'shard', axis=0, tiled=True)]
    reduce_scatter x1 -> x0, waiting for transfers between devices: 82.4 us -> none  [per_device(): lax.psum_scatter(jnp.einsum('dmf,dmk->fmk', column_block, subspace, prefe...]
    ppermute x0 -> x42, waiting for transfers between devices: none -> 63.5 us  [swap(): return lax.ppermute(x, axis, [(i, i ^ bit) for i in range(size)])]
    ppermute x0 -> x42, starting transfers between devices: none -> 42.6 us  [swap(): return lax.ppermute(x, axis, [(i, i ^ bit) for i in range(size)])]
    pallas_call x0 -> x16, Pallas kernels: none -> 32.8 us  [the longest x4 12.7 us: pack(): pl.pallas_call(body, grid_spec=pltpu.PrefetchScalarGridSpec(num_scalar_pr...]
    dot_general x6 -> x0, matrix products: 24.5 us -> none  [the longest x1 8.72 us: per_device(): jnp.einsum('dmk,fmk->dmf', subspace, lax.all_gather(direction, 'shard', a...]
    unnamed x15 -> x22, local copies, waits for them, and re-layouts: 23 us -> 7.55 us
  transfers between devices with their start and end apart: 6 -> 42, of which waited for: 6 -> 11; matrix products, arithmetic and copies ran while one was open for 6% -> 1% of each run, Pallas kernels for 0% -> 18%
where the time goes in v2:
time: 150 us; the launch traced here: 149 us
  waiting for transfers between devices  63.5 us (42%)
  starting transfers between devices  42.6 us (28%)
  Pallas kernels  32.8 us (22%)
  local copies, waits for them, and re-layouts  9.32 us (6%)
    ppermute x42, waiting for transfers between devices, swap(): return lax.ppermute(x, axis, [(i, i ^ bit) for i in range(size)])  63.5 us
    ppermute x42, starting transfers between devices, swap(): return lax.ppermute(x, axis, [(i, i ^ bit) for i in range(size)])  42.6 us
    pallas_call x4, Pallas kernels, pack(): pl.pallas_call(body, grid_spec=pltpu.PrefetchScalarGridSpec(num_scalar_pr...  12.7 us
    pallas_call x1, Pallas kernels, update(): pl.pallas_call(body, grid_spec=pltpu.PrefetchScalarGridSpec(num_scalar_pr...  9.48 us
    unnamed x22, local copies, waits for them, and re-layouts  7.55 us
    pallas_call x10, Pallas kernels, call(): pl.pallas_call(body, in_specs=[SMEM] * len(scalars) + [VMEM] * len(args),...  6.98 us
    pallas_call x1, Pallas kernels, moments(): pl.pallas_call(body, in_specs=[SMEM] + [VMEM] * 6, out_specs=(VMEM,) * 4,...  3.65 us
  transfers between devices with their start and end apart: 42, of which 11 were waited for; matrix products, arithmetic and copies ran while one was open for 1% of the time, Pallas kernels for 18%

profile of v2, /device:TPU:1, one launch (start us, length us, event | category | flops | bytes accessed | tf_op | source)
XLA Modules:
  0.0 149.4 jit_solution(8884582363877097022)
XLA Ops:
  0.7 1.9 %copy-done = bf16[1,192,2,4096]{3,2,1,0:T(2,128)(2,1)S(1)} copy-done((bf16[1,192,2,4096]{3,2,1,0:T(2,128)(2,1)S(1)}, bf16[1,192,2,4096]{3,2,1,0:T(2,128)(2,1)}, u32[]{:S(2)}) %copy-start) | copy-done | bytes 3145752
  2.6 3.3 %shard_map.87 = (bf16[4,384,128]{2,1,0:T(8,128)(2,1)S(1)}, bf16[4,384,128]{2,1,0:T(8,128)(2,1)}) custom-call(s32[3]{0:T(128)S(1)} %pad_add_fusion.place_ref, bf16[192,2,4096]{2,1,0:T(2,128)(2,1)S(1)} %bitcast.7), custom_call_target="tpu_custom_call" | custom-call | tf_op jit(solution)/shard_map/pallas_call | solution.py:110
  5.9 3.0 %collective-permute-start.7 = (bf16[4,384,128]{2,1,0:T(8,128)(2,1)S(1)}, bf16[4,384,128]{2,1,0:T(8,128)(2,1)S(1)}, u32[]{:S(2)}, u32[]{:S(2)}) collective-permute-start(bf16[4,384,128]{2,1,0:T(8,128)(2,1)S(1)} %get-tuple-element.42), channel_id=1, source_target_pairs={{0,24},{8,16},{16,8},{24,0},{1,25},{9,17},{17,9},{25,1},{2,26},{10... | collective-permute-start | bytes 1179656 | tf_op jit(solution)/shard_map/ppermute | solution.py:64
  8.9 3.4 %shard_map.86 = (bf16[4,384,128]{2,1,0:T(8,128)(2,1)}, bf16[4,384,128]{2,1,0:T(8,128)(2,1)}) custom-call(s32[3]{0:T(128)S(1)} %pad_add_fusion.place_ref, bf16[192,2,4096]{2,1,0:T(2,128)(2,1)S(1)} %bitcast.8), custom_call_target="tpu_custom_call" | custom-call | tf_op jit(solution)/shard_map/pallas_call | solution.py:110
  12.4 1.4 collective-permute-start.1
  13.8 3.4 %shard_map.85 = (bf16[4,384,128]{2,1,0:T(8,128)(2,1)}, bf16[4,384,128]{2,1,0:T(8,128)(2,1)}) custom-call(s32[3]{0:T(128)S(1)} %pad_add_fusion.place_ref, bf16[192,2,4096]{2,1,0:T(2,128)(2,1)S(1)} %bitcast.9), custom_call_target="tpu_custom_call" | custom-call | tf_op jit(solution)/shard_map/pallas_call | solution.py:110
  17.2 1.4 collective-permute-start
  19.6 2.6 %shard_map.84 = (bf16[4,384,128]{2,1,0:T(8,128)(2,1)S(1)}, bf16[4,384,128]{2,1,0:T(8,128)(2,1)S(1)}) custom-call(s32[3]{0:T(128)S(1)} %pad_add_fusion.place_ref, bf16[192,2,4096]{2,1,0:T(2,128)(2,1)S(1)} %bitcast.10), custom_call_target="tpu_custom_call" | custom-call | tf_op jit(solution)/shard_map/pallas_call | solution.py:110
  23.0 0.8 copy-done.7
  23.7 1.0 reshape.14
  25.0 18.8 %collective-permute-done.6.c_ref = bf16[4,384,128]{2,1,0:T(8,128)(2,1)} collective-permute-done((bf16[4,384,128]{2,1,0:T(8,128)(2,1)}, bf16[4,384,128]{2,1,0:T(8,128)(2,1)}, u32[]{:S(2)}, u32[]{:S(2)}) %collective-permute-start.6) | collective-permute-done | bytes 393248 | tf_op jit(solution)/shard_map/ppermute | solution.py:64
  43.9 1.0 copy-done.4
  44.8 1.0 copy-done.8
  45.8 1.6 %shard_map.90 = (bf16[4,384,128]{2,1,0:T(8,128)(2,1)S(1)}, f32[2,128,512]{2,1,0:T(8,128)S(1)}, bf16[2,128,512]{2,1,0:T(8,128)(2,1)S(1)}) custom-call(bf16[4,384,128]{2,1,0:T(8,128)(2,1)S(1)} %copy-done.8, bf16[4,384,128]{2,1,0:T(8,128)(2,1)} %collective-permute-done.5.b_ref, bf16[4,384,128]{2,1,0:T(8,128)(2,1)} %collective-permute-done.6.c_ref, ...), custom_call_target="tpu_custom_call" | custom-call | tf_op jit(solution)/shard_map/pallas_call | solution.py:79
  47.5 0.8 collective-permute-start.8
  48.4 1.4 copy-done.6
  50.4 2.3 %collective-permute-start.9 = (bf16[128,512]{1,0:T(8,128)(2,1)S(1)}, bf16[128,512]{1,0:T(8,128)(2,1)S(1)}, u32[]{:S(2)}, u32[]{:S(2)}) collective-permute-start(bf16[128,512]{1,0:T(8,128)(2,1)S(1)} %get-tuple-element.45), channel_id=1, source_target_pairs={{0,4},{1,5},{2,6},{3,7},{4,0},{5,1},{6,2},{7,3},{8,12},{9,13},{10,... | collective-permute-start | bytes 393224 | tf_op jit(solution)/shard_map/ppermute | solution.py:64
  52.8 1.1 collective-permute-start.10
  54.2 7.5 %collective-permute-done.9.c_ref = bf16[128,512]{1,0:T(8,128)(2,1)S(1)} collective-permute-done((bf16[128,512]{1,0:T(8,128)(2,1)S(1)}, bf16[128,512]{1,0:T(8,128)(2,1)S(1)}, u32[]{:S(2)}, u32[]{:S(2)}) %collective-permute-start.9) | collective-permute-done | bytes 131104 | tf_op jit(solution)/shard_map/ppermute | solution.py:64
  62.3 4.0 %collective-permute-start.29 = (bf16[128,512]{1,0:T(8,128)(2,1)S(1)}, bf16[128,512]{1,0:T(8,128)(2,1)S(1)}, u32[]{:S(2)}, u32[]{:S(2)}) collective-permute-start(bf16[128,512]{1,0:T(8,128)(2,1)S(1)} %shard_map.92.a_ref.refs_0_), channel_id=1, source_target_pairs={{0,6},{1,7},{2,4},{3,5},{4,2},{5,3},{6,0},{7,1},{8,14},{9,15},{10,... | collective-permute-start | bytes 393224 | tf_op jit(solution)/shard_map/ppermute | solution.py:64
  66.3 1.5 collective-permute-start.28
  68.0 1.0 collective-permute-start.30
  69.0 2.8 %collective-permute-start.33 = (bf16[128,512]{1,0:T(8,128)(2,1)S(1)}, bf16[128,512]{1,0:T(8,128)(2,1)S(1)}, u32[]{:S(2)}, u32[]{:S(2)}) collective-permute-start(bf16[128,512]{1,0:T(8,128)(2,1)S(1)} %collective-permute-done.29.refs_3_), channel_id=1, source_target_pairs={{0,1},{1,0},{2,3},{3,2},{4,5},{5,4},{6,7},{7,6},{8,9},{9,8},{10,11... | collective-permute-start | bytes 393224 | tf_op jit(solution)/shard_map/ppermute | solution.py:64
  71.8 6.4 %collective-permute-done.28.refs_2_ = bf16[128,512]{1,0:T(8,128)(2,1)S(1)} collective-permute-done((bf16[128,512]{1,0:T(8,128)(2,1)S(1)}, bf16[128,512]{1,0:T(8,128)(2,1)S(1)}, u32[]{:S(2)}, u32[]{:S(2)}) %collective-permute-start.28) | collective-permute-done | bytes 131104 | tf_op jit(solution)/shard_map/ppermute | solution.py:64
  78.2 1.0 collective-permute-start.32
  79.2 2.0 %collective-permute-start.13 = (bf16[128,512]{1,0:T(8,128)(2,1)S(1)}, bf16[128,512]{1,0:T(8,128)(2,1)S(1)}, u32[]{:S(2)}, u32[]{:S(2)}) collective-permute-start(bf16[128,512]{1,0:T(8,128)(2,1)S(1)} %shard_map.92.a_ref.refs_0_), channel_id=1, source_target_pairs={{0,24},{8,16},{16,8},{24,0},{1,25},{9,17},{17,9},{25,1},{2,26},{10... | collective-permute-start | bytes 393224 | tf_op jit(solution)/shard_map/ppermute | solution.py:64
  81.2 1.0 shard_map.95.a_ref
  82.2 1.4 collective-permute-start.36
  84.0 1.0 collective-permute-start.11
  85.3 1.2 collective-permute-start.34
  86.5 6.3 %collective-permute-done.12.c_ref = bf16[128,512]{1,0:T(8,128)(2,1)S(1)} collective-permute-done((bf16[128,512]{1,0:T(8,128)(2,1)S(1)}, bf16[128,512]{1,0:T(8,128)(2,1)S(1)}, u32[]{:S(2)}, u32[]{:S(2)}) %collective-permute-start.12) | collective-permute-done | bytes 131104 | tf_op jit(solution)/shard_map/ppermute | solution.py:64
  92.8 3.7 %shard_map.93 = (f32[512,2,256]{2,1,0:T(2,128)}, f32[512,2,256]{2,1,0:T(2,128)}, bf16[128,512]{1,0:T(8,128)(2,1)S(1)}, bf16[4,128,512]{2,1,0:T(8,128)(2,1)S(1)}) custom-call(s32[3]{0:T(128)S(1)} %pad_add_fusion.place_ref, bf16[128,512]{1,0:T(8,128)(2,1)S(1)} %shard_map.92.a_ref.refs_0_, bf16[128,512]{1,0:T(8,128)(2,1)S(1)} %collective-permute-done.11.b_ref, ...), custom_call_target="tpu_custom_call" | custom-call | tf_op jit(solution)/shard_map/pallas_call | solution.py:181
  96.5 3.3 %collective-permute-start.16 = (bf16[128,512]{1,0:T(8,128)(2,1)S(1)}, bf16[128,512]{1,0:T(8,128)(2,1)S(1)}, u32[]{:S(2)}, u32[]{:S(2)}) collective-permute-start(bf16[128,512]{1,0:T(8,128)(2,1)S(1)} %get-tuple-element.48), channel_id=1, source_target_pairs={{0,6},{1,7},{2,4},{3,5},{4,2},{5,3},{6,0},{7,1},{8,14},{9,15},{10,... | collective-permute-start | bytes 393224 | tf_op jit(solution)/shard_map/ppermute | solution.py:64
  100.1 1.7 %shard_map.96 = (f32[384,256]{1,0:T(8,128)S(1)}, f32[256,256]{1,0:T(8,128)S(1)}, f32[256,256]{1,0:T(8,128)S(1)}) custom-call(s32[3]{0:T(128)S(1)} %pad_add_fusion.place_ref, bf16[384,256]{1,0:T(8,128)(2,1)S(1)} %shard_map.95.a_ref, bf16[384,256]{1,0:T(8,128)(2,1)S(1)} %collective-permute-done.34.b_ref, bf16[384,256]{1,0:T(8,128)(2,1)S(1)} %collective-permute-done.35.c_ref, ...), custom_call_target="tpu_custom_call" | custom-call | tf_op jit(solution)/shard_map/pallas_call | solution.py:79
  101.8 1.9 %collective-permute-start.37 = (f32[256,256]{1,0:T(8,128)S(1)}, f32[256,256]{1,0:T(8,128)S(1)}, u32[]{:S(2)}, u32[]{:S(2)}) collective-permute-start(f32[256,256]{1,0:T(8,128)S(1)} %get-tuple-element.55), channel_id=1, source_target_pairs={{0,1},{1,0},{2,3},{3,2},{4,5},{5,4},{6,7},{7,6},{8,9},{9,8},{10,11... | collective-permute-start | bytes 786440 | tf_op jit(solution)/shard_map/ppermute | solution.py:64
  103.7 5.9 %collective-permute-done.15.refs_2_ = bf16[128,512]{1,0:T(8,128)(2,1)S(1)} collective-permute-done((bf16[128,512]{1,0:T(8,128)(2,1)S(1)}, bf16[128,512]{1,0:T(8,128)(2,1)S(1)}, u32[]{:S(2)}, u32[]{:S(2)}) %collective-permute-start.15) | collective-permute-done | bytes 131104 | tf_op jit(solution)/shard_map/ppermute | solution.py:64
  109.6 1.8 %collective-permute-start.19 = (bf16[3,128,512]{2,1,0:T(8,128)(2,1)S(1)}, bf16[3,128,512]{2,1,0:T(8,128)(2,1)S(1)}, u32[]{:S(2)}, u32[]{:S(2)}) collective-permute-start(bf16[3,128,512]{2,1,0:T(8,128)(2,1)S(1)} %pad_maximum_fusion.1), channel_id=1, source_target_pairs={{0,24},{8,16},{16,8},{24,0},{1,25},{9,17},{17,9},{25,1},{2,26},{10... | collective-permute-start | bytes 1179656 | tf_op jit(solution)/shard_map/ppermute | solution.py:64
  112.3 2.3 %collective-permute-start.23 = (bf16[128,512]{1,0:T(8,128)(2,1)S(1)}, bf16[128,512]{1,0:T(8,128)(2,1)S(1)}, u32[]{:S(2)}, u32[]{:S(2)}) collective-permute-start(bf16[128,512]{1,0:T(8,128)(2,1)S(1)} %collective-permute-done.16.refs_3_), channel_id=1, source_target_pairs={{0,1},{1,0},{2,3},{3,2},{4,5},{5,4},{6,7},{7,6},{8,9},{9,8},{10,11... | collective-permute-start | bytes 393224 | tf_op jit(solution)/shard_map/ppermute | solution.py:64
  114.7 0.9 collective-permute-done.23.refs_10_
  116.0 1.2 collective-permute-start.40
  117.2 2.6 %collective-permute-done.19.refs_6_ = bf16[3,128,512]{2,1,0:T(8,128)(2,1)S(1)} collective-permute-done((bf16[3,128,512]{2,1,0:T(8,128)(2,1)S(1)}, bf16[3,128,512]{2,1,0:T(8,128)(2,1)S(1)}, u32[]{:S(2)}, u32[]{:S(2)}) %collective-permute-start.19) | collective-permute-done | bytes 393248 | tf_op jit(solution)/shard_map/ppermute | solution.py:64
  119.7 10.3 %collective-permute-done.18.refs_5_ = bf16[3,128,512]{2,1,0:T(8,128)(2,1)S(1)} collective-permute-done((bf16[3,128,512]{2,1,0:T(8,128)(2,1)S(1)}, bf16[3,128,512]{2,1,0:T(8,128)(2,1)S(1)}, u32[]{:S(2)}, u32[]{:S(2)}) %collective-permute-start.18) | collective-permute-done | bytes 393248 | tf_op jit(solution)/shard_map/ppermute | solution.py:64
  131.4 3.2 %collective-permute-done.38.b_ref = bf16[256,256]{1,0:T(8,128)(2,1)S(1)} collective-permute-done((bf16[256,256]{1,0:T(8,128)(2,1)S(1)}, bf16[256,256]{1,0:T(8,128)(2,1)S(1)}, u32[]{:S(2)}, u32[]{:S(2)}) %collective-permute-start.38) | collective-permute-done | bytes 131104 | tf_op jit(solution)/shard_map/ppermute | solution.py:64
  134.6 1.3 collective-permute-start.21
  136.0 0.9 collective-permute-done.21.refs_8_
  137.3 9.5 %shard_map.94 = f32[192,2,4096]{2,1,0:T(2,128)} custom-call(s32[3]{0:T(128)S(1)} %pad_add_fusion.place_ref, f32[192,2,4096]{2,1,0:T(2,128)S(1)} %bitcast.12, bf16[384,512]{1,0:T(8,128)(2,1)S(1)} %pad_maximum_fusion.s_ref, bf16[4,128,512]{2,1,0:T(8,128)(2,1)S(1)} %get-tuple-element.47.refs_0_, bf16[128,512]{1,0:T(8,128)(2,1)S(1)} %collective-permute-done.14.refs_1_, ...), custom_call_target="tpu_custom_call" | custom-call | tf_op jit(solution)/shard_map/pallas_call | solution.py:305
  146.8 1.8 %shard_map.99 = bf16[384,256]{1,0:T(8,128)(2,1)S(1)} custom-call(s32[3]{0:T(128)S(1)} %pad_add_fusion.place_ref, f32[384,256]{1,0:T(8,128)S(1)} %get-tuple-element.53.spanned_ref, f32[256,256]{1,0:T(8,128)S(1)} %shard_map.98.own_ref, f32[256,256]{1,0:T(8,128)S(1)} %collective-permute-done.41.other_ref), custom_call_target="tpu_custom_call" | custom-call | tf_op jit(solution)/shard_map/pallas_call | solution.py:79
  148.7 0.8 reshape.15
  (83 shorter events, 8.3 us)
Async XLA Ops:
  0.7 1.9 %copy-start = (bf16[1,192,2,4096]{3,2,1,0:T(2,128)(2,1)S(1)}, bf16[1,192,2,4096]{3,2,1,0:T(2,128)(2,1)}, u32[]{:S(2)}) copy-start(bf16[1,192,2,4096]{3,2,1,0:T(2,128)(2,1)} %param.5) | copy-start | bytes 9437188
  5.9 12.7 %collective-permute-start.7 = (bf16[4,384,128]{2,1,0:T(8,128)(2,1)S(1)}, bf16[4,384,128]{2,1,0:T(8,128)(2,1)S(1)}, u32[]{:S(2)}, u32[]{:S(2)}) collective-permute-start(bf16[4,384,128]{2,1,0:T(8,128)(2,1)S(1)} %get-tuple-element.42), channel_id=1, source_target_pairs={{0,24},{8,16},{16,8},{24,0},{1,25},{9,17},{17,9},{25,1},{2,26},{10... | collective-permute-start | bytes 1179656 | tf_op jit(solution)/shard_map/ppermute | solution.py:64
  8.9 39.5 %collective-permute-start.2 = (bf16[4,384,128]{2,1,0:T(8,128)(2,1)}, bf16[4,384,128]{2,1,0:T(8,128)(2,1)S(1)}, u32[]{:S(2)}, u32[]{:S(2)}) collective-permute-start(bf16[4,384,128]{2,1,0:T(8,128)(2,1)} %get-tuple-element.34), channel_id=1, source_target_pairs={{0,24},{8,16},{16,8},{24,0},{1,25},{9,17},{17,9},{25,1},{2,26},{10... | collective-permute-start | bytes 1179656 | tf_op jit(solution)/shard_map/ppermute | solution.py:64
  12.4 36.0 %collective-permute-start.1 = (bf16[4,384,128]{2,1,0:T(8,128)(2,1)}, bf16[4,384,128]{2,1,0:T(8,128)(2,1)S(1)}, u32[]{:S(2)}, u32[]{:S(2)}) collective-permute-start(bf16[4,384,128]{2,1,0:T(8,128)(2,1)} %get-tuple-element.33), channel_id=1, source_target_pairs={{0,16},{8,24},{16,0},{24,8},{1,17},{9,25},{17,1},{25,9},{2,18},{10... | collective-permute-start | bytes 1179656 | tf_op jit(solution)/shard_map/ppermute | solution.py:64
  13.8 30.1 %collective-permute-start.6 = (bf16[4,384,128]{2,1,0:T(8,128)(2,1)}, bf16[4,384,128]{2,1,0:T(8,128)(2,1)}, u32[]{:S(2)}, u32[]{:S(2)}) collective-permute-start(bf16[4,384,128]{2,1,0:T(8,128)(2,1)} %get-tuple-element.41), channel_id=1, source_target_pairs={{0,16},{8,24},{16,0},{24,8},{1,17},{9,25},{17,1},{25,9},{2,18},{10... | collective-permute-start | bytes 1179656 | tf_op jit(solution)/shard_map/ppermute | solution.py:64
  17.2 31.1 %collective-permute-start = (bf16[4,384,128]{2,1,0:T(8,128)(2,1)}, bf16[4,384,128]{2,1,0:T(8,128)(2,1)S(1)}, u32[]{:S(2)}, u32[]{:S(2)}) collective-permute-start(bf16[4,384,128]{2,1,0:T(8,128)(2,1)} %get-tuple-element.32), channel_id=1, source_target_pairs={{0,8},{8,0},{16,24},{24,16},{1,9},{9,1},{17,25},{25,17},{2,10},{10... | collective-permute-start | bytes 1179656 | tf_op jit(solution)/shard_map/ppermute | solution.py:64
  19.4 24.5 %collective-permute-start.5 = (bf16[4,384,128]{2,1,0:T(8,128)(2,1)}, bf16[4,384,128]{2,1,0:T(8,128)(2,1)}, u32[]{:S(2)}, u32[]{:S(2)}) collective-permute-start(bf16[4,384,128]{2,1,0:T(8,128)(2,1)} %get-tuple-element.40), channel_id=1, source_target_pairs={{0,8},{8,0},{16,24},{24,16},{1,9},{9,1},{17,25},{25,17},{2,10},{10... | collective-permute-start | bytes 1179656 | tf_op jit(solution)/shard_map/ppermute | solution.py:64
  19.6 73.2 %copy-start.1 = (f32[512,2,256]{2,1,0:T(2,128)S(1)}, f32[512,2,256]{2,1,0:T(2,128)}, u32[]{:S(2)}) copy-start(f32[512,2,256]{2,1,0:T(2,128)} %one_ref.1) | copy-start | bytes 3145732
  19.6 73.2 %copy-start.2 = (f32[512,2,256]{2,1,0:T(2,128)S(1)}, f32[512,2,256]{2,1,0:T(2,128)}, u32[]{:S(2)}) copy-start(f32[512,2,256]{2,1,0:T(2,128)} %two_ref.1) | copy-start | bytes 3145732
  47.5 89.8 %slice-start = ((s8[6291456]{0:T(1024)(128)(4,1)}), s8[4194304]{0:T(1024)(128)(4,1)S(1)}, s32[]{:S(2)}) async-start(s8[6291456]{0:T(1024)(128)(4,1)} %bitcast.11), calls=%async_computation | async-start | bytes 8388608
  47.5 2.9 %collective-permute-start.8 = (bf16[2,128,512]{2,1,0:T(8,128)(2,1)S(1)}, bf16[2,128,512]{2,1,0:T(8,128)(2,1)S(1)}, u32[]{:S(2)}, u32[]{:S(2)}) collective-permute-start(bf16[2,128,512]{2,1,0:T(8,128)(2,1)S(1)} %get-tuple-element.44), channel_id=1, source_target_pairs={{0,1},{1,0},{2,3},{3,2},{4,5},{5,4},{6,7},{7,6},{8,9},{9,8},{10,11... | collective-permute-start | bytes 786440 | tf_op jit(solution)/shard_map/ppermute | solution.py:64
  48.4 1.4 copy-start.6
  50.3 3.6 %collective-permute-start.3 = (bf16[2,128,512]{2,1,0:T(8,128)(2,1)S(1)}, bf16[2,128,512]{2,1,0:T(8,128)(2,1)S(1)}, u32[]{:S(2)}, u32[]{:S(2)}) collective-permute-start(bf16[2,128,512]{2,1,0:T(8,128)(2,1)S(1)} %get-tuple-element.36), channel_id=1, source_target_pairs={{0,1},{1,0},{2,3},{3,2},{4,5},{5,4},{6,7},{7,6},{8,9},{9,8},{10,11... | collective-permute-start | bytes 786440 | tf_op jit(solution)/shard_map/ppermute | solution.py:64
  50.4 11.2 %collective-permute-start.9 = (bf16[128,512]{1,0:T(8,128)(2,1)S(1)}, bf16[128,512]{1,0:T(8,128)(2,1)S(1)}, u32[]{:S(2)}, u32[]{:S(2)}) collective-permute-start(bf16[128,512]{1,0:T(8,128)(2,1)S(1)} %get-tuple-element.45), channel_id=1, source_target_pairs={{0,4},{1,5},{2,6},{3,7},{4,0},{5,1},{6,2},{7,3},{8,12},{9,13},{10,... | collective-permute-start | bytes 393224 | tf_op jit(solution)/shard_map/ppermute | solution.py:64
  52.8 8.9 %collective-permute-start.10 = (bf16[128,512]{1,0:T(8,128)(2,1)S(1)}, bf16[128,512]{1,0:T(8,128)(2,1)S(1)}, u32[]{:S(2)}, u32[]{:S(2)}) collective-permute-start(bf16[128,512]{1,0:T(8,128)(2,1)S(1)} %get-tuple-element.46), channel_id=1, source_target_pairs={{0,6},{1,7},{2,4},{3,5},{4,2},{5,3},{6,0},{7,1},{8,14},{9,15},{10,... | collective-permute-start | bytes 393224 | tf_op jit(solution)/shard_map/ppermute | solution.py:64
  53.9 8.4 %collective-permute-start.4 = (bf16[128,512]{1,0:T(8,128)(2,1)S(1)}, bf16[128,512]{1,0:T(8,128)(2,1)S(1)}, u32[]{:S(2)}, u32[]{:S(2)}) collective-permute-start(bf16[128,512]{1,0:T(8,128)(2,1)S(1)} %get-tuple-element.38), channel_id=1, source_target_pairs={{0,2},{1,3},{2,0},{3,1},{4,6},{5,7},{6,4},{7,5},{8,10},{9,11},{10,... | collective-permute-start | bytes 393224 | tf_op jit(solution)/shard_map/ppermute | solution.py:64
  62.3 6.7 %collective-permute-start.29 = (bf16[128,512]{1,0:T(8,128)(2,1)S(1)}, bf16[128,512]{1,0:T(8,128)(2,1)S(1)}, u32[]{:S(2)}, u32[]{:S(2)}) collective-permute-start(bf16[128,512]{1,0:T(8,128)(2,1)S(1)} %shard_map.92.a_ref.refs_0_), channel_id=1, source_target_pairs={{0,6},{1,7},{2,4},{3,5},{4,2},{5,3},{6,0},{7,1},{8,14},{9,15},{10,... | collective-permute-start | bytes 393224 | tf_op jit(solution)/shard_map/ppermute | solution.py:64
  66.3 11.9 %collective-permute-start.28 = (bf16[128,512]{1,0:T(8,128)(2,1)S(1)}, bf16[128,512]{1,0:T(8,128)(2,1)S(1)}, u32[]{:S(2)}, u32[]{:S(2)}) collective-permute-start(bf16[128,512]{1,0:T(8,128)(2,1)S(1)} %shard_map.92.a_ref.refs_0_), channel_id=1, source_target_pairs={{0,4},{1,5},{2,6},{3,7},{4,0},{5,1},{6,2},{7,3},{8,12},{9,13},{10,... | collective-permute-start | bytes 393224 | tf_op jit(solution)/shard_map/ppermute | solution.py:64
  67.8 11.4 %collective-permute-start.27 = (bf16[128,512]{1,0:T(8,128)(2,1)S(1)}, bf16[128,512]{1,0:T(8,128)(2,1)S(1)}, u32[]{:S(2)}, u32[]{:S(2)}) collective-permute-start(bf16[128,512]{1,0:T(8,128)(2,1)S(1)} %shard_map.92.a_ref.refs_0_), channel_id=1, source_target_pairs={{0,2},{1,3},{2,0},{3,1},{4,6},{5,7},{6,4},{7,5},{8,10},{9,11},{10,... | collective-permute-start | bytes 393224 | tf_op jit(solution)/shard_map/ppermute | solution.py:64
  68.0 13.2 %collective-permute-start.30 = (bf16[128,512]{1,0:T(8,128)(2,1)S(1)}, bf16[128,512]{1,0:T(8,128)(2,1)S(1)}, u32[]{:S(2)}, u32[]{:S(2)}) collective-permute-start(bf16[128,512]{1,0:T(8,128)(2,1)S(1)} %shard_map.92.a_ref.refs_0_), channel_id=1, source_target_pairs={{0,1},{1,0},{2,3},{3,2},{4,5},{5,4},{6,7},{7,6},{8,9},{9,8},{10,11... | collective-permute-start | bytes 393224 | tf_op jit(solution)/shard_map/ppermute | solution.py:64
  69.0 12.2 %collective-permute-start.33 = (bf16[128,512]{1,0:T(8,128)(2,1)S(1)}, bf16[128,512]{1,0:T(8,128)(2,1)S(1)}, u32[]{:S(2)}, u32[]{:S(2)}) collective-permute-start(bf16[128,512]{1,0:T(8,128)(2,1)S(1)} %collective-permute-done.29.refs_3_), channel_id=1, source_target_pairs={{0,1},{1,0},{2,3},{3,2},{4,5},{5,4},{6,7},{7,6},{8,9},{9,8},{10,11... | collective-permute-start | bytes 393224 | tf_op jit(solution)/shard_map/ppermute | solution.py:64
  78.2 3.0 %collective-permute-start.32 = (bf16[128,512]{1,0:T(8,128)(2,1)S(1)}, bf16[128,512]{1,0:T(8,128)(2,1)S(1)}, u32[]{:S(2)}, u32[]{:S(2)}) collective-permute-start(bf16[128,512]{1,0:T(8,128)(2,1)S(1)} %collective-permute-done.28.refs_2_), channel_id=1, source_target_pairs={{0,1},{1,0},{2,3},{3,2},{4,5},{5,4},{6,7},{7,6},{8,9},{9,8},{10,11... | collective-permute-start | bytes 393224 | tf_op jit(solution)/shard_map/ppermute | solution.py:64
  79.2 2.0 %collective-permute-start.31 = (bf16[128,512]{1,0:T(8,128)(2,1)S(1)}, bf16[128,512]{1,0:T(8,128)(2,1)S(1)}, u32[]{:S(2)}, u32[]{:S(2)}) collective-permute-start(bf16[128,512]{1,0:T(8,128)(2,1)S(1)} %collective-permute-done.27.refs_1_), channel_id=1, source_target_pairs={{0,1},{1,0},{2,3},{3,2},{4,5},{5,4},{6,7},{7,6},{8,9},{9,8},{10,11... | collective-permute-start | bytes 393224 | tf_op jit(solution)/shard_map/ppermute | solution.py:64
  79.2 6.1 %collective-permute-start.13 = (bf16[128,512]{1,0:T(8,128)(2,1)S(1)}, bf16[128,512]{1,0:T(8,128)(2,1)S(1)}, u32[]{:S(2)}, u32[]{:S(2)}) collective-permute-start(bf16[128,512]{1,0:T(8,128)(2,1)S(1)} %shard_map.92.a_ref.refs_0_), channel_id=1, source_target_pairs={{0,24},{8,16},{16,8},{24,0},{1,25},{9,17},{17,9},{25,1},{2,26},{10... | collective-permute-start | bytes 393224 | tf_op jit(solution)/shard_map/ppermute | solution.py:64
  81.2 56.1 %slice-start.1 = ((s8[6291456]{0:T(1024)(128)(4,1)}), s8[2097152]{0:T(1024)(128)(4,1)S(1)}, s32[]{:S(2)}) async-start(s8[6291456]{0:T(1024)(128)(4,1)} %bitcast.11), calls=%async_computation.1 | async-start | bytes 4194304
  82.2 17.6 %collective-permute-start.36 = (bf16[384,256]{1,0:T(8,128)(2,1)S(1)}, bf16[384,256]{1,0:T(8,128)(2,1)S(1)}, u32[]{:S(2)}, u32[]{:S(2)}) collective-permute-start(bf16[384,256]{1,0:T(8,128)(2,1)S(1)} %shard_map.95.a_ref), channel_id=1, source_target_pairs={{0,24},{8,16},{16,8},{24,0},{1,25},{9,17},{17,9},{25,1},{2,26},{10... | collective-permute-start | bytes 589832 | tf_op jit(solution)/shard_map/ppermute | solution.py:64
  83.6 9.2 %collective-permute-start.12 = (bf16[128,512]{1,0:T(8,128)(2,1)S(1)}, bf16[128,512]{1,0:T(8,128)(2,1)S(1)}, u32[]{:S(2)}, u32[]{:S(2)}) collective-permute-start(bf16[128,512]{1,0:T(8,128)(2,1)S(1)} %shard_map.92.a_ref.refs_0_), channel_id=1, source_target_pairs={{0,16},{8,24},{16,0},{24,8},{1,17},{9,25},{17,1},{25,9},{2,18},{10... | collective-permute-start | bytes 393224 | tf_op jit(solution)/shard_map/ppermute | solution.py:64
  84.0 8.9 %collective-permute-start.11 = (bf16[128,512]{1,0:T(8,128)(2,1)S(1)}, bf16[128,512]{1,0:T(8,128)(2,1)S(1)}, u32[]{:S(2)}, u32[]{:S(2)}) collective-permute-start(bf16[128,512]{1,0:T(8,128)(2,1)S(1)} %shard_map.92.a_ref.refs_0_), channel_id=1, source_target_pairs={{0,8},{8,0},{16,24},{24,16},{1,9},{9,1},{17,25},{25,17},{2,10},{10... | collective-permute-start | bytes 393224 | tf_op jit(solution)/shard_map/ppermute | solution.py:64
  84.9 15.1 %collective-permute-start.35 = (bf16[384,256]{1,0:T(8,128)(2,1)S(1)}, bf16[384,256]{1,0:T(8,128)(2,1)S(1)}, u32[]{:S(2)}, u32[]{:S(2)}) collective-permute-start(bf16[384,256]{1,0:T(8,128)(2,1)S(1)} %shard_map.95.a_ref), channel_id=1, source_target_pairs={{0,16},{8,24},{16,0},{24,8},{1,17},{9,25},{17,1},{25,9},{2,18},{10... | collective-permute-start | bytes 589832 | tf_op jit(solution)/shard_map/ppermute | solution.py:64
  85.3 14.8 %collective-permute-start.34 = (bf16[384,256]{1,0:T(8,128)(2,1)S(1)}, bf16[384,256]{1,0:T(8,128)(2,1)S(1)}, u32[]{:S(2)}, u32[]{:S(2)}) collective-permute-start(bf16[384,256]{1,0:T(8,128)(2,1)S(1)} %shard_map.95.a_ref), channel_id=1, source_target_pairs={{0,8},{8,0},{16,24},{24,16},{1,9},{9,1},{17,25},{25,17},{2,10},{10... | collective-permute-start | bytes 589832 | tf_op jit(solution)/shard_map/ppermute | solution.py:64
  96.5 7.2 %collective-permute-start.16 = (bf16[128,512]{1,0:T(8,128)(2,1)S(1)}, bf16[128,512]{1,0:T(8,128)(2,1)S(1)}, u32[]{:S(2)}, u32[]{:S(2)}) collective-permute-start(bf16[128,512]{1,0:T(8,128)(2,1)S(1)} %get-tuple-element.48), channel_id=1, source_target_pairs={{0,6},{1,7},{2,4},{3,5},{4,2},{5,3},{6,0},{7,1},{8,14},{9,15},{10,... | collective-permute-start | bytes 393224 | tf_op jit(solution)/shard_map/ppermute | solution.py:64
  99.8 9.8 %collective-permute-start.15 = (bf16[128,512]{1,0:T(8,128)(2,1)S(1)}, bf16[128,512]{1,0:T(8,128)(2,1)S(1)}, u32[]{:S(2)}, u32[]{:S(2)}) collective-permute-start(bf16[128,512]{1,0:T(8,128)(2,1)S(1)} %get-tuple-element.48), channel_id=1, source_target_pairs={{0,4},{1,5},{2,6},{3,7},{4,0},{5,1},{6,2},{7,3},{8,12},{9,13},{10,... | collective-permute-start | bytes 393224 | tf_op jit(solution)/shard_map/ppermute | solution.py:64
  99.8 9.8 %collective-permute-start.14 = (bf16[128,512]{1,0:T(8,128)(2,1)S(1)}, bf16[128,512]{1,0:T(8,128)(2,1)S(1)}, u32[]{:S(2)}, u32[]{:S(2)}) collective-permute-start(bf16[128,512]{1,0:T(8,128)(2,1)S(1)} %get-tuple-element.48), channel_id=1, source_target_pairs={{0,2},{1,3},{2,0},{3,1},{4,6},{5,7},{6,4},{7,5},{8,10},{9,11},{10,... | collective-permute-start | bytes 393224 | tf_op jit(solution)/shard_map/ppermute | solution.py:64
  101.8 12.8 %collective-permute-start.37 = (f32[256,256]{1,0:T(8,128)S(1)}, f32[256,256]{1,0:T(8,128)S(1)}, u32[]{:S(2)}, u32[]{:S(2)}) collective-permute-start(f32[256,256]{1,0:T(8,128)S(1)} %get-tuple-element.55), channel_id=1, source_target_pairs={{0,1},{1,0},{2,3},{3,2},{4,5},{5,4},{6,7},{7,6},{8,9},{9,8},{10,11... | collective-permute-start | bytes 786440 | tf_op jit(solution)/shard_map/ppermute | solution.py:64
  109.6 10.1 %collective-permute-start.19 = (bf16[3,128,512]{2,1,0:T(8,128)(2,1)S(1)}, bf16[3,128,512]{2,1,0:T(8,128)(2,1)S(1)}, u32[]{:S(2)}, u32[]{:S(2)}) collective-permute-start(bf16[3,128,512]{2,1,0:T(8,128)(2,1)S(1)} %pad_maximum_fusion.1), channel_id=1, source_target_pairs={{0,24},{8,16},{16,8},{24,0},{1,25},{9,17},{17,9},{25,1},{2,26},{10... | collective-permute-start | bytes 1179656 | tf_op jit(solution)/shard_map/ppermute | solution.py:64
  111.4 18.6 %collective-permute-start.18 = (bf16[3,128,512]{2,1,0:T(8,128)(2,1)S(1)}, bf16[3,128,512]{2,1,0:T(8,128)(2,1)S(1)}, u32[]{:S(2)}, u32[]{:S(2)}) collective-permute-start(bf16[3,128,512]{2,1,0:T(8,128)(2,1)S(1)} %pad_maximum_fusion.1), channel_id=1, source_target_pairs={{0,16},{8,24},{16,0},{24,8},{1,17},{9,25},{17,1},{25,9},{2,18},{10... | collective-permute-start | bytes 1179656 | tf_op jit(solution)/shard_map/ppermute | solution.py:64
  111.7 18.3 %collective-permute-start.17 = (bf16[3,128,512]{2,1,0:T(8,128)(2,1)S(1)}, bf16[3,128,512]{2,1,0:T(8,128)(2,1)S(1)}, u32[]{:S(2)}, u32[]{:S(2)}) collective-permute-start(bf16[3,128,512]{2,1,0:T(8,128)(2,1)S(1)} %pad_maximum_fusion.1), channel_id=1, source_target_pairs={{0,8},{8,0},{16,24},{24,16},{1,9},{9,1},{17,25},{25,17},{2,10},{10... | collective-permute-start | bytes 1179656 | tf_op jit(solution)/shard_map/ppermute | solution.py:64
  112.3 3.3 %collective-permute-start.23 = (bf16[128,512]{1,0:T(8,128)(2,1)S(1)}, bf16[128,512]{1,0:T(8,128)(2,1)S(1)}, u32[]{:S(2)}, u32[]{:S(2)}) collective-permute-start(bf16[128,512]{1,0:T(8,128)(2,1)S(1)} %collective-permute-done.16.refs_3_), channel_id=1, source_target_pairs={{0,1},{1,0},{2,3},{3,2},{4,5},{5,4},{6,7},{7,6},{8,9},{9,8},{10,11... | collective-permute-start | bytes 393224 | tf_op jit(solution)/shard_map/ppermute | solution.py:64
  114.6 1.3 collective-permute-start.22
  115.6 21.7 %collective-permute-start.20 = (bf16[4,128,512]{2,1,0:T(8,128)(2,1)S(1)}, bf16[4,128,512]{2,1,0:T(8,128)(2,1)S(1)}, u32[]{:S(2)}, u32[]{:S(2)}) collective-permute-start(bf16[4,128,512]{2,1,0:T(8,128)(2,1)S(1)} %get-tuple-element.47.refs_0_), channel_id=1, source_target_pairs={{0,1},{1,0},{2,3},{3,2},{4,5},{5,4},{6,7},{7,6},{8,9},{9,8},{10,11... | collective-permute-start | bytes 1572872 | tf_op jit(solution)/shard_map/ppermute | solution.py:64
  116.0 14.6 %collective-permute-start.40 = (bf16[256,256]{1,0:T(8,128)(2,1)S(1)}, bf16[256,256]{1,0:T(8,128)(2,1)S(1)}, u32[]{:S(2)}, u32[]{:S(2)}) collective-permute-start(bf16[256,256]{1,0:T(8,128)(2,1)S(1)} %get-tuple-element.57), channel_id=1, source_target_pairs={{0,6},{1,7},{2,4},{3,5},{4,2},{5,3},{6,0},{7,1},{8,14},{9,15},{10,... | collective-permute-start | bytes 393224 | tf_op jit(solution)/shard_map/ppermute | solution.py:64
  119.7 10.9 %collective-permute-start.39 = (bf16[256,256]{1,0:T(8,128)(2,1)S(1)}, bf16[256,256]{1,0:T(8,128)(2,1)S(1)}, u32[]{:S(2)}, u32[]{:S(2)}) collective-permute-start(bf16[256,256]{1,0:T(8,128)(2,1)S(1)} %get-tuple-element.57), channel_id=1, source_target_pairs={{0,4},{1,5},{2,6},{3,7},{4,0},{5,1},{6,2},{7,3},{8,12},{9,13},{10,... | collective-permute-start | bytes 393224 | tf_op jit(solution)/shard_map/ppermute | solution.py:64
  130.0 4.6 %collective-permute-start.38 = (bf16[256,256]{1,0:T(8,128)(2,1)S(1)}, bf16[256,256]{1,0:T(8,128)(2,1)S(1)}, u32[]{:S(2)}, u32[]{:S(2)}) collective-permute-start(bf16[256,256]{1,0:T(8,128)(2,1)S(1)} %get-tuple-element.57), channel_id=1, source_target_pairs={{0,2},{1,3},{2,0},{3,1},{4,6},{5,7},{6,4},{7,5},{8,10},{9,11},{10,... | collective-permute-start | bytes 393224 | tf_op jit(solution)/shard_map/ppermute | solution.py:64
  130.0 7.3 %collective-permute-start.26 = (bf16[3,128,512]{2,1,0:T(8,128)(2,1)S(1)}, bf16[3,128,512]{2,1,0:T(8,128)(2,1)S(1)}, u32[]{:S(2)}, u32[]{:S(2)}) collective-permute-start(bf16[3,128,512]{2,1,0:T(8,128)(2,1)S(1)} %collective-permute-done.19.refs_6_), channel_id=1, source_target_pairs={{0,1},{1,0},{2,3},{3,2},{4,5},{5,4},{6,7},{7,6},{8,9},{9,8},{10,11... | collective-permute-start | bytes 1179656 | tf_op jit(solution)/shard_map/ppermute | solution.py:64
  130.6 6.7 %collective-permute-start.25 = (bf16[3,128,512]{2,1,0:T(8,128)(2,1)S(1)}, bf16[3,128,512]{2,1,0:T(8,128)(2,1)S(1)}, u32[]{:S(2)}, u32[]{:S(2)}) collective-permute-start(bf16[3,128,512]{2,1,0:T(8,128)(2,1)S(1)} %collective-permute-done.18.refs_5_), channel_id=1, source_target_pairs={{0,1},{1,0},{2,3},{3,2},{4,5},{5,4},{6,7},{7,6},{8,9},{9,8},{10,11... | collective-permute-start | bytes 1179656 | tf_op jit(solution)/shard_map/ppermute | solution.py:64
  130.7 6.6 %collective-permute-start.24 = (bf16[3,128,512]{2,1,0:T(8,128)(2,1)S(1)}, bf16[3,128,512]{2,1,0:T(8,128)(2,1)S(1)}, u32[]{:S(2)}, u32[]{:S(2)}) collective-permute-start(bf16[3,128,512]{2,1,0:T(8,128)(2,1)S(1)} %collective-permute-done.17.refs_4_), channel_id=1, source_target_pairs={{0,1},{1,0},{2,3},{3,2},{4,5},{5,4},{6,7},{7,6},{8,9},{9,8},{10,11... | collective-permute-start | bytes 1179656 | tf_op jit(solution)/shard_map/ppermute | solution.py:64
  134.6 2.3 %collective-permute-start.21 = (bf16[128,512]{1,0:T(8,128)(2,1)S(1)}, bf16[128,512]{1,0:T(8,128)(2,1)S(1)}, u32[]{:S(2)}, u32[]{:S(2)}) collective-permute-start(bf16[128,512]{1,0:T(8,128)(2,1)S(1)} %collective-permute-done.14.refs_1_), channel_id=1, source_target_pairs={{0,1},{1,0},{2,3},{3,2},{4,5},{5,4},{6,7},{7,6},{8,9},{9,8},{10,11... | collective-permute-start | bytes 393224 | tf_op jit(solution)/shard_map/ppermute | solution.py:64
  136.9 9.9 %collective-permute-start.41 = (f32[256,256]{1,0:T(8,128)S(1)}, f32[256,256]{1,0:T(8,128)S(1)}, u32[]{:S(2)}, u32[]{:S(2)}) collective-permute-start(f32[256,256]{1,0:T(8,128)S(1)} %shard_map.98.own_ref), channel_id=1, source_target_pairs={{0,1},{1,0},{2,3},{3,2},{4,5},{5,4},{6,7},{7,6},{8,9},{9,8},{10,11... | collective-permute-start | bytes 786440 | tf_op jit(solution)/shard_map/ppermute | solution.py:64
  (5 other events, 4.3 us)

commit v3 on v2

--- a/solution.py
+++ b/solution.py
@@ -66,7 +66,7 @@
 
 VMEM = pl.BlockSpec(memory_space=pltpu.VMEM)
 SMEM = pl.BlockSpec(memory_space=pltpu.SMEM)
-PARAMS = pltpu.CompilerParams(vmem_limit_bytes=24 * 2**20)
+PARAMS = pltpu.CompilerParams(vmem_limit_bytes=16 * 2**20)
 xor = jnp.bitwise_xor
 
 
@@ -74,7 +74,11 @@
     return pltpu.with_memory_space_constraint(x, pltpu.VMEM)
 
 
-def call(body, outs, *args, place=None):
+def cost(us):
+    return pl.CostEstimate(flops=0, transcendentals=0, bytes_accessed=int(us * 3.5e6))
+
+
+def call(body, outs, *args, place=None, us=0.3):
     scalars = [] if place is None else [place]
     return pl.pallas_call(
         body,
@@ -82,45 +86,45 @@
         out_specs=(VMEM,) * len(outs),
         out_shape=tuple(pltpu.VMEM(shape, dtype) for shape, dtype in outs),
         compiler_params=PARAMS,
+        cost_estimate=cost(us),
     )(*scalars, *[pin(a) for a in args])
 
 
-def pack(place, x, a):
+def after(x, *others):
+    return lax.optimization_barrier((x, others))[0]
+
+
+def hbm(x):
+    return pltpu.with_memory_space_constraint(x, pltpu.HBM)
+
+
+def pack(place, x, half):
     rows = x.shape[0]
 
-    def body(place_ref, x_ref, high_ref, low_ref):
-        i = pl.program_id(0)
-        piece = x_ref[...].reshape(2 * rows, 128)
-
-        @pl.when(i < 4)
-        def _():
-            high_ref[i] = piece
-
-        @pl.when(i >= 4)
-        def _():
-            low_ref[i - 4] = piece
+    def body(place_ref, x_ref, *out_refs):
+        for a in range(4):
+            at = pl.ds(pl.multiple_of(xor(place_ref[0], a) * 128, 128), 128)
+            out_refs[a][pl.program_id(0)] = x_ref[:, :, at].reshape(2 * rows, 128)
 
     def where(i, place_ref):
-        k, l = 2 * (1 - i // 4) + i % 2, i // 2 % 2
-        shard = xor(place_ref[1], k) * 2 + xor(place_ref[2], l)
-        return 0, 0, shard * 4 + xor(place_ref[0], a)
-
-    half = pltpu.VMEM((4, 2 * rows, 128), bf16)
-    whole = pl.BlockSpec(memory_space=pltpu.VMEM)
+        k, l = 2 * half + i % 2, i // 2
+        return 0, 0, xor(place_ref[1], k) * 2 + xor(place_ref[2], l)
+
     return pl.pallas_call(
         body,
         grid_spec=pltpu.PrefetchScalarGridSpec(
             num_scalar_prefetch=1,
-            grid=(8,),
-            in_specs=[pl.BlockSpec((rows, 2, 128), where)],
-            out_specs=(whole, whole),
+            grid=(4,),
+            in_specs=[pl.BlockSpec((rows, 2, 512), where)],
+            out_specs=(VMEM,) * 4,
         ),
-        out_shape=(half, half),
+        out_shape=(pltpu.VMEM((4, 2 * rows, 128), bf16),) * 4,
         compiler_params=PARAMS,
-    )(place, x)
-
-
-def project(pieces, masked):
+        cost_estimate=cost(3.3),
+    )(place, hbm(x))
+
+
+def project(pieces, masked, us):
     rows = masked.shape[0]
 
     def body(a_ref, b_ref, c_ref, d_ref, s_ref, g_ref, keep_ref, send_ref):
@@ -143,6 +147,7 @@
         [((4, rows, 128), bf16), ((2, 128, 512), f32), ((2, 128, 512), bf16)],
         *pieces,
         masked,
+        us=us,
     )
 
 
@@ -164,31 +169,41 @@
     return call(body, [((128, 512), bf16)], *parts)[0]
 
 
+def own_direction(place, half, one, two):
+    def body(place_ref, half_ref, one_ref, two_ref, own_ref):
+        at = pl.ds(pl.multiple_of(place_ref[0] * 128, 128), 128)
+        for m in range(2):
+            lanes = slice(256 * m, 256 * (m + 1))
+            projected = half_ref[:, lanes].astype(f32)
+            own_ref[:, lanes] = adam(projected, one_ref[at, m, :], two_ref[at, m, :])[2]
+
+    return call(body, [((128, 512), bf16)], half, one, two, place=place, us=0.9)[0]
+
+
 def moments(place, gathered, one, two):
-    def body(place_ref, a_ref, b_ref, c_ref, d_ref, one_ref, two_ref, new_one_ref, new_two_ref, own_ref, all_ref):
-        for a, ref in enumerate((a_ref, b_ref, c_ref, d_ref)):
+    def body(place_ref, *refs):
+        halves, (one_ref, two_ref, new_one_ref, new_two_ref, all_ref) = refs[:4], refs[4:]
+        for a in range(4):
             at = pl.ds(pl.multiple_of(xor(place_ref[0], a) * 128, 128), 128)
             for m in range(2):
                 lanes = slice(256 * m, 256 * (m + 1))
-                projected = ref[:, lanes].astype(f32)
+                projected = halves[a][:, lanes].astype(f32)
                 new_one, new_two, direction = adam(projected, one_ref[at, m, :], two_ref[at, m, :])
                 new_one_ref[at, m, :] = new_one
                 new_two_ref[at, m, :] = new_two
                 all_ref[a, :, lanes] = direction
-                if a == 0:
-                    own_ref[:, lanes] = direction
 
     return pl.pallas_call(
         body,
         in_specs=[SMEM] + [VMEM] * 6,
-        out_specs=(VMEM,) * 4,
+        out_specs=(VMEM,) * 3,
         out_shape=(
             jax.ShapeDtypeStruct(one.shape, f32),
             jax.ShapeDtypeStruct(one.shape, f32),
-            pltpu.VMEM((128, 512), bf16),
             pltpu.VMEM((4, 128, 512), bf16),
         ),
         compiler_params=PARAMS,
+        cost_estimate=cost(3.5),
     )(place, *[pin(x) for x in gathered], one, two)
 
 
@@ -208,7 +223,7 @@
         odd = lax.broadcasted_iota(jnp.int32, (rows, 256), 0) % 2 == 1
         out_ref[...] = jnp.where(odd, total[:, 256:], total[:, :256]).astype(bf16)
 
-    return call(body, [((rows, 256), bf16)], high, low, *pieces)[0]
+    return call(body, [((rows, 256), bf16)], high, low, *pieces, us=1.0)[0]
 
 
 def grams(place, parts):
@@ -223,34 +238,27 @@
         mine = jnp.where(parity == place_ref[2], spanned, 0.0)
         theirs = jnp.where(parity == place_ref[2], 0.0, spanned)
         for part, out_ref in ((theirs, other_ref), (mine, own_ref)):
-            out_ref[...] = lax.dot_general(
-                part,
-                part,
-                (((0,), (0,)), ((), ())),
-                preferred_element_type=f32,
-                precision=lax.Precision.HIGHEST,
-            )
-
-    square = ((256, 256), f32)
-    return call(body, [((rows, 256), f32), square, square], *parts, place=place)
-
-
-def gram_core(own, came):
+            left, right = part[:, :128], part[:, 128:]
+            for i, (x, y) in enumerate(((left, left), (left, right), (right, right))):
+                out_ref[128 * i : 128 * (i + 1)] = lax.dot_general(
+                    x,
+                    y,
+                    (((0,), (0,)), ((), ())),
+                    preferred_element_type=f32,
+                    precision=lax.Precision.HIGHEST,
+                )
+
+    blocks = ((384, 128), f32)
+    return call(body, [((rows, 256), f32), blocks, blocks], *parts, place=place, us=1.8)
+
+
+def gram_add(own, came):
     def body(own_ref, came_ref, sum_ref, ship_ref):
-        total = own_ref[...] + came_ref[...]
+        total = own_ref[...] + came_ref[...].astype(f32)
         sum_ref[...] = total
         ship_ref[...] = total.astype(bf16)
 
-    return call(body, [((256, 256), f32), ((256, 256), bf16)], own, came)
-
-
-def gram_chips(parts):
-    def body(a_ref, b_ref, c_ref, d_ref, out_ref):
-        out_ref[...] = (a_ref[...] + b_ref[...].astype(f32)) + (
-            c_ref[...].astype(f32) + d_ref[...].astype(f32)
-        )
-
-    return call(body, [((256, 256), f32)], *parts)[0]
+    return call(body, [((384, 128), f32), ((384, 128), bf16)], own, came)
 
 
 def polish(place, spanned, own, other):
@@ -262,57 +270,72 @@
         mine = parity == place_ref[2]
         total = jnp.zeros_like(spanned)
         for chosen, gram_ref in ((mine, own_ref), (jnp.logical_not(mine), other_ref)):
-            gram = gram_ref[...]
-            normalizer = norm_of(gram, (0, 1))
+            a, b, d = gram_ref[:128], gram_ref[128:256], gram_ref[256:]
+            squares = jnp.sum(a * a) + 2.0 * jnp.sum(b * b) + jnp.sum(d * d)
+            normalizer = 1.7 / jnp.sqrt(jnp.sqrt(squares) + 1e-06)
             oriented = jnp.where(chosen, spanned, 0.0) * normalizer
-            ortho = gram * (normalizer * normalizer)
+            gram = jnp.concatenate(
+                [jnp.concatenate([a, b], axis=1), jnp.concatenate([b.T, d], axis=1)], axis=0
+            )
             total += 1.5 * oriented - 0.5 * jnp.dot(
-                oriented, ortho, preferred_element_type=f32, precision=lax.Precision.HIGHEST
+                oriented,
+                gram * (normalizer * normalizer),
+                preferred_element_type=f32,
+                precision=lax.Precision.HIGHEST,
             )
-        out_ref[...] = (math.sqrt(D) * total).astype(bf16)
-
-    return call(body, [((rows, 256), bf16)], spanned, own, other, place=place)[0]
-
-
-def update(place, weights, masked, held):
+        out_ref[...] = (math.sqrt(D) * total).astype(bf16).reshape(rows // 2, 2, 256)
+
+    return pl.pallas_call(
+        body,
+        in_specs=[SMEM] + [VMEM] * 3,
+        out_specs=VMEM,
+        out_shape=jax.ShapeDtypeStruct((rows // 2, 2, 256), bf16),
+        compiler_params=PARAMS,
+        cost_estimate=cost(1.8),
+    )(place, pin(spanned), pin(own), pin(other))
+
+
+def update(place, weights, masked, l0, ks, arrays, pieces, earlier):
     rows = weights.shape[0]
+    steps = [(l, n) for l in range(len(pieces)) for n in range(len(ks))]
+
+    def where(i, place_ref):
+        k = ks[0] + i % len(ks)
+        return 0, 0, xor(place_ref[1], k) * 2 + xor(place_ref[2], l0 + i // len(ks))
 
     def body(place_ref, w_ref, s_ref, *refs):
-        sides, out_ref = (refs[:7], refs[7:14]), refs[14]
-        for i in range(8):
-            l, k = i // 4, i % 4
+        held, out_ref, all_ref = refs[: len(arrays)], refs[-2], refs[-1]
+        for i, (l, n) in enumerate(steps):
 
             @pl.when(pl.program_id(0) == i)
             def _():
-                side = sides[l]
                 for a in range(4):
-                    if k == 0:
-                        piece = side[0][a]
-                    elif a == 0:
-                        piece = side[k][...]
-                    else:
-                        piece = side[3 + a][k - 1]
-                    at = pl.ds(pl.multiple_of(xor(place_ref[0], a) * 128, 128), 128)
-                    change = lax.dot_general(
-                        s_ref[...], piece, (((1,), (1,)), ((), ())), preferred_element_type=f32
-                    )
-                    out_ref[:, :, at] = w_ref[:, :, at] - (change * inv_root).reshape(rows, 2, 128)
-
-    def where(i, place_ref):
-        return 0, 0, xor(place_ref[1], i % 4) * 2 + xor(place_ref[2], i // 4)
-
-    block = pl.BlockSpec((rows, 2, 512), where)
+                    which, at, relative = pieces[l][n][a]
+                    group = xor(place_ref[0], a) if relative else a
+                    to = pl.ds(pl.multiple_of(group * 128, 128), 128)
+                    all_ref[to] = held[which][at]
+
+        change = lax.dot_general(
+            s_ref[...], all_ref[...], (((1,), (1,)), ((), ())), preferred_element_type=f32
+        )
+        at = pl.ds(pl.multiple_of(where(pl.program_id(0), place_ref)[2] * 512, 512), 512)
+        out_ref[...] = w_ref[:, :, at] - (change * inv_root).reshape(rows, 2, 512)
+
+    before = [] if earlier is None else [earlier]
     return pl.pallas_call(
         body,
         grid_spec=pltpu.PrefetchScalarGridSpec(
             num_scalar_prefetch=1,
-            grid=(8,),
-            in_specs=[block] + [VMEM] * 15,
-            out_specs=block,
+            grid=(len(steps),),
+            in_specs=[VMEM] * (2 + len(arrays)) + [pl.BlockSpec(memory_space=pl.ANY)] * len(before),
+            out_specs=pl.BlockSpec((rows, 2, 512), where),
+            scratch_shapes=[pltpu.VMEM((512, 512), bf16)],
         ),
         out_shape=jax.ShapeDtypeStruct(weights.shape, f32),
+        input_output_aliases={3 + len(arrays): 0} if before else {},
         compiler_params=PARAMS,
-    )(place, weights, pin(masked), *[pin(x) for x in held[0] + held[1]])
+        cost_estimate=cost(0.5 + len(steps)),
+    )(place, weights, pin(masked), *[pin(x) for x in arrays], *before)
 
 
 def per_device(partials, weights, subspace, moment_one, moment_two):
@@ -335,33 +358,65 @@
     zero = jnp.zeros_like(flat)
     masked = jnp.concatenate([jnp.where(odd, zero, flat), jnp.where(odd, flat, zero)], axis=1)
 
-    packed = [pack(place, partials[0], a) for a in range(4)]
-    high = [packed[0][0]] + [group(packed[a][0], a) for a in (1, 2, 3)]
-    low = [packed[0][1]] + [group(packed[a][1], a) for a in (1, 2, 3)]
-
-    gradient_high, keep, send = project(high, masked)
+    high = pack(place, partials[0], 1)
+    low = pack(after(place, high), partials[0], 0)
+    high = [high[0]] + [group(high[a], a) for a in (1, 2, 3)]
+    low = [low[0]] + [group(after(low[a], high[1]), a) for a in (1, 2, 3)]
+
+    gradient_high, keep, send = project(high, masked, 1.0)
     q2, q3 = add_core(keep, core(send), bf16)
     r2, r3 = chip(q2, 2), chip(q3, 3)
-    gradient_low, keep, send = project(low, masked)
+    low[3] = after(low[3], r2, r3)
+    gradient_low, keep, send = project(low, masked, 1.0)
     q0, q1 = add_core(keep, core(send), f32)
     half = finish([q0, chip(q1, 1), r2, r3])
 
-    halves = [half] + [chip(half, k) for k in (1, 2, 3)]
     gathered = [half] + [group(half, a) for a in (1, 2, 3)]
-    far_halves = [core(h) for h in halves]
-
-    part = span(gradient_high, gradient_low, halves + far_halves)
-    spanned, own, other = grams(place, [part] + [group(part, a) for a in (1, 2, 3)])
-    own, ship = gram_core(own, core(other))
-    own = gram_chips([own] + [chip(ship, k) for k in (1, 2, 3)])
-    new_subspace = polish(place, spanned, own, core(own)).reshape(rows, 2, 256)
-
-    new_one, new_two, mine, local = moments(place, gathered, moment_one, moment_two)
+    late = after(half, gathered[1], gathered[2])
+    halves = [half] + [chip(late if k == 1 else half, k) for k in (1, 2, 3)]
+    far_half = core(late)
+    mine = own_direction(place, half, moment_one, moment_two)
+
+    new_one, new_two, local = moments(place, gathered, moment_one, moment_two)
+
+    halves += [far_half] + [core(h) for h in halves[1:]]
+    halves[0] = after(halves[0], gathered[3])
+    part = span(gradient_high, gradient_low, halves)
+    parts = [part] + [group(part, a) for a in (1, 2, 3)]
+    mine = after(mine, part)
     along = [chip(mine, k) for k in (1, 2, 3)]
-    stack = jnp.stack(along)
-    near = [local] + along + [group(stack, a) for a in (1, 2, 3)]
-    far = [core(x) for x in near]
-    new_weights = update(place, weights, masked, (near, far))
+    spanned, own, other = grams(place, parts)
+    own, ship = gram_add(own, core(other))
+    own, ship = gram_add(own, chip(ship, 1))
+    own, _ = gram_add(own, chip(ship, 2))
+    new_subspace = polish(place, spanned, own, core(own))
+
+    along = jnp.stack(along)
+    held = [along] + [group(along, a) for a in (1, 2, 3)]
+    weights = pin(weights)
+    new_weights = update(
+        place,
+        weights,
+        masked,
+        0,
+        (0,),
+        [local, core(local)],
+        [[[(l, a, True) for a in range(4)]] for l in range(2)],
+        None,
+    )
+    held = after(held, new_weights, own)
+    far = [core(x) for x in held]
+    for l, side in ((0, held), (1, far)):
+        new_weights = update(
+            place,
+            weights,
+            masked,
+            l,
+            (1, 2, 3),
+            side,
+            [[[(a, n, True) for a in range(4)] for n in range(3)]],
+            new_weights,
+        )
     return new_weights, new_one, new_two, new_subspace
 
 

time: 150 us -> 122 us (0.81)
  local copies, waits for them, and re-layouts: 9.32 us -> 1.02 us
  waiting for transfers between devices: 63.5 us -> 56 us
  starting transfers between devices: 42.6 us -> 35.9 us
  Pallas kernels: 32.8 us -> 27.3 us
    unnamed x22 -> x8, local copies, waits for them, and re-layouts: 7.55 us -> 0.02 us
    ppermute x42 -> x39, waiting for transfers between devices: 63.5 us -> 56 us  [swap(): return lax.ppermute(x, axis, [(i, i ^ bit) for i in range(size)])]
    ppermute x42 -> x39, starting transfers between devices: 42.6 us -> 35.9 us  [swap(): return lax.ppermute(x, axis, [(i, i ^ bit) for i in range(size)])]
    pallas_call x4 -> x2, Pallas kernels: 12.7 us -> 6.6 us  [pack(): pl.pallas_call(body, grid_spec=pltpu.PrefetchScalarGridSpec(num_scalar_pr...]
    pallas_call x1 -> x2, Pallas kernels: 3.65 us -> 6.05 us  [the longest x1 3.54 us: moments(): pl.pallas_call(body, in_specs=[SMEM] + [VMEM] * 6, out_specs=(VMEM,) * 3,...]
    pallas_call x10 -> x11, Pallas kernels: 6.98 us -> 5.58 us  [call(): pl.pallas_call(body, in_specs=[SMEM] * len(scalars) + [VMEM] * len(args),...]
    pallas_call x1 -> x3, Pallas kernels: 9.48 us -> 9.09 us  [update(): pl.pallas_call(body, grid_spec=pltpu.PrefetchScalarGridSpec(num_scalar_pr...]
  transfers between devices with their start and end apart: 42 -> 39, of which waited for: 11 -> 17; matrix products, arithmetic and copies ran while one was open for 1% -> 1% of each run, Pallas kernels for 18% -> 15%
where the time goes in v3:
time: 122 us; the launch traced here: 121 us
  waiting for transfers between devices  56 us (46%)
  starting transfers between devices  35.9 us (29%)
  Pallas kernels  27.3 us (22%)
    ppermute x39, waiting for transfers between devices, swap(): return lax.ppermute(x, axis, [(i, i ^ bit) for i in range(size)])  56 us
    ppermute x39, starting transfers between devices, swap(): return lax.ppermute(x, axis, [(i, i ^ bit) for i in range(size)])  35.9 us
    pallas_call x3, Pallas kernels, update(): pl.pallas_call(body, grid_spec=pltpu.PrefetchScalarGridSpec(num_scalar_pr...  9.09 us
    pallas_call x2, Pallas kernels, pack(): pl.pallas_call(body, grid_spec=pltpu.PrefetchScalarGridSpec(num_scalar_pr...  6.6 us
    pallas_call x11, Pallas kernels, call(): pl.pallas_call(body, in_specs=[SMEM] * len(scalars) + [VMEM] * len(args),...  5.58 us
    pallas_call x1, Pallas kernels, moments(): pl.pallas_call(body, in_specs=[SMEM] + [VMEM] * 6, out_specs=(VMEM,) * 3,...  3.54 us
    pallas_call x1, Pallas kernels, polish(): pl.pallas_call(body, in_specs=[SMEM] + [VMEM] * 3, out_specs=VMEM, out_sh...  2.5 us
  transfers between devices with their start and end apart: 39, of which 17 were waited for; matrix products, arithmetic and copies ran while one was open for 1% of the time, Pallas kernels for 15%

profile of v3, /device:TPU:1, one launch (start us, length us, event | category | flops | bytes accessed | tf_op | source)
XLA Modules:
  0.0 121.4 jit_solution(4722369031524989996)
XLA Ops:
  0.7 3.3 %shard_map.84 = (bf16[4,384,128]{2,1,0:T(8,128)(2,1)S(1)}, bf16[4,384,128]{2,1,0:T(8,128)(2,1)S(1)}, bf16[4,384,128]{2,1,0:T(8,128)(2,1)S(1)}, bf16[4,384,128]{2,1,0:T(8,128)(2,1)S(1)}) custom-call(s32[3]{0:T(128)S(1)} %pad_add_fusion.place_ref, bf16[192,2,4096]{2,1,0:T(2,128)(2,1)} %bitcast.9), custom_call_target="tpu_custom_call" | custom-call | bytes 11550000 | tf_op jit(solution)/shard_map/pallas_call | solution.py:113
  4.0 2.1 %collective-permute-start = (bf16[4,384,128]{2,1,0:T(8,128)(2,1)S(1)}, bf16[4,384,128]{2,1,0:T(8,128)(2,1)S(1)}, u32[]{:S(2)}, u32[]{:S(2)}) collective-permute-start(bf16[4,384,128]{2,1,0:T(8,128)(2,1)S(1)} %get-tuple-element.46), channel_id=1, source_target_pairs={{0,8},{8,0},{16,24},{24,16},{1,9},{9,1},{17,25},{25,17},{2,10},{10... | collective-permute-start | bytes 1179656 | tf_op jit(solution)/shard_map/ppermute | solution.py:64
  6.1 1.2 %collective-permute-start.4 = (bf16[4,384,128]{2,1,0:T(8,128)(2,1)S(1)}, bf16[4,384,128]{2,1,0:T(8,128)(2,1)S(1)}, u32[]{:S(2)}, u32[]{:S(2)}) collective-permute-start(bf16[4,384,128]{2,1,0:T(8,128)(2,1)S(1)} %get-tuple-element.47), channel_id=1, source_target_pairs={{0,16},{8,24},{16,0},{24,8},{1,17},{9,25},{17,1},{25,9},{2,18},{10... | collective-permute-start | bytes 1179656 | tf_op jit(solution)/shard_map/ppermute | solution.py:64
  7.4 1.0 reshape.11
  8.4 3.3 %shard_map.85 = (bf16[4,384,128]{2,1,0:T(8,128)(2,1)S(1)}, bf16[4,384,128]{2,1,0:T(8,128)(2,1)S(1)}, bf16[4,384,128]{2,1,0:T(8,128)(2,1)S(1)}, bf16[4,384,128]{2,1,0:T(8,128)(2,1)S(1)}) custom-call(s32[3]{0:T(128)S(1)} %pad_add_fusion.place_ref, bf16[192,2,4096]{2,1,0:T(2,128)(2,1)} %bitcast.10), custom_call_target="tpu_custom_call" | custom-call | bytes 11550000 | tf_op jit(solution)/shard_map/pallas_call | solution.py:113
  12.0 2.9 %collective-permute-done.b_ref = bf16[4,384,128]{2,1,0:T(8,128)(2,1)S(1)} collective-permute-done((bf16[4,384,128]{2,1,0:T(8,128)(2,1)S(1)}, bf16[4,384,128]{2,1,0:T(8,128)(2,1)S(1)}, u32[]{:S(2)}, u32[]{:S(2)}) %collective-permute-start) | collective-permute-done | bytes 393248 | tf_op jit(solution)/shard_map/ppermute | solution.py:64
  14.9 0.8 collective-permute-done.4.c_ref
  15.8 8.5 %collective-permute-done.5.d_ref = bf16[4,384,128]{2,1,0:T(8,128)(2,1)S(1)} collective-permute-done((bf16[4,384,128]{2,1,0:T(8,128)(2,1)S(1)}, bf16[4,384,128]{2,1,0:T(8,128)(2,1)S(1)}, u32[]{:S(2)}, u32[]{:S(2)}) %collective-permute-start.5) | collective-permute-done | bytes 393248 | tf_op jit(solution)/shard_map/ppermute | solution.py:64
  24.8 1.8 %collective-permute-start.6 = (bf16[2,128,512]{2,1,0:T(8,128)(2,1)S(1)}, bf16[2,128,512]{2,1,0:T(8,128)(2,1)S(1)}, u32[]{:S(2)}, u32[]{:S(2)}) collective-permute-start(bf16[2,128,512]{2,1,0:T(8,128)(2,1)S(1)} %get-tuple-element.58), channel_id=1, source_target_pairs={{0,1},{1,0},{2,3},{3,2},{4,5},{5,4},{6,7},{7,6},{8,9},{9,8},{10,11... | collective-permute-start | bytes 786440 | tf_op jit(solution)/shard_map/ppermute | solution.py:64
  26.7 1.2 %collective-permute-start.3 = (bf16[4,384,128]{2,1,0:T(8,128)(2,1)S(1)}, bf16[4,384,128]{2,1,0:T(8,128)(2,1)S(1)}, u32[]{:S(2)}, u32[]{:S(2)}) collective-permute-start(bf16[4,384,128]{2,1,0:T(8,128)(2,1)S(1)} %get-tuple-element.56), channel_id=1, source_target_pairs={{0,24},{8,16},{16,8},{24,0},{1,25},{9,17},{17,9},{25,1},{2,26},{10... | collective-permute-start | bytes 1179656 | tf_op jit(solution)/shard_map/ppermute | solution.py:64
  27.9 0.9 collective-permute-start.2
  29.4 2.4 %collective-permute-start.7 = (bf16[128,512]{1,0:T(8,128)(2,1)S(1)}, bf16[128,512]{1,0:T(8,128)(2,1)S(1)}, u32[]{:S(2)}, u32[]{:S(2)}) collective-permute-start(bf16[128,512]{1,0:T(8,128)(2,1)S(1)} %get-tuple-element.59), channel_id=1, source_target_pairs={{0,4},{1,5},{2,6},{3,7},{4,0},{5,1},{6,2},{7,3},{8,12},{9,13},{10,... | collective-permute-start | bytes 393224 | tf_op jit(solution)/shard_map/ppermute | solution.py:64
  31.8 1.1 collective-permute-start.8
  32.8 7.5 %collective-permute-done.7.c_ref = bf16[128,512]{1,0:T(8,128)(2,1)S(1)} collective-permute-done((bf16[128,512]{1,0:T(8,128)(2,1)S(1)}, bf16[128,512]{1,0:T(8,128)(2,1)S(1)}, u32[]{:S(2)}, u32[]{:S(2)}) %collective-permute-start.7) | collective-permute-done | bytes 131104 | tf_op jit(solution)/shard_map/ppermute | solution.py:64
  40.3 6.7 %collective-permute-done.2.c_ref = bf16[4,384,128]{2,1,0:T(8,128)(2,1)S(1)} collective-permute-done((bf16[4,384,128]{2,1,0:T(8,128)(2,1)S(1)}, bf16[4,384,128]{2,1,0:T(8,128)(2,1)S(1)}, u32[]{:S(2)}, u32[]{:S(2)}) %collective-permute-start.2) | collective-permute-done | bytes 393248 | tf_op jit(solution)/shard_map/ppermute | solution.py:64
  48.2 1.2 collective-permute-done.9.came_ref
  49.4 1.4 %collective-permute-start.10 = (bf16[128,512]{1,0:T(8,128)(2,1)S(1)}, bf16[128,512]{1,0:T(8,128)(2,1)S(1)}, u32[]{:S(2)}, u32[]{:S(2)}) collective-permute-start(bf16[128,512]{1,0:T(8,128)(2,1)S(1)} %get-tuple-element.65), channel_id=1, source_target_pairs={{0,2},{1,3},{2,0},{3,1},{4,6},{5,7},{6,4},{7,5},{8,10},{9,11},{10,... | collective-permute-start | bytes 393224 | tf_op jit(solution)/shard_map/ppermute | solution.py:64
  50.8 3.4 %collective-permute-done.10.b_ref = bf16[128,512]{1,0:T(8,128)(2,1)S(1)} collective-permute-done((bf16[128,512]{1,0:T(8,128)(2,1)S(1)}, bf16[128,512]{1,0:T(8,128)(2,1)S(1)}, u32[]{:S(2)}, u32[]{:S(2)}) %collective-permute-start.10) | collective-permute-done | bytes 131104 | tf_op jit(solution)/shard_map/ppermute | solution.py:64
  54.3 1.2 collective-permute-start.13
  55.8 3.3 %collective-permute-start.16 = (bf16[128,512]{1,0:T(8,128)(2,1)S(1)}, bf16[128,512]{1,0:T(8,128)(2,1)S(1)}, u32[]{:S(2)}, u32[]{:S(2)}) collective-permute-start(bf16[128,512]{1,0:T(8,128)(2,1)S(1)} %shard_map.90.half_ref.refs_0_), channel_id=1, source_target_pairs={{0,6},{1,7},{2,4},{3,5},{4,2},{5,3},{6,0},{7,1},{8,14},{9,15},{10,... | collective-permute-start | bytes 393224 | tf_op jit(solution)/shard_map/ppermute | solution.py:64
  59.6 1.3 %collective-permute-start.14 = (bf16[128,512]{1,0:T(8,128)(2,1)S(1)}, bf16[128,512]{1,0:T(8,128)(2,1)S(1)}, u32[]{:S(2)}, u32[]{:S(2)}) collective-permute-start(bf16[128,512]{1,0:T(8,128)(2,1)S(1)} %shard_map.90.half_ref.refs_0_), channel_id=1, source_target_pairs={{0,2},{1,3},{2,0},{3,1},{4,6},{5,7},{6,4},{7,5},{8,10},{9,11},{10,... | collective-permute-start | bytes 393224 | tf_op jit(solution)/shard_map/ppermute | solution.py:64
  60.9 0.9 collective-permute-start.11
  61.8 2.9 %collective-permute-start.17 = (bf16[128,512]{1,0:T(8,128)(2,1)S(1)}, bf16[128,512]{1,0:T(8,128)(2,1)S(1)}, u32[]{:S(2)}, u32[]{:S(2)}) collective-permute-start(bf16[128,512]{1,0:T(8,128)(2,1)S(1)} %shard_map.90.half_ref.refs_0_), channel_id=1, source_target_pairs={{0,1},{1,0},{2,3},{3,2},{4,5},{5,4},{6,7},{7,6},{8,9},{9,8},{10,11... | collective-permute-start | bytes 393224 | tf_op jit(solution)/shard_map/ppermute | solution.py:64
  65.2 4.6 %collective-permute-done.15.refs_2_ = bf16[128,512]{1,0:T(8,128)(2,1)S(1)} collective-permute-done((bf16[128,512]{1,0:T(8,128)(2,1)S(1)}, bf16[128,512]{1,0:T(8,128)(2,1)S(1)}, u32[]{:S(2)}, u32[]{:S(2)}) %collective-permute-start.15) | collective-permute-done | bytes 131104 | tf_op jit(solution)/shard_map/ppermute | solution.py:64
  69.7 1.4 %collective-permute-start.19 = (bf16[128,512]{1,0:T(8,128)(2,1)S(1)}, bf16[128,512]{1,0:T(8,128)(2,1)S(1)}, u32[]{:S(2)}, u32[]{:S(2)}) collective-permute-start(bf16[128,512]{1,0:T(8,128)(2,1)S(1)} %collective-permute-done.15.refs_2_), channel_id=1, source_target_pairs={{0,1},{1,0},{2,3},{3,2},{4,5},{5,4},{6,7},{7,6},{8,9},{9,8},{10,11... | collective-permute-start | bytes 393224 | tf_op jit(solution)/shard_map/ppermute | solution.py:64
  71.1 1.0 collective-permute-done.19.refs_6_
  72.5 1.0 shard_map.92.a_ref
  73.4 1.3 %collective-permute-start.30 = (bf16[384,256]{1,0:T(8,128)(2,1)S(1)}, bf16[384,256]{1,0:T(8,128)(2,1)S(1)}, u32[]{:S(2)}, u32[]{:S(2)}) collective-permute-start(bf16[384,256]{1,0:T(8,128)(2,1)S(1)} %shard_map.92.a_ref), channel_id=1, source_target_pairs={{0,24},{8,16},{16,8},{24,0},{1,25},{9,17},{17,9},{25,1},{2,26},{10... | collective-permute-start | bytes 589832 | tf_op jit(solution)/shard_map/ppermute | solution.py:64
  74.7 1.1 collective-permute-start.29
  76.1 0.9 shard_map.91
  77.1 2.3 %collective-permute-start.23 = (bf16[128,512]{1,0:T(8,128)(2,1)S(1)}, bf16[128,512]{1,0:T(8,128)(2,1)S(1)}, u32[]{:S(2)}, u32[]{:S(2)}) collective-permute-start(bf16[128,512]{1,0:T(8,128)(2,1)S(1)} %shard_map.91), channel_id=1, source_target_pairs={{0,6},{1,7},{2,4},{3,5},{4,2},{5,3},{6,0},{7,1},{8,14},{9,15},{10,... | collective-permute-start | bytes 393224 | tf_op jit(solution)/shard_map/ppermute | solution.py:64
  79.4 1.4 %collective-permute-done.30.d_ref = bf16[384,256]{1,0:T(8,128)(2,1)S(1)} collective-permute-done((bf16[384,256]{1,0:T(8,128)(2,1)S(1)}, bf16[384,256]{1,0:T(8,128)(2,1)S(1)}, u32[]{:S(2)}, u32[]{:S(2)}) %collective-permute-start.30) | collective-permute-done | bytes 196640 | tf_op jit(solution)/shard_map/ppermute | solution.py:64
  80.8 3.5 %shard_map.93 = (f32[512,2,256]{2,1,0:T(2,128)}, f32[512,2,256]{2,1,0:T(2,128)}, bf16[4,128,512]{2,1,0:T(8,128)(2,1)S(1)}) custom-call(s32[3]{0:T(128)S(1)} %pad_add_fusion.place_ref, bf16[128,512]{1,0:T(8,128)(2,1)S(1)} %shard_map.90.half_ref.refs_0_, bf16[128,512]{1,0:T(8,128)(2,1)S(1)} %collective-permute-done.12.refs_1_, ...), custom_call_target="tpu_custom_call" | custom-call | bytes 12250000 | tf_op jit(solution)/shard_map/pallas_call | solution.py:196
  84.3 1.1 collective-permute-done.29.c_ref
  85.4 0.7 collective-permute-start.27
  86.1 1.8 %shard_map.95 = (f32[384,256]{1,0:T(8,128)S(1)}, f32[384,128]{1,0:T(8,128)S(1)}, f32[384,128]{1,0:T(8,128)S(1)}) custom-call(s32[3]{0:T(128)S(1)} %pad_add_fusion.place_ref, bf16[384,256]{1,0:T(8,128)(2,1)S(1)} %shard_map.92.a_ref, bf16[384,256]{1,0:T(8,128)(2,1)S(1)} %collective-permute-done.28.b_ref, bf16[384,256]{1,0:T(8,128)(2,1)S(1)} %collective-permute-done.29.c_ref, ...), custom_call_target="tpu_custom_call" | custom-call | bytes 6300000 | tf_op jit(solution)/shard_map/pallas_call | solution.py:83
  88.0 2.3 %collective-permute-done.22 = bf16[128,512]{1,0:T(8,128)(2,1)S(1)} collective-permute-done((bf16[128,512]{1,0:T(8,128)(2,1)S(1)}, bf16[128,512]{1,0:T(8,128)(2,1)S(1)}, u32[]{:S(2)}, u32[]{:S(2)}) %collective-permute-start.22) | collective-permute-done | bytes 131104 | tf_op jit(solution)/shard_map/ppermute | solution.py:64
  90.3 1.3 %collective-permute-start.26 = (bf16[3,128,512]{2,1,0:T(8,128)(2,1)S(1)}, bf16[3,128,512]{2,1,0:T(8,128)(2,1)S(1)}, u32[]{:S(2)}, u32[]{:S(2)}) collective-permute-start(bf16[3,128,512]{2,1,0:T(8,128)(2,1)S(1)} %pad_maximum_fusion.1.refs_0_), channel_id=1, source_target_pairs={{0,24},{8,16},{16,8},{24,0},{1,25},{9,17},{17,9},{25,1},{2,26},{10... | collective-permute-start | bytes 1179656 | tf_op jit(solution)/shard_map/ppermute | solution.py:64
  91.6 1.1 collective-permute-start.25
  93.1 3.7 %collective-permute-done.32.came_ref = bf16[384,128]{1,0:T(8,128)(2,1)S(1)} collective-permute-done((bf16[384,128]{1,0:T(8,128)(2,1)S(1)}, bf16[384,128]{1,0:T(8,128)(2,1)S(1)}, u32[]{:S(2)}, u32[]{:S(2)}) %collective-permute-start.32) | collective-permute-done | bytes 98336 | tf_op jit(solution)/shard_map/ppermute | solution.py:64
  96.9 0.8 collective-permute-start.33
  97.8 2.4 %shard_map.94.refs_4_ = f32[192,2,4096]{2,1,0:T(2,128)} custom-call(s32[3]{0:T(128)S(1)} %pad_add_fusion.place_ref, f32[192,2,4096]{2,1,0:T(2,128)S(1)} %bitcast.8, bf16[384,512]{1,0:T(8,128)(2,1)S(1)} %pad_maximum_fusion.s_ref, bf16[4,128,512]{2,1,0:T(8,128)(2,1)S(1)} %get-tuple-element.71.refs_0_, bf16[4,128,512]{2,1,0:T(8,128)(2,1)S(1)} %collective-permute-done.27.refs_1_), custom_call_target="tpu_custom_call" | custom-call | bytes 8750000 | tf_op jit(solution)/shard_map/pallas_call | solution.py:325
  100.2 2.2 %collective-permute-done.33.came_ref = bf16[384,128]{1,0:T(8,128)(2,1)S(1)} collective-permute-done((bf16[384,128]{1,0:T(8,128)(2,1)S(1)}, bf16[384,128]{1,0:T(8,128)(2,1)S(1)}, u32[]{:S(2)}, u32[]{:S(2)}) %collective-permute-start.33) | collective-permute-done | bytes 98336 | tf_op jit(solution)/shard_map/ppermute | solution.py:64
  102.4 0.7 shard_map.98
  103.1 7.7 %collective-permute-done.25.refs_2_ = bf16[3,128,512]{2,1,0:T(8,128)(2,1)S(1)} collective-permute-done((bf16[3,128,512]{2,1,0:T(8,128)(2,1)S(1)}, bf16[3,128,512]{2,1,0:T(8,128)(2,1)S(1)}, u32[]{:S(2)}, u32[]{:S(2)}) %collective-permute-start.25) | collective-permute-done | bytes 393248 | tf_op jit(solution)/shard_map/ppermute | solution.py:64
  112.2 3.3 %shard_map.99.refs_4_ = f32[192,2,4096]{2,1,0:T(2,128)} custom-call(s32[3]{0:T(128)S(1)} %pad_add_fusion.place_ref, f32[192,2,4096]{2,1,0:T(2,128)S(1)} %bitcast.8, bf16[384,512]{1,0:T(8,128)(2,1)S(1)} %pad_maximum_fusion.s_ref, bf16[3,128,512]{2,1,0:T(8,128)(2,1)S(1)} %pad_maximum_fusion.1.refs_0_, ...), custom_call_target="tpu_custom_call", output_to_operand_aliasing={{}: (7, {})} | custom-call | bytes 12250000 | tf_op jit(solution)/shard_map/pallas_call | solution.py:325
  115.6 2.5 %shard_map.101 = bf16[192,2,256]{2,1,0:T(2,128)(2,1)} custom-call(s32[3]{0:T(128)S(1)} %pad_add_fusion.place_ref, f32[384,256]{1,0:T(8,128)S(1)} %get-tuple-element.85.spanned_ref, f32[384,128]{1,0:T(8,128)S(1)} %get-tuple-element.78.own_ref, f32[384,128]{1,0:T(8,128)S(1)} %collective-permute-done.38.other_ref), custom_call_target="tpu_custom_call" | custom-call | bytes 6300000 | tf_op jit(solution)/shard_map/pallas_call | solution.py:288
  118.1 3.3 %shard_map.100 = f32[192,2,4096]{2,1,0:T(2,128)} custom-call(s32[3]{0:T(128)S(1)} %pad_add_fusion.place_ref, f32[192,2,4096]{2,1,0:T(2,128)S(1)} %bitcast.8, bf16[384,512]{1,0:T(8,128)(2,1)S(1)} %pad_maximum_fusion.s_ref, bf16[3,128,512]{2,1,0:T(8,128)(2,1)S(1)} %collective-permute-done.34.refs_0_, ...), custom_call_target="tpu_custom_call", output_to_operand_aliasing={{}: (7, {})} | custom-call | bytes 12250000 | tf_op jit(solution)/shard_map/pallas_call | solution.py:325
  (64 shorter events, 6.7 us)
Async XLA Ops:
  4.0 10.9 %collective-permute-start = (bf16[4,384,128]{2,1,0:T(8,128)(2,1)S(1)}, bf16[4,384,128]{2,1,0:T(8,128)(2,1)S(1)}, u32[]{:S(2)}, u32[]{:S(2)}) collective-permute-start(bf16[4,384,128]{2,1,0:T(8,128)(2,1)S(1)} %get-tuple-element.46), channel_id=1, source_target_pairs={{0,8},{8,0},{16,24},{24,16},{1,9},{9,1},{17,25},{25,17},{2,10},{10... | collective-permute-start | bytes 1179656 | tf_op jit(solution)/shard_map/ppermute | solution.py:64
  6.1 9.7 %collective-permute-start.4 = (bf16[4,384,128]{2,1,0:T(8,128)(2,1)S(1)}, bf16[4,384,128]{2,1,0:T(8,128)(2,1)S(1)}, u32[]{:S(2)}, u32[]{:S(2)}) collective-permute-start(bf16[4,384,128]{2,1,0:T(8,128)(2,1)S(1)} %get-tuple-element.47), channel_id=1, source_target_pairs={{0,16},{8,24},{16,0},{24,8},{1,17},{9,25},{17,1},{25,9},{2,18},{10... | collective-permute-start | bytes 1179656 | tf_op jit(solution)/shard_map/ppermute | solution.py:64
  7.3 17.0 %collective-permute-start.5 = (bf16[4,384,128]{2,1,0:T(8,128)(2,1)S(1)}, bf16[4,384,128]{2,1,0:T(8,128)(2,1)S(1)}, u32[]{:S(2)}, u32[]{:S(2)}) collective-permute-start(bf16[4,384,128]{2,1,0:T(8,128)(2,1)S(1)} %get-tuple-element.48), channel_id=1, source_target_pairs={{0,24},{8,16},{16,8},{24,0},{1,25},{9,17},{17,9},{25,1},{2,26},{10... | collective-permute-start | bytes 1179656 | tf_op jit(solution)/shard_map/ppermute | solution.py:64
  8.4 67.8 %copy-start = (f32[512,2,256]{2,1,0:T(2,128)S(1)}, f32[512,2,256]{2,1,0:T(2,128)}, u32[]{:S(2)}) copy-start(f32[512,2,256]{2,1,0:T(2,128)} %refs_4_.1) | copy-start | bytes 3145732
  8.4 67.8 %copy-start.1 = (f32[512,2,256]{2,1,0:T(2,128)S(1)}, f32[512,2,256]{2,1,0:T(2,128)}, u32[]{:S(2)}) copy-start(f32[512,2,256]{2,1,0:T(2,128)} %refs_5_.1) | copy-start | bytes 3145732
  24.3 73.4 %slice-start = ((s8[6291456]{0:T(1024)(128)(4,1)}), s8[4194304]{0:T(1024)(128)(4,1)S(1)}, s32[]{:S(2)}) async-start(s8[6291456]{0:T(1024)(128)(4,1)} %bitcast.7), calls=%async_computation | async-start | bytes 8388608
  24.8 4.5 %collective-permute-start.6 = (bf16[2,128,512]{2,1,0:T(8,128)(2,1)S(1)}, bf16[2,128,512]{2,1,0:T(8,128)(2,1)S(1)}, u32[]{:S(2)}, u32[]{:S(2)}) collective-permute-start(bf16[2,128,512]{2,1,0:T(8,128)(2,1)S(1)} %get-tuple-element.58), channel_id=1, source_target_pairs={{0,1},{1,0},{2,3},{3,2},{4,5},{5,4},{6,7},{7,6},{8,9},{9,8},{10,11... | collective-permute-start | bytes 786440 | tf_op jit(solution)/shard_map/ppermute | solution.py:64
  26.7 13.7 %collective-permute-start.3 = (bf16[4,384,128]{2,1,0:T(8,128)(2,1)S(1)}, bf16[4,384,128]{2,1,0:T(8,128)(2,1)S(1)}, u32[]{:S(2)}, u32[]{:S(2)}) collective-permute-start(bf16[4,384,128]{2,1,0:T(8,128)(2,1)S(1)} %get-tuple-element.56), channel_id=1, source_target_pairs={{0,24},{8,16},{16,8},{24,0},{1,25},{9,17},{17,9},{25,1},{2,26},{10... | collective-permute-start | bytes 1179656 | tf_op jit(solution)/shard_map/ppermute | solution.py:64
  27.9 19.2 %collective-permute-start.2 = (bf16[4,384,128]{2,1,0:T(8,128)(2,1)S(1)}, bf16[4,384,128]{2,1,0:T(8,128)(2,1)S(1)}, u32[]{:S(2)}, u32[]{:S(2)}) collective-permute-start(bf16[4,384,128]{2,1,0:T(8,128)(2,1)S(1)} %get-tuple-element.54), channel_id=1, source_target_pairs={{0,16},{8,24},{16,0},{24,8},{1,17},{9,25},{17,1},{25,9},{2,18},{10... | collective-permute-start | bytes 1179656 | tf_op jit(solution)/shard_map/ppermute | solution.py:64
  28.8 18.3 %collective-permute-start.1 = (bf16[4,384,128]{2,1,0:T(8,128)(2,1)S(1)}, bf16[4,384,128]{2,1,0:T(8,128)(2,1)S(1)}, u32[]{:S(2)}, u32[]{:S(2)}) collective-permute-start(bf16[4,384,128]{2,1,0:T(8,128)(2,1)S(1)} %get-tuple-element.52), channel_id=1, source_target_pairs={{0,8},{8,0},{16,24},{24,16},{1,9},{9,1},{17,25},{25,17},{2,10},{10... | collective-permute-start | bytes 1179656 | tf_op jit(solution)/shard_map/ppermute | solution.py:64
  29.4 10.9 %collective-permute-start.7 = (bf16[128,512]{1,0:T(8,128)(2,1)S(1)}, bf16[128,512]{1,0:T(8,128)(2,1)S(1)}, u32[]{:S(2)}, u32[]{:S(2)}) collective-permute-start(bf16[128,512]{1,0:T(8,128)(2,1)S(1)} %get-tuple-element.59), channel_id=1, source_target_pairs={{0,4},{1,5},{2,6},{3,7},{4,0},{5,1},{6,2},{7,3},{8,12},{9,13},{10,... | collective-permute-start | bytes 393224 | tf_op jit(solution)/shard_map/ppermute | solution.py:64
  31.8 8.6 %collective-permute-start.8 = (bf16[128,512]{1,0:T(8,128)(2,1)S(1)}, bf16[128,512]{1,0:T(8,128)(2,1)S(1)}, u32[]{:S(2)}, u32[]{:S(2)}) collective-permute-start(bf16[128,512]{1,0:T(8,128)(2,1)S(1)} %get-tuple-element.60), channel_id=1, source_target_pairs={{0,6},{1,7},{2,4},{3,5},{4,2},{5,3},{6,0},{7,1},{8,14},{9,15},{10,... | collective-permute-start | bytes 393224 | tf_op jit(solution)/shard_map/ppermute | solution.py:64
  47.6 1.8 %collective-permute-start.9 = (bf16[2,128,512]{2,1,0:T(8,128)(2,1)S(1)}, bf16[2,128,512]{2,1,0:T(8,128)(2,1)S(1)}, u32[]{:S(2)}, u32[]{:S(2)}) collective-permute-start(bf16[2,128,512]{2,1,0:T(8,128)(2,1)S(1)} %get-tuple-element.63), channel_id=1, source_target_pairs={{0,1},{1,0},{2,3},{3,2},{4,5},{5,4},{6,7},{7,6},{8,9},{9,8},{10,11... | collective-permute-start | bytes 786440 | tf_op jit(solution)/shard_map/ppermute | solution.py:64
  49.4 4.8 %collective-permute-start.10 = (bf16[128,512]{1,0:T(8,128)(2,1)S(1)}, bf16[128,512]{1,0:T(8,128)(2,1)S(1)}, u32[]{:S(2)}, u32[]{:S(2)}) collective-permute-start(bf16[128,512]{1,0:T(8,128)(2,1)S(1)} %get-tuple-element.65), channel_id=1, source_target_pairs={{0,2},{1,3},{2,0},{3,1},{4,6},{5,7},{6,4},{7,5},{8,10},{9,11},{10,... | collective-permute-start | bytes 393224 | tf_op jit(solution)/shard_map/ppermute | solution.py:64
  54.3 4.8 %collective-permute-start.13 = (bf16[128,512]{1,0:T(8,128)(2,1)S(1)}, bf16[128,512]{1,0:T(8,128)(2,1)S(1)}, u32[]{:S(2)}, u32[]{:S(2)}) collective-permute-start(bf16[128,512]{1,0:T(8,128)(2,1)S(1)} %shard_map.90.half_ref.refs_0_), channel_id=1, source_target_pairs={{0,16},{8,24},{16,0},{24,8},{1,17},{9,25},{17,1},{25,9},{2,18},{10... | collective-permute-start | bytes 393224 | tf_op jit(solution)/shard_map/ppermute | solution.py:64
  55.5 4.1 %collective-permute-start.12 = (bf16[128,512]{1,0:T(8,128)(2,1)S(1)}, bf16[128,512]{1,0:T(8,128)(2,1)S(1)}, u32[]{:S(2)}, u32[]{:S(2)}) collective-permute-start(bf16[128,512]{1,0:T(8,128)(2,1)S(1)} %shard_map.90.half_ref.refs_0_), channel_id=1, source_target_pairs={{0,8},{8,0},{16,24},{24,16},{1,9},{9,1},{17,25},{25,17},{2,10},{10... | collective-permute-start | bytes 393224 | tf_op jit(solution)/shard_map/ppermute | solution.py:64
  55.8 8.9 %collective-permute-start.16 = (bf16[128,512]{1,0:T(8,128)(2,1)S(1)}, bf16[128,512]{1,0:T(8,128)(2,1)S(1)}, u32[]{:S(2)}, u32[]{:S(2)}) collective-permute-start(bf16[128,512]{1,0:T(8,128)(2,1)S(1)} %shard_map.90.half_ref.refs_0_), channel_id=1, source_target_pairs={{0,6},{1,7},{2,4},{3,5},{4,2},{5,3},{6,0},{7,1},{8,14},{9,15},{10,... | collective-permute-start | bytes 393224 | tf_op jit(solution)/shard_map/ppermute | solution.py:64
  59.1 10.6 %collective-permute-start.15 = (bf16[128,512]{1,0:T(8,128)(2,1)S(1)}, bf16[128,512]{1,0:T(8,128)(2,1)S(1)}, u32[]{:S(2)}, u32[]{:S(2)}) collective-permute-start(bf16[128,512]{1,0:T(8,128)(2,1)S(1)} %shard_map.90.half_ref.refs_0_), channel_id=1, source_target_pairs={{0,4},{1,5},{2,6},{3,7},{4,0},{5,1},{6,2},{7,3},{8,12},{9,13},{10,... | collective-permute-start | bytes 393224 | tf_op jit(solution)/shard_map/ppermute | solution.py:64
  59.6 11.5 %collective-permute-start.14 = (bf16[128,512]{1,0:T(8,128)(2,1)S(1)}, bf16[128,512]{1,0:T(8,128)(2,1)S(1)}, u32[]{:S(2)}, u32[]{:S(2)}) collective-permute-start(bf16[128,512]{1,0:T(8,128)(2,1)S(1)} %shard_map.90.half_ref.refs_0_), channel_id=1, source_target_pairs={{0,2},{1,3},{2,0},{3,1},{4,6},{5,7},{6,4},{7,5},{8,10},{9,11},{10,... | collective-permute-start | bytes 393224 | tf_op jit(solution)/shard_map/ppermute | solution.py:64
  60.9 10.2 %collective-permute-start.11 = (bf16[128,512]{1,0:T(8,128)(2,1)S(1)}, bf16[128,512]{1,0:T(8,128)(2,1)S(1)}, u32[]{:S(2)}, u32[]{:S(2)}) collective-permute-start(bf16[128,512]{1,0:T(8,128)(2,1)S(1)} %shard_map.90.half_ref.refs_0_), channel_id=1, source_target_pairs={{0,24},{8,16},{16,8},{24,0},{1,25},{9,17},{17,9},{25,1},{2,26},{10... | collective-permute-start | bytes 393224 | tf_op jit(solution)/shard_map/ppermute | solution.py:64
  61.8 10.3 %collective-permute-start.17 = (bf16[128,512]{1,0:T(8,128)(2,1)S(1)}, bf16[128,512]{1,0:T(8,128)(2,1)S(1)}, u32[]{:S(2)}, u32[]{:S(2)}) collective-permute-start(bf16[128,512]{1,0:T(8,128)(2,1)S(1)} %shard_map.90.half_ref.refs_0_), channel_id=1, source_target_pairs={{0,1},{1,0},{2,3},{3,2},{4,5},{5,4},{6,7},{7,6},{8,9},{9,8},{10,11... | collective-permute-start | bytes 393224 | tf_op jit(solution)/shard_map/ppermute | solution.py:64
  64.7 6.4 %collective-permute-start.20 = (bf16[128,512]{1,0:T(8,128)(2,1)S(1)}, bf16[128,512]{1,0:T(8,128)(2,1)S(1)}, u32[]{:S(2)}, u32[]{:S(2)}) collective-permute-start(bf16[128,512]{1,0:T(8,128)(2,1)S(1)} %collective-permute-done.16.refs_3_), channel_id=1, source_target_pairs={{0,1},{1,0},{2,3},{3,2},{4,5},{5,4},{6,7},{7,6},{8,9},{9,8},{10,11... | collective-permute-start | bytes 393224 | tf_op jit(solution)/shard_map/ppermute | solution.py:64
  69.7 2.4 %collective-permute-start.19 = (bf16[128,512]{1,0:T(8,128)(2,1)S(1)}, bf16[128,512]{1,0:T(8,128)(2,1)S(1)}, u32[]{:S(2)}, u32[]{:S(2)}) collective-permute-start(bf16[128,512]{1,0:T(8,128)(2,1)S(1)} %collective-permute-done.15.refs_2_), channel_id=1, source_target_pairs={{0,1},{1,0},{2,3},{3,2},{4,5},{5,4},{6,7},{7,6},{8,9},{9,8},{10,11... | collective-permute-start | bytes 393224 | tf_op jit(solution)/shard_map/ppermute | solution.py:64
  71.1 1.3 %collective-permute-start.18 = (bf16[128,512]{1,0:T(8,128)(2,1)S(1)}, bf16[128,512]{1,0:T(8,128)(2,1)S(1)}, u32[]{:S(2)}, u32[]{:S(2)}) collective-permute-start(bf16[128,512]{1,0:T(8,128)(2,1)S(1)} %collective-permute-done.14.refs_1_), channel_id=1, source_target_pairs={{0,1},{1,0},{2,3},{3,2},{4,5},{5,4},{6,7},{7,6},{8,9},{9,8},{10,11... | collective-permute-start | bytes 393224 | tf_op jit(solution)/shard_map/ppermute | solution.py:64
  72.5 25.3 %slice-start.1 = ((s8[6291456]{0:T(1024)(128)(4,1)}), s8[2097152]{0:T(1024)(128)(4,1)S(1)}, s32[]{:S(2)}) async-start(s8[6291456]{0:T(1024)(128)(4,1)} %bitcast.7), calls=%async_computation.1 | async-start | bytes 4194304
  73.4 7.3 %collective-permute-start.30 = (bf16[384,256]{1,0:T(8,128)(2,1)S(1)}, bf16[384,256]{1,0:T(8,128)(2,1)S(1)}, u32[]{:S(2)}, u32[]{:S(2)}) collective-permute-start(bf16[384,256]{1,0:T(8,128)(2,1)S(1)} %shard_map.92.a_ref), channel_id=1, source_target_pairs={{0,24},{8,16},{16,8},{24,0},{1,25},{9,17},{17,9},{25,1},{2,26},{10... | collective-permute-start | bytes 589832 | tf_op jit(solution)/shard_map/ppermute | solution.py:64
  74.7 10.7 %collective-permute-start.29 = (bf16[384,256]{1,0:T(8,128)(2,1)S(1)}, bf16[384,256]{1,0:T(8,128)(2,1)S(1)}, u32[]{:S(2)}, u32[]{:S(2)}) collective-permute-start(bf16[384,256]{1,0:T(8,128)(2,1)S(1)} %shard_map.92.a_ref), channel_id=1, source_target_pairs={{0,16},{8,24},{16,0},{24,8},{1,17},{9,25},{17,1},{25,9},{2,18},{10... | collective-permute-start | bytes 589832 | tf_op jit(solution)/shard_map/ppermute | solution.py:64
  75.9 10.2 %collective-permute-start.28 = (bf16[384,256]{1,0:T(8,128)(2,1)S(1)}, bf16[384,256]{1,0:T(8,128)(2,1)S(1)}, u32[]{:S(2)}, u32[]{:S(2)}) collective-permute-start(bf16[384,256]{1,0:T(8,128)(2,1)S(1)} %shard_map.92.a_ref), channel_id=1, source_target_pairs={{0,8},{8,0},{16,24},{24,16},{1,9},{9,1},{17,25},{25,17},{2,10},{10... | collective-permute-start | bytes 589832 | tf_op jit(solution)/shard_map/ppermute | solution.py:64
  77.1 10.9 %collective-permute-start.23 = (bf16[128,512]{1,0:T(8,128)(2,1)S(1)}, bf16[128,512]{1,0:T(8,128)(2,1)S(1)}, u32[]{:S(2)}, u32[]{:S(2)}) collective-permute-start(bf16[128,512]{1,0:T(8,128)(2,1)S(1)} %shard_map.91), channel_id=1, source_target_pairs={{0,6},{1,7},{2,4},{3,5},{4,2},{5,3},{6,0},{7,1},{8,14},{9,15},{10,... | collective-permute-start | bytes 393224 | tf_op jit(solution)/shard_map/ppermute | solution.py:64
  79.4 10.9 %collective-permute-start.22 = (bf16[128,512]{1,0:T(8,128)(2,1)S(1)}, bf16[128,512]{1,0:T(8,128)(2,1)S(1)}, u32[]{:S(2)}, u32[]{:S(2)}) collective-permute-start(bf16[128,512]{1,0:T(8,128)(2,1)S(1)} %shard_map.91), channel_id=1, source_target_pairs={{0,4},{1,5},{2,6},{3,7},{4,0},{5,1},{6,2},{7,3},{8,12},{9,13},{10,... | collective-permute-start | bytes 393224 | tf_op jit(solution)/shard_map/ppermute | solution.py:64
  80.8 9.5 %collective-permute-start.21 = (bf16[128,512]{1,0:T(8,128)(2,1)S(1)}, bf16[128,512]{1,0:T(8,128)(2,1)S(1)}, u32[]{:S(2)}, u32[]{:S(2)}) collective-permute-start(bf16[128,512]{1,0:T(8,128)(2,1)S(1)} %shard_map.91), channel_id=1, source_target_pairs={{0,2},{1,3},{2,0},{3,1},{4,6},{5,7},{6,4},{7,5},{8,10},{9,11},{10,... | collective-permute-start | bytes 393224 | tf_op jit(solution)/shard_map/ppermute | solution.py:64
  85.4 12.3 %collective-permute-start.27 = (bf16[4,128,512]{2,1,0:T(8,128)(2,1)S(1)}, bf16[4,128,512]{2,1,0:T(8,128)(2,1)S(1)}, u32[]{:S(2)}, u32[]{:S(2)}) collective-permute-start(bf16[4,128,512]{2,1,0:T(8,128)(2,1)S(1)} %get-tuple-element.71.refs_0_), channel_id=1, source_target_pairs={{0,1},{1,0},{2,3},{3,2},{4,5},{5,4},{6,7},{7,6},{8,9},{9,8},{10,11... | collective-permute-start | bytes 1572872 | tf_op jit(solution)/shard_map/ppermute | solution.py:64
  87.9 5.1 %collective-permute-start.31 = (f32[384,128]{1,0:T(8,128)S(1)}, f32[384,128]{1,0:T(8,128)S(1)}, u32[]{:S(2)}, u32[]{:S(2)}) collective-permute-start(f32[384,128]{1,0:T(8,128)S(1)} %get-tuple-element.73), channel_id=1, source_target_pairs={{0,1},{1,0},{2,3},{3,2},{4,5},{5,4},{6,7},{7,6},{8,9},{9,8},{10,11... | collective-permute-start | bytes 589832 | tf_op jit(solution)/shard_map/ppermute | solution.py:64
  90.3 12.8 %collective-permute-start.26 = (bf16[3,128,512]{2,1,0:T(8,128)(2,1)S(1)}, bf16[3,128,512]{2,1,0:T(8,128)(2,1)S(1)}, u32[]{:S(2)}, u32[]{:S(2)}) collective-permute-start(bf16[3,128,512]{2,1,0:T(8,128)(2,1)S(1)} %pad_maximum_fusion.1.refs_0_), channel_id=1, source_target_pairs={{0,24},{8,16},{16,8},{24,0},{1,25},{9,17},{17,9},{25,1},{2,26},{10... | collective-permute-start | bytes 1179656 | tf_op jit(solution)/shard_map/ppermute | solution.py:64
  91.6 19.1 %collective-permute-start.25 = (bf16[3,128,512]{2,1,0:T(8,128)(2,1)S(1)}, bf16[3,128,512]{2,1,0:T(8,128)(2,1)S(1)}, u32[]{:S(2)}, u32[]{:S(2)}) collective-permute-start(bf16[3,128,512]{2,1,0:T(8,128)(2,1)S(1)} %pad_maximum_fusion.1.refs_0_), channel_id=1, source_target_pairs={{0,16},{8,24},{16,0},{24,8},{1,17},{9,25},{17,1},{25,9},{2,18},{10... | collective-permute-start | bytes 1179656 | tf_op jit(solution)/shard_map/ppermute | solution.py:64
  92.8 18.0 %collective-permute-start.24 = (bf16[3,128,512]{2,1,0:T(8,128)(2,1)S(1)}, bf16[3,128,512]{2,1,0:T(8,128)(2,1)S(1)}, u32[]{:S(2)}, u32[]{:S(2)}) collective-permute-start(bf16[3,128,512]{2,1,0:T(8,128)(2,1)S(1)} %pad_maximum_fusion.1.refs_0_), channel_id=1, source_target_pairs={{0,8},{8,0},{16,24},{24,16},{1,9},{9,1},{17,25},{25,17},{2,10},{10... | collective-permute-start | bytes 1179656 | tf_op jit(solution)/shard_map/ppermute | solution.py:64
  93.0 3.8 %collective-permute-start.32 = (bf16[384,128]{1,0:T(8,128)(2,1)S(1)}, bf16[384,128]{1,0:T(8,128)(2,1)S(1)}, u32[]{:S(2)}, u32[]{:S(2)}) collective-permute-start(bf16[384,128]{1,0:T(8,128)(2,1)S(1)} %get-tuple-element.75), channel_id=1, source_target_pairs={{0,2},{1,3},{2,0},{3,1},{4,6},{5,7},{6,4},{7,5},{8,10},{9,11},{10,... | collective-permute-start | bytes 294920 | tf_op jit(solution)/shard_map/ppermute | solution.py:64
  96.9 5.5 %collective-permute-start.33 = (bf16[384,128]{1,0:T(8,128)(2,1)S(1)}, bf16[384,128]{1,0:T(8,128)(2,1)S(1)}, u32[]{:S(2)}, u32[]{:S(2)}) collective-permute-start(bf16[384,128]{1,0:T(8,128)(2,1)S(1)} %get-tuple-element.77), channel_id=1, source_target_pairs={{0,4},{1,5},{2,6},{3,7},{4,0},{5,1},{6,2},{7,3},{8,12},{9,13},{10,... | collective-permute-start | bytes 294920 | tf_op jit(solution)/shard_map/ppermute | solution.py:64
  110.7 7.4 %collective-permute-start.34 = (bf16[3,128,512]{2,1,0:T(8,128)(2,1)S(1)}, bf16[3,128,512]{2,1,0:T(8,128)(2,1)S(1)}, u32[]{:S(2)}, u32[]{:S(2)}) collective-permute-start(bf16[3,128,512]{2,1,0:T(8,128)(2,1)S(1)} %pad_maximum_fusion.1.refs_0_), channel_id=1, source_target_pairs={{0,1},{1,0},{2,3},{3,2},{4,5},{5,4},{6,7},{7,6},{8,9},{9,8},{10,11... | collective-permute-start | bytes 1179656 | tf_op jit(solution)/shard_map/ppermute | solution.py:64
  111.2 6.9 %collective-permute-start.35 = (bf16[3,128,512]{2,1,0:T(8,128)(2,1)S(1)}, bf16[3,128,512]{2,1,0:T(8,128)(2,1)S(1)}, u32[]{:S(2)}, u32[]{:S(2)}) collective-permute-start(bf16[3,128,512]{2,1,0:T(8,128)(2,1)S(1)} %collective-permute-done.24.refs_1_), channel_id=1, source_target_pairs={{0,1},{1,0},{2,3},{3,2},{4,5},{5,4},{6,7},{7,6},{8,9},{9,8},{10,11... | collective-permute-start | bytes 1179656 | tf_op jit(solution)/shard_map/ppermute | solution.py:64
  111.2 6.8 %collective-permute-start.36 = (bf16[3,128,512]{2,1,0:T(8,128)(2,1)S(1)}, bf16[3,128,512]{2,1,0:T(8,128)(2,1)S(1)}, u32[]{:S(2)}, u32[]{:S(2)}) collective-permute-start(bf16[3,128,512]{2,1,0:T(8,128)(2,1)S(1)} %collective-permute-done.25.refs_2_), channel_id=1, source_target_pairs={{0,1},{1,0},{2,3},{3,2},{4,5},{5,4},{6,7},{7,6},{8,9},{9,8},{10,11... | collective-permute-start | bytes 1179656 | tf_op jit(solution)/shard_map/ppermute | solution.py:64
  111.7 6.4 %collective-permute-start.37 = (bf16[3,128,512]{2,1,0:T(8,128)(2,1)S(1)}, bf16[3,128,512]{2,1,0:T(8,128)(2,1)S(1)}, u32[]{:S(2)}, u32[]{:S(2)}) collective-permute-start(bf16[3,128,512]{2,1,0:T(8,128)(2,1)S(1)} %collective-permute-done.26.refs_3_), channel_id=1, source_target_pairs={{0,1},{1,0},{2,3},{3,2},{4,5},{5,4},{6,7},{7,6},{8,9},{9,8},{10,11... | collective-permute-start | bytes 1179656 | tf_op jit(solution)/shard_map/ppermute | solution.py:64
  111.8 3.8 %collective-permute-start.38 = (f32[384,128]{1,0:T(8,128)S(1)}, f32[384,128]{1,0:T(8,128)S(1)}, u32[]{:S(2)}, u32[]{:S(2)}) collective-permute-start(f32[384,128]{1,0:T(8,128)S(1)} %get-tuple-element.78.own_ref), channel_id=1, source_target_pairs={{0,1},{1,0},{2,3},{3,2},{4,5},{5,4},{6,7},{7,6},{8,9},{9,8},{10,11... | collective-permute-start | bytes 589832 | tf_op jit(solution)/shard_map/ppermute | solution.py:64

commit v4 on v3

--- a/solution.py
+++ b/solution.py
@@ -102,9 +102,14 @@
     rows = x.shape[0]
 
     def body(place_ref, x_ref, *out_refs):
-        for a in range(4):
-            at = pl.ds(pl.multiple_of(xor(place_ref[0], a) * 128, 128), 128)
-            out_refs[a][pl.program_id(0)] = x_ref[:, :, at].reshape(2 * rows, 128)
+        i = pl.program_id(0)
+        for l, order in ((0, (1, 3, 0, 2)), (1, (2, 3, 0, 1))):
+
+            @pl.when(i // 2 == l)
+            def _():
+                for n, a in enumerate(order):
+                    at = pl.ds(pl.multiple_of(xor(place_ref[0], a) * 128, 128), 128)
+                    out_refs[l + n // 2 * 2][n % 2, i % 2] = x_ref[:, :, at].reshape(2 * rows, 128)
 
     def where(i, place_ref):
         k, l = 2 * half + i % 2, i // 2
@@ -118,19 +123,30 @@
             in_specs=[pl.BlockSpec((rows, 2, 512), where)],
             out_specs=(VMEM,) * 4,
         ),
-        out_shape=(pltpu.VMEM((4, 2 * rows, 128), bf16),) * 4,
+        out_shape=(pltpu.VMEM((2, 2, 2 * rows, 128), bf16),) * 4,
         compiler_params=PARAMS,
         cost_estimate=cost(3.3),
     )(place, hbm(x))
 
 
-def project(pieces, masked, us):
+def pair(stay_x, stay_y, came_x, came_y):
+    def body(stay_x_ref, stay_y_ref, came_x_ref, came_y_ref, x_ref, y_ref):
+        x_ref[...] = (stay_x_ref[1].astype(f32) + came_x_ref[1].astype(f32)).astype(bf16)
+        y_ref[...] = (stay_y_ref[1].astype(f32) + came_y_ref[1].astype(f32)).astype(bf16)
+
+    out = (stay_x.shape[1:], bf16)
+    return call(body, [out, out], stay_x, stay_y, came_x, came_y)
+
+
+def project(held, masked):
     rows = masked.shape[0]
 
-    def body(a_ref, b_ref, c_ref, d_ref, s_ref, g_ref, keep_ref, send_ref):
+    def body(*refs):
+        sides, (s_ref, g_ref, keep_ref, send_ref) = (refs[:3], refs[3:6]), refs[6:]
         for i in (2, 3, 0, 1):
-            total = (a_ref[i].astype(f32) + b_ref[i].astype(f32)) + (
-                c_ref[i].astype(f32) + d_ref[i].astype(f32)
+            stay, came, last = sides[i // 2]
+            total = (stay[0, i % 2].astype(f32) + came[0, i % 2].astype(f32)) + last[i % 2].astype(
+                f32
             )
             gradient = total.astype(bf16)
             g_ref[i] = gradient
@@ -145,28 +161,33 @@
     return call(
         body,
         [((4, rows, 128), bf16), ((2, 128, 512), f32), ((2, 128, 512), bf16)],
-        *pieces,
+        *held,
         masked,
-        us=us,
-    )
-
-
-def add_core(keep, came, first):
-    def body(keep_ref, came_ref, a_ref, b_ref):
-        a_ref[...] = (keep_ref[0] + came_ref[0].astype(f32)).astype(first)
-        b_ref[...] = (keep_ref[1] + came_ref[1].astype(f32)).astype(bf16)
-
-    return call(body, [((128, 512), first), ((128, 512), bf16)], keep, came)
-
-
-def finish(parts):
-    def body(a_ref, b_ref, c_ref, d_ref, half_ref):
-        total = (a_ref[...] + b_ref[...].astype(f32)) + (
-            c_ref[...].astype(f32) + d_ref[...].astype(f32)
-        )
-        half_ref[...] = (total * inv_root).astype(bf16)
-
-    return call(body, [((128, 512), bf16)], *parts)[0]
+        us=0.01,
+    )
+
+
+def add_core(keep, came):
+    def body(keep_ref, came_ref, out_ref):
+        out_ref[...] = (keep_ref[...] + came_ref[...].astype(f32)).astype(bf16)
+
+    return call(body, [((2, 128, 512), bf16)], keep, came)[0]
+
+
+def add_chip(keep, came, chips):
+    def body(keep_ref, came_ref, chips_ref, own_ref, next_ref):
+        total = keep_ref[...] + came_ref[...].astype(f32) + chips_ref[...].astype(f32)
+        own_ref[...] = total[0]
+        next_ref[...] = total[1].astype(bf16)
+
+    return call(body, [((128, 512), f32), ((128, 512), bf16)], keep, came, chips)
+
+
+def finish(own, came):
+    def body(own_ref, came_ref, half_ref):
+        half_ref[...] = ((own_ref[...] + came_ref[...].astype(f32)) * inv_root).astype(bf16)
+
+    return call(body, [((128, 512), bf16)], own, came)[0]
 
 
 def own_direction(place, half, one, two):
@@ -360,16 +381,20 @@
 
     high = pack(place, partials[0], 1)
     low = pack(after(place, high), partials[0], 0)
-    high = [high[0]] + [group(high[a], a) for a in (1, 2, 3)]
-    low = [low[0]] + [group(after(low[a], high[1]), a) for a in (1, 2, 3)]
-
-    gradient_high, keep, send = project(high, masked, 1.0)
-    q2, q3 = add_core(keep, core(send), bf16)
-    r2, r3 = chip(q2, 2), chip(q3, 3)
-    low[3] = after(low[3], r2, r3)
-    gradient_low, keep, send = project(low, masked, 1.0)
-    q0, q1 = add_core(keep, core(send), f32)
-    half = finish([q0, chip(q1, 1), r2, r3])
+
+    def over_groups(x, y, stay_x, stay_y):
+        came_x, came_y = group(x, 1), group(y, 2)
+        sum_x, sum_y = pair(stay_x, stay_y, came_x, came_y)
+        return [stay_x, came_x, group(sum_x, 2), stay_y, came_y, group(sum_y, 1)]
+
+    high = over_groups(high[0], high[1], after(high[2], low), high[3])
+    low = over_groups(*after(low[:2], high[1], high[4]), *low[2:])
+
+    gradient_high, keep, send = project(high, masked)
+    chips = chip(add_core(keep, core(send)), 2)
+    gradient_low, keep, send = project(low, masked)
+    own, following = add_chip(keep, core(after(send, chips)), chips)
+    half = finish(own, chip(following, 1))
 
     gathered = [half] + [group(half, a) for a in (1, 2, 3)]
     late = after(half, gathered[1], gathered[2])

time: 122 us -> 117 us (0.959)
  waiting for transfers between devices: 56 us -> 48.4 us
  starting transfers between devices: 35.9 us -> 38.4 us
    ppermute x39 -> x40, waiting for transfers between devices: 56 us -> 48.4 us  [swap(): return lax.ppermute(x, axis, [(i, i ^ bit) for i in range(size)])]
    ppermute x39 -> x40, starting transfers between devices: 35.9 us -> 38.4 us  [swap(): return lax.ppermute(x, axis, [(i, i ^ bit) for i in range(size)])]
    pallas_call x11 -> x13, Pallas kernels: 5.58 us -> 5.63 us  [call(): pl.pallas_call(body, in_specs=[SMEM] * len(scalars) + [VMEM] * len(args),...]
  transfers between devices with their start and end apart: 39 -> 40, of which waited for: 17 -> 21; matrix products, arithmetic and copies ran while one was open for 1% -> 1% of each run, Pallas kernels for 15% -> 17%
where the time goes in v4:
time: 117 us; the launch traced here: 116 us
  waiting for transfers between devices  48.4 us (41%)
  starting transfers between devices  38.4 us (33%)
  Pallas kernels  27.4 us (23%)
    ppermute x40, waiting for transfers between devices, swap(): return lax.ppermute(x, axis, [(i, i ^ bit) for i in range(size)])  48.4 us
    ppermute x40, starting transfers between devices, swap(): return lax.ppermute(x, axis, [(i, i ^ bit) for i in range(size)])  38.4 us
    pallas_call x3, Pallas kernels, update(): pl.pallas_call(body, grid_spec=pltpu.PrefetchScalarGridSpec(num_scalar_pr...  9.09 us
    pallas_call x2, Pallas kernels, pack(): pl.pallas_call(body, grid_spec=pltpu.PrefetchScalarGridSpec(num_scalar_pr...  6.59 us
    pallas_call x13, Pallas kernels, call(): pl.pallas_call(body, in_specs=[SMEM] * len(scalars) + [VMEM] * len(args),...  5.63 us
    pallas_call x1, Pallas kernels, moments(): pl.pallas_call(body, in_specs=[SMEM] + [VMEM] * 6, out_specs=(VMEM,) * 3,...  3.54 us
    pallas_call x1, Pallas kernels, polish(): pl.pallas_call(body, in_specs=[SMEM] + [VMEM] * 3, out_specs=VMEM, out_sh...  2.5 us
  transfers between devices with their start and end apart: 40, of which 21 were waited for; matrix products, arithmetic and copies ran while one was open for 1% of the time, Pallas kernels for 17%

profile of v4, /device:TPU:1, one launch (start us, length us, event | category | flops | bytes accessed | tf_op | source)
XLA Modules:
  0.0 116.5 jit_solution(3118587773921037704)
XLA Ops:
  0.7 3.3 %shard_map.84 = (bf16[2,2,384,128]{3,2,1,0:T(8,128)(2,1)S(1)}, bf16[2,2,384,128]{3,2,1,0:T(8,128)(2,1)S(1)}, bf16[2,2,384,128]{3,2,1,0:T(8,128)(2,1)S(1)}, bf16[2,2,384,128]{3,2,1,0:T(8,128)(2,1)S(1)}) custom-call(s32[3]{0:T(128)S(1)} %pad_add_fusion.place_ref, bf16[192,2,4096]{2,1,0:T(2,128)(2,1)} %bitcast.9), custom_call_target="tpu_custom_call" | custom-call | bytes 11550000 | tf_op jit(solution)/shard_map/pallas_call | solution.py:118
  4.0 2.1 %collective-permute-start = (bf16[2,2,384,128]{3,2,1,0:T(8,128)(2,1)S(1)}, bf16[2,2,384,128]{3,2,1,0:T(8,128)(2,1)S(1)}, u32[]{:S(2)}, u32[]{:S(2)}) collective-permute-start(bf16[2,2,384,128]{3,2,1,0:T(8,128)(2,1)S(1)} %get-tuple-element.47), channel_id=1, source_target_pairs={{0,8},{8,0},{16,24},{24,16},{1,9},{9,1},{17,25},{25,17},{2,10},{10... | collective-permute-start | bytes 1179656 | tf_op jit(solution)/shard_map/ppermute | solution.py:64
  6.1 1.2 %collective-permute-start.1 = (bf16[2,2,384,128]{3,2,1,0:T(8,128)(2,1)S(1)}, bf16[2,2,384,128]{3,2,1,0:T(8,128)(2,1)S(1)}, u32[]{:S(2)}, u32[]{:S(2)}) collective-permute-start(bf16[2,2,384,128]{3,2,1,0:T(8,128)(2,1)S(1)} %get-tuple-element.48), channel_id=1, source_target_pairs={{0,16},{8,24},{16,0},{24,8},{1,17},{9,25},{17,1},{25,9},{2,18},{10... | collective-permute-start | bytes 1179656 | tf_op jit(solution)/shard_map/ppermute | solution.py:64
  7.4 1.0 reshape.11
  8.4 3.3 %shard_map.85 = (bf16[2,2,384,128]{3,2,1,0:T(8,128)(2,1)S(1)}, bf16[2,2,384,128]{3,2,1,0:T(8,128)(2,1)S(1)}, bf16[2,2,384,128]{3,2,1,0:T(8,128)(2,1)S(1)}, bf16[2,2,384,128]{3,2,1,0:T(8,128)(2,1)S(1)}) custom-call(s32[3]{0:T(128)S(1)} %pad_add_fusion.place_ref, bf16[192,2,4096]{2,1,0:T(2,128)(2,1)} %bitcast.10), custom_call_target="tpu_custom_call" | custom-call | bytes 11550000 | tf_op jit(solution)/shard_map/pallas_call | solution.py:118
  11.7 3.3 %collective-permute-done.came_x_ref.refs_1_ = bf16[2,2,384,128]{3,2,1,0:T(8,128)(2,1)S(1)} collective-permute-done((bf16[2,2,384,128]{3,2,1,0:T(8,128)(2,1)S(1)}, bf16[2,2,384,128]{3,2,1,0:T(8,128)(2,1)S(1)}, u32[]{:S(2)}, u32[]{:S(2)}) %collective-permute-start) | collective-permute-done | bytes 393248 | tf_op jit(solution)/shard_map/ppermute | solution.py:64
  15.0 0.8 collective-permute-done.1.came_y_ref.refs_4_
  15.9 1.3 %collective-permute-start.6 = (bf16[2,384,128]{2,1,0:T(8,128)(2,1)S(1)}, bf16[2,384,128]{2,1,0:T(8,128)(2,1)S(1)}, u32[]{:S(2)}, u32[]{:S(2)}) collective-permute-start(bf16[2,384,128]{2,1,0:T(8,128)(2,1)S(1)} %get-tuple-element.63), channel_id=1, source_target_pairs={{0,16},{8,24},{16,0},{24,8},{1,17},{9,25},{17,1},{25,9},{2,18},{10... | collective-permute-start | bytes 589832 | tf_op jit(solution)/shard_map/ppermute | solution.py:64
  17.8 1.2 %collective-permute-start.2 = (bf16[2,2,384,128]{3,2,1,0:T(8,128)(2,1)S(1)}, bf16[2,2,384,128]{3,2,1,0:T(8,128)(2,1)S(1)}, u32[]{:S(2)}, u32[]{:S(2)}) collective-permute-start(bf16[2,2,384,128]{3,2,1,0:T(8,128)(2,1)S(1)} %get-tuple-element.55), channel_id=1, source_target_pairs={{0,8},{8,0},{16,24},{24,16},{1,9},{9,1},{17,25},{25,17},{2,10},{10... | collective-permute-start | bytes 1179656 | tf_op jit(solution)/shard_map/ppermute | solution.py:64
  19.2 1.3 %collective-permute-done.6.refs_2_ = bf16[2,384,128]{2,1,0:T(8,128)(2,1)S(1)} collective-permute-done((bf16[2,384,128]{2,1,0:T(8,128)(2,1)S(1)}, bf16[2,384,128]{2,1,0:T(8,128)(2,1)S(1)}, u32[]{:S(2)}, u32[]{:S(2)}) %collective-permute-start.6) | collective-permute-done | bytes 196640 | tf_op jit(solution)/shard_map/ppermute | solution.py:64
  20.5 1.5 %collective-permute-done.7.refs_5_ = bf16[2,384,128]{2,1,0:T(8,128)(2,1)S(1)} collective-permute-done((bf16[2,384,128]{2,1,0:T(8,128)(2,1)S(1)}, bf16[2,384,128]{2,1,0:T(8,128)(2,1)S(1)}, u32[]{:S(2)}, u32[]{:S(2)}) %collective-permute-start.7) | collective-permute-done | bytes 196640 | tf_op jit(solution)/shard_map/ppermute | solution.py:64
  22.5 5.2 %collective-permute-start.8 = (bf16[2,128,512]{2,1,0:T(8,128)(2,1)S(1)}, bf16[2,128,512]{2,1,0:T(8,128)(2,1)S(1)}, u32[]{:S(2)}, u32[]{:S(2)}) collective-permute-start(bf16[2,128,512]{2,1,0:T(8,128)(2,1)S(1)} %get-tuple-element.66), channel_id=1, source_target_pairs={{0,1},{1,0},{2,3},{3,2},{4,5},{5,4},{6,7},{7,6},{8,9},{9,8},{10,11... | collective-permute-start | bytes 786440 | tf_op jit(solution)/shard_map/ppermute | solution.py:64
  27.7 1.2 collective-permute-done.8.came_ref
  28.9 2.4 %collective-permute-start.9 = (bf16[2,128,512]{2,1,0:T(8,128)(2,1)S(1)}, bf16[2,128,512]{2,1,0:T(8,128)(2,1)S(1)}, u32[]{:S(2)}, u32[]{:S(2)}) collective-permute-start(bf16[2,128,512]{2,1,0:T(8,128)(2,1)S(1)} %shard_map.90), channel_id=1, source_target_pairs={{0,4},{1,5},{2,6},{3,7},{4,0},{5,1},{6,2},{7,3},{8,12},{9,13},{10,... | collective-permute-start | bytes 786440 | tf_op jit(solution)/shard_map/ppermute | solution.py:64
  32.0 4.3 %collective-permute-done.4.refs_2_ = bf16[2,384,128]{2,1,0:T(8,128)(2,1)S(1)} collective-permute-done((bf16[2,384,128]{2,1,0:T(8,128)(2,1)S(1)}, bf16[2,384,128]{2,1,0:T(8,128)(2,1)S(1)}, u32[]{:S(2)}, u32[]{:S(2)}) %collective-permute-start.4) | collective-permute-done | bytes 196640 | tf_op jit(solution)/shard_map/ppermute | solution.py:64
  37.0 6.0 %collective-permute-done.9.chips_ref = bf16[2,128,512]{2,1,0:T(8,128)(2,1)S(1)} collective-permute-done((bf16[2,128,512]{2,1,0:T(8,128)(2,1)S(1)}, bf16[2,128,512]{2,1,0:T(8,128)(2,1)S(1)}, u32[]{:S(2)}, u32[]{:S(2)}) %collective-permute-start.9) | collective-permute-done | bytes 262176 | tf_op jit(solution)/shard_map/ppermute | solution.py:64
  43.1 1.2 %collective-permute-start.10 = (bf16[2,128,512]{2,1,0:T(8,128)(2,1)S(1)}, bf16[2,128,512]{2,1,0:T(8,128)(2,1)S(1)}, u32[]{:S(2)}, u32[]{:S(2)}) collective-permute-start(bf16[2,128,512]{2,1,0:T(8,128)(2,1)S(1)} %get-tuple-element.67), channel_id=1, source_target_pairs={{0,1},{1,0},{2,3},{3,2},{4,5},{5,4},{6,7},{7,6},{8,9},{9,8},{10,11... | collective-permute-start | bytes 786440 | tf_op jit(solution)/shard_map/ppermute | solution.py:64
  44.3 1.2 collective-permute-done.10.came_ref
  46.0 4.3 %collective-permute-done.11.came_ref = bf16[128,512]{1,0:T(8,128)(2,1)S(1)} collective-permute-done((bf16[128,512]{1,0:T(8,128)(2,1)S(1)}, bf16[128,512]{1,0:T(8,128)(2,1)S(1)}, u32[]{:S(2)}, u32[]{:S(2)}) %collective-permute-start.11) | collective-permute-done | bytes 131104 | tf_op jit(solution)/shard_map/ppermute | solution.py:64
  50.8 3.3 %collective-permute-start.17 = (bf16[128,512]{1,0:T(8,128)(2,1)S(1)}, bf16[128,512]{1,0:T(8,128)(2,1)S(1)}, u32[]{:S(2)}, u32[]{:S(2)}) collective-permute-start(bf16[128,512]{1,0:T(8,128)(2,1)S(1)} %shard_map.92.half_ref.refs_0_), channel_id=1, source_target_pairs={{0,6},{1,7},{2,4},{3,5},{4,2},{5,3},{6,0},{7,1},{8,14},{9,15},{10,... | collective-permute-start | bytes 393224 | tf_op jit(solution)/shard_map/ppermute | solution.py:64
  54.8 1.8 %collective-permute-start.12 = (bf16[128,512]{1,0:T(8,128)(2,1)S(1)}, bf16[128,512]{1,0:T(8,128)(2,1)S(1)}, u32[]{:S(2)}, u32[]{:S(2)}) collective-permute-start(bf16[128,512]{1,0:T(8,128)(2,1)S(1)} %shard_map.92.half_ref.refs_0_), channel_id=1, source_target_pairs={{0,24},{8,16},{16,8},{24,0},{1,25},{9,17},{17,9},{25,1},{2,26},{10... | collective-permute-start | bytes 393224 | tf_op jit(solution)/shard_map/ppermute | solution.py:64
  56.6 2.9 %collective-permute-start.18 = (bf16[128,512]{1,0:T(8,128)(2,1)S(1)}, bf16[128,512]{1,0:T(8,128)(2,1)S(1)}, u32[]{:S(2)}, u32[]{:S(2)}) collective-permute-start(bf16[128,512]{1,0:T(8,128)(2,1)S(1)} %shard_map.92.half_ref.refs_0_), channel_id=1, source_target_pairs={{0,1},{1,0},{2,3},{3,2},{4,5},{5,4},{6,7},{7,6},{8,9},{9,8},{10,11... | collective-permute-start | bytes 393224 | tf_op jit(solution)/shard_map/ppermute | solution.py:64
  59.5 0.7 collective-permute-start.21
  60.1 4.5 %collective-permute-done.16.refs_2_ = bf16[128,512]{1,0:T(8,128)(2,1)S(1)} collective-permute-done((bf16[128,512]{1,0:T(8,128)(2,1)S(1)}, bf16[128,512]{1,0:T(8,128)(2,1)S(1)}, u32[]{:S(2)}, u32[]{:S(2)}) %collective-permute-start.16) | collective-permute-done | bytes 131104 | tf_op jit(solution)/shard_map/ppermute | solution.py:64
  64.7 1.4 %collective-permute-start.20 = (bf16[128,512]{1,0:T(8,128)(2,1)S(1)}, bf16[128,512]{1,0:T(8,128)(2,1)S(1)}, u32[]{:S(2)}, u32[]{:S(2)}) collective-permute-start(bf16[128,512]{1,0:T(8,128)(2,1)S(1)} %collective-permute-done.16.refs_2_), channel_id=1, source_target_pairs={{0,1},{1,0},{2,3},{3,2},{4,5},{5,4},{6,7},{7,6},{8,9},{9,8},{10,11... | collective-permute-start | bytes 393224 | tf_op jit(solution)/shard_map/ppermute | solution.py:64
  66.1 1.0 collective-permute-done.20.refs_6_
  67.4 0.9 shard_map.94.a_ref
  68.4 2.2 %collective-permute-start.31 = (bf16[384,256]{1,0:T(8,128)(2,1)S(1)}, bf16[384,256]{1,0:T(8,128)(2,1)S(1)}, u32[]{:S(2)}, u32[]{:S(2)}) collective-permute-start(bf16[384,256]{1,0:T(8,128)(2,1)S(1)} %shard_map.94.a_ref), channel_id=1, source_target_pairs={{0,24},{8,16},{16,8},{24,0},{1,25},{9,17},{17,9},{25,1},{2,26},{10... | collective-permute-start | bytes 589832 | tf_op jit(solution)/shard_map/ppermute | solution.py:64
  71.1 0.9 shard_map.93
  72.1 2.4 %collective-permute-start.24 = (bf16[128,512]{1,0:T(8,128)(2,1)S(1)}, bf16[128,512]{1,0:T(8,128)(2,1)S(1)}, u32[]{:S(2)}, u32[]{:S(2)}) collective-permute-start(bf16[128,512]{1,0:T(8,128)(2,1)S(1)} %shard_map.93), channel_id=1, source_target_pairs={{0,6},{1,7},{2,4},{3,5},{4,2},{5,3},{6,0},{7,1},{8,14},{9,15},{10,... | collective-permute-start | bytes 393224 | tf_op jit(solution)/shard_map/ppermute | solution.py:64
  74.5 1.2 %collective-permute-done.31.d_ref = bf16[384,256]{1,0:T(8,128)(2,1)S(1)} collective-permute-done((bf16[384,256]{1,0:T(8,128)(2,1)S(1)}, bf16[384,256]{1,0:T(8,128)(2,1)S(1)}, u32[]{:S(2)}, u32[]{:S(2)}) %collective-permute-start.31) | collective-permute-done | bytes 196640 | tf_op jit(solution)/shard_map/ppermute | solution.py:64
  75.7 3.5 %shard_map.95 = (f32[512,2,256]{2,1,0:T(2,128)}, f32[512,2,256]{2,1,0:T(2,128)}, bf16[4,128,512]{2,1,0:T(8,128)(2,1)S(1)}) custom-call(s32[3]{0:T(128)S(1)} %pad_add_fusion.place_ref, bf16[128,512]{1,0:T(8,128)(2,1)S(1)} %shard_map.92.half_ref.refs_0_, bf16[128,512]{1,0:T(8,128)(2,1)S(1)} %collective-permute-done.13.refs_1_, ...), custom_call_target="tpu_custom_call" | custom-call | bytes 12250000 | tf_op jit(solution)/shard_map/pallas_call | solution.py:217
  79.3 1.1 collective-permute-done.30.c_ref
  80.4 0.7 collective-permute-start.28
  81.1 1.8 %shard_map.97 = (f32[384,256]{1,0:T(8,128)S(1)}, f32[384,128]{1,0:T(8,128)S(1)}, f32[384,128]{1,0:T(8,128)S(1)}) custom-call(s32[3]{0:T(128)S(1)} %pad_add_fusion.place_ref, bf16[384,256]{1,0:T(8,128)(2,1)S(1)} %shard_map.94.a_ref, bf16[384,256]{1,0:T(8,128)(2,1)S(1)} %collective-permute-done.29.b_ref, bf16[384,256]{1,0:T(8,128)(2,1)S(1)} %collective-permute-done.30.c_ref, ...), custom_call_target="tpu_custom_call" | custom-call | bytes 6300000 | tf_op jit(solution)/shard_map/pallas_call | solution.py:83
  82.9 2.3 %collective-permute-done.23 = bf16[128,512]{1,0:T(8,128)(2,1)S(1)} collective-permute-done((bf16[128,512]{1,0:T(8,128)(2,1)S(1)}, bf16[128,512]{1,0:T(8,128)(2,1)S(1)}, u32[]{:S(2)}, u32[]{:S(2)}) %collective-permute-start.23) | collective-permute-done | bytes 131104 | tf_op jit(solution)/shard_map/ppermute | solution.py:64
  85.3 2.2 %collective-permute-start.27 = (bf16[3,128,512]{2,1,0:T(8,128)(2,1)S(1)}, bf16[3,128,512]{2,1,0:T(8,128)(2,1)S(1)}, u32[]{:S(2)}, u32[]{:S(2)}) collective-permute-start(bf16[3,128,512]{2,1,0:T(8,128)(2,1)S(1)} %pad_maximum_fusion.1.refs_0_), channel_id=1, source_target_pairs={{0,24},{8,16},{16,8},{24,0},{1,25},{9,17},{17,9},{25,1},{2,26},{10... | collective-permute-start | bytes 1179656 | tf_op jit(solution)/shard_map/ppermute | solution.py:64
  88.1 3.7 %collective-permute-done.33.came_ref = bf16[384,128]{1,0:T(8,128)(2,1)S(1)} collective-permute-done((bf16[384,128]{1,0:T(8,128)(2,1)S(1)}, bf16[384,128]{1,0:T(8,128)(2,1)S(1)}, u32[]{:S(2)}, u32[]{:S(2)}) %collective-permute-start.33) | collective-permute-done | bytes 98336 | tf_op jit(solution)/shard_map/ppermute | solution.py:64
  91.9 1.0 collective-permute-start.34
  92.9 2.4 %shard_map.96.refs_4_ = f32[192,2,4096]{2,1,0:T(2,128)} custom-call(s32[3]{0:T(128)S(1)} %pad_add_fusion.place_ref, f32[192,2,4096]{2,1,0:T(2,128)S(1)} %bitcast.8, bf16[384,512]{1,0:T(8,128)(2,1)S(1)} %pad_maximum_fusion.refs_6_.s_ref, bf16[4,128,512]{2,1,0:T(8,128)(2,1)S(1)} %get-tuple-element.75.refs_0_, ...), custom_call_target="tpu_custom_call" | custom-call | bytes 8750000 | tf_op jit(solution)/shard_map/pallas_call | solution.py:346
  95.3 2.1 %collective-permute-done.34.came_ref = bf16[384,128]{1,0:T(8,128)(2,1)S(1)} collective-permute-done((bf16[384,128]{1,0:T(8,128)(2,1)S(1)}, bf16[384,128]{1,0:T(8,128)(2,1)S(1)}, u32[]{:S(2)}, u32[]{:S(2)}) %collective-permute-start.34) | collective-permute-done | bytes 98336 | tf_op jit(solution)/shard_map/ppermute | solution.py:64
  97.4 0.7 shard_map.100
  98.1 7.6 %collective-permute-done.26.refs_2_ = bf16[3,128,512]{2,1,0:T(8,128)(2,1)S(1)} collective-permute-done((bf16[3,128,512]{2,1,0:T(8,128)(2,1)S(1)}, bf16[3,128,512]{2,1,0:T(8,128)(2,1)S(1)}, u32[]{:S(2)}, u32[]{:S(2)}) %collective-permute-start.26) | collective-permute-done | bytes 393248 | tf_op jit(solution)/shard_map/ppermute | solution.py:64
  105.7 0.6 collective-permute-start.35
  106.3 0.5 collective-permute-start.37
  107.3 3.3 %shard_map.101.refs_4_ = f32[192,2,4096]{2,1,0:T(2,128)} custom-call(s32[3]{0:T(128)S(1)} %pad_add_fusion.place_ref, f32[192,2,4096]{2,1,0:T(2,128)S(1)} %bitcast.8, bf16[384,512]{1,0:T(8,128)(2,1)S(1)} %pad_maximum_fusion.refs_6_.s_ref, bf16[3,128,512]{2,1,0:T(8,128)(2,1)S(1)} %pad_maximum_fusion.1.refs_0_, ...), custom_call_target="tpu_custom_call", output_to_operand_aliasing={{}: (7, {})} | custom-call | bytes 12250000 | tf_op jit(solution)/shard_map/pallas_call | solution.py:346
  110.6 2.5 %shard_map.103 = bf16[192,2,256]{2,1,0:T(2,128)(2,1)} custom-call(s32[3]{0:T(128)S(1)} %pad_add_fusion.place_ref, f32[384,256]{1,0:T(8,128)S(1)} %get-tuple-element.89.spanned_ref, f32[384,128]{1,0:T(8,128)S(1)} %get-tuple-element.82.own_ref, f32[384,128]{1,0:T(8,128)S(1)} %collective-permute-done.39.other_ref), custom_call_target="tpu_custom_call" | custom-call | bytes 6300000 | tf_op jit(solution)/shard_map/pallas_call | solution.py:309
  113.2 3.3 %shard_map.102 = f32[192,2,4096]{2,1,0:T(2,128)} custom-call(s32[3]{0:T(128)S(1)} %pad_add_fusion.place_ref, f32[192,2,4096]{2,1,0:T(2,128)S(1)} %bitcast.8, bf16[384,512]{1,0:T(8,128)(2,1)S(1)} %pad_maximum_fusion.refs_6_.s_ref, bf16[3,128,512]{2,1,0:T(8,128)(2,1)S(1)} %collective-permute-done.35.refs_0_, ...), custom_call_target="tpu_custom_call", output_to_operand_aliasing={{}: (7, {})} | custom-call | bytes 12250000 | tf_op jit(solution)/shard_map/pallas_call | solution.py:346
  (68 shorter events, 6.8 us)
Async XLA Ops:
  4.0 10.9 %collective-permute-start = (bf16[2,2,384,128]{3,2,1,0:T(8,128)(2,1)S(1)}, bf16[2,2,384,128]{3,2,1,0:T(8,128)(2,1)S(1)}, u32[]{:S(2)}, u32[]{:S(2)}) collective-permute-start(bf16[2,2,384,128]{3,2,1,0:T(8,128)(2,1)S(1)} %get-tuple-element.47), channel_id=1, source_target_pairs={{0,8},{8,0},{16,24},{24,16},{1,9},{9,1},{17,25},{25,17},{2,10},{10... | collective-permute-start | bytes 1179656 | tf_op jit(solution)/shard_map/ppermute | solution.py:64
  6.1 9.7 %collective-permute-start.1 = (bf16[2,2,384,128]{3,2,1,0:T(8,128)(2,1)S(1)}, bf16[2,2,384,128]{3,2,1,0:T(8,128)(2,1)S(1)}, u32[]{:S(2)}, u32[]{:S(2)}) collective-permute-start(bf16[2,2,384,128]{3,2,1,0:T(8,128)(2,1)S(1)} %get-tuple-element.48), channel_id=1, source_target_pairs={{0,16},{8,24},{16,0},{24,8},{1,17},{9,25},{17,1},{25,9},{2,18},{10... | collective-permute-start | bytes 1179656 | tf_op jit(solution)/shard_map/ppermute | solution.py:64
  15.9 55.2 %copy-start = (f32[512,2,256]{2,1,0:T(2,128)S(1)}, f32[512,2,256]{2,1,0:T(2,128)}, u32[]{:S(2)}) copy-start(f32[512,2,256]{2,1,0:T(2,128)} %refs_4_.1) | copy-start | bytes 3145732
  15.9 55.2 %copy-start.1 = (f32[512,2,256]{2,1,0:T(2,128)S(1)}, f32[512,2,256]{2,1,0:T(2,128)}, u32[]{:S(2)}) copy-start(f32[512,2,256]{2,1,0:T(2,128)} %refs_5_.1) | copy-start | bytes 3145732
  15.9 4.6 %collective-permute-start.6 = (bf16[2,384,128]{2,1,0:T(8,128)(2,1)S(1)}, bf16[2,384,128]{2,1,0:T(8,128)(2,1)S(1)}, u32[]{:S(2)}, u32[]{:S(2)}) collective-permute-start(bf16[2,384,128]{2,1,0:T(8,128)(2,1)S(1)} %get-tuple-element.63), channel_id=1, source_target_pairs={{0,16},{8,24},{16,0},{24,8},{1,17},{9,25},{17,1},{25,9},{2,18},{10... | collective-permute-start | bytes 589832 | tf_op jit(solution)/shard_map/ppermute | solution.py:64
  17.2 4.8 %collective-permute-start.7 = (bf16[2,384,128]{2,1,0:T(8,128)(2,1)S(1)}, bf16[2,384,128]{2,1,0:T(8,128)(2,1)S(1)}, u32[]{:S(2)}, u32[]{:S(2)}) collective-permute-start(bf16[2,384,128]{2,1,0:T(8,128)(2,1)S(1)} %get-tuple-element.64), channel_id=1, source_target_pairs={{0,8},{8,0},{16,24},{24,16},{1,9},{9,1},{17,25},{25,17},{2,10},{10... | collective-permute-start | bytes 589832 | tf_op jit(solution)/shard_map/ppermute | solution.py:64
  17.8 13.6 %collective-permute-start.2 = (bf16[2,2,384,128]{3,2,1,0:T(8,128)(2,1)S(1)}, bf16[2,2,384,128]{3,2,1,0:T(8,128)(2,1)S(1)}, u32[]{:S(2)}, u32[]{:S(2)}) collective-permute-start(bf16[2,2,384,128]{3,2,1,0:T(8,128)(2,1)S(1)} %get-tuple-element.55), channel_id=1, source_target_pairs={{0,8},{8,0},{16,24},{24,16},{1,9},{9,1},{17,25},{25,17},{2,10},{10... | collective-permute-start | bytes 1179656 | tf_op jit(solution)/shard_map/ppermute | solution.py:64
  19.0 12.4 %collective-permute-start.3 = (bf16[2,2,384,128]{3,2,1,0:T(8,128)(2,1)S(1)}, bf16[2,2,384,128]{3,2,1,0:T(8,128)(2,1)S(1)}, u32[]{:S(2)}, u32[]{:S(2)}) collective-permute-start(bf16[2,2,384,128]{3,2,1,0:T(8,128)(2,1)S(1)} %get-tuple-element.57), channel_id=1, source_target_pairs={{0,16},{8,24},{16,0},{24,8},{1,17},{9,25},{17,1},{25,9},{2,18},{10... | collective-permute-start | bytes 1179656 | tf_op jit(solution)/shard_map/ppermute | solution.py:64
  22.5 6.4 %collective-permute-start.8 = (bf16[2,128,512]{2,1,0:T(8,128)(2,1)S(1)}, bf16[2,128,512]{2,1,0:T(8,128)(2,1)S(1)}, u32[]{:S(2)}, u32[]{:S(2)}) collective-permute-start(bf16[2,128,512]{2,1,0:T(8,128)(2,1)S(1)} %get-tuple-element.66), channel_id=1, source_target_pairs={{0,1},{1,0},{2,3},{3,2},{4,5},{5,4},{6,7},{7,6},{8,9},{9,8},{10,11... | collective-permute-start | bytes 786440 | tf_op jit(solution)/shard_map/ppermute | solution.py:64
  28.9 14.1 %collective-permute-start.9 = (bf16[2,128,512]{2,1,0:T(8,128)(2,1)S(1)}, bf16[2,128,512]{2,1,0:T(8,128)(2,1)S(1)}, u32[]{:S(2)}, u32[]{:S(2)}) collective-permute-start(bf16[2,128,512]{2,1,0:T(8,128)(2,1)S(1)} %shard_map.90), channel_id=1, source_target_pairs={{0,4},{1,5},{2,6},{3,7},{4,0},{5,1},{6,2},{7,3},{8,12},{9,13},{10,... | collective-permute-start | bytes 786440 | tf_op jit(solution)/shard_map/ppermute | solution.py:64
  31.3 61.6 %slice-start = ((s8[6291456]{0:T(1024)(128)(4,1)}), s8[4194304]{0:T(1024)(128)(4,1)S(1)}, s32[]{:S(2)}) async-start(s8[6291456]{0:T(1024)(128)(4,1)} %bitcast.7), calls=%async_computation | async-start | bytes 8388608
  31.4 4.9 %collective-permute-start.4 = (bf16[2,384,128]{2,1,0:T(8,128)(2,1)S(1)}, bf16[2,384,128]{2,1,0:T(8,128)(2,1)S(1)}, u32[]{:S(2)}, u32[]{:S(2)}) collective-permute-start(bf16[2,384,128]{2,1,0:T(8,128)(2,1)S(1)} %get-tuple-element.58), channel_id=1, source_target_pairs={{0,16},{8,24},{16,0},{24,8},{1,17},{9,25},{17,1},{25,9},{2,18},{10... | collective-permute-start | bytes 589832 | tf_op jit(solution)/shard_map/ppermute | solution.py:64
  31.7 4.8 %collective-permute-start.5 = (bf16[2,384,128]{2,1,0:T(8,128)(2,1)S(1)}, bf16[2,384,128]{2,1,0:T(8,128)(2,1)S(1)}, u32[]{:S(2)}, u32[]{:S(2)}) collective-permute-start(bf16[2,384,128]{2,1,0:T(8,128)(2,1)S(1)} %get-tuple-element.59), channel_id=1, source_target_pairs={{0,8},{8,0},{16,24},{24,16},{1,9},{9,1},{17,25},{25,17},{2,10},{10... | collective-permute-start | bytes 589832 | tf_op jit(solution)/shard_map/ppermute | solution.py:64
  43.1 2.4 %collective-permute-start.10 = (bf16[2,128,512]{2,1,0:T(8,128)(2,1)S(1)}, bf16[2,128,512]{2,1,0:T(8,128)(2,1)S(1)}, u32[]{:S(2)}, u32[]{:S(2)}) collective-permute-start(bf16[2,128,512]{2,1,0:T(8,128)(2,1)S(1)} %get-tuple-element.67), channel_id=1, source_target_pairs={{0,1},{1,0},{2,3},{3,2},{4,5},{5,4},{6,7},{7,6},{8,9},{9,8},{10,11... | collective-permute-start | bytes 786440 | tf_op jit(solution)/shard_map/ppermute | solution.py:64
  45.5 4.8 %collective-permute-start.11 = (bf16[128,512]{1,0:T(8,128)(2,1)S(1)}, bf16[128,512]{1,0:T(8,128)(2,1)S(1)}, u32[]{:S(2)}, u32[]{:S(2)}) collective-permute-start(bf16[128,512]{1,0:T(8,128)(2,1)S(1)} %get-tuple-element.69), channel_id=1, source_target_pairs={{0,2},{1,3},{2,0},{3,1},{4,6},{5,7},{6,4},{7,5},{8,10},{9,11},{10,... | collective-permute-start | bytes 393224 | tf_op jit(solution)/shard_map/ppermute | solution.py:64
  50.3 3.9 %collective-permute-start.14 = (bf16[128,512]{1,0:T(8,128)(2,1)S(1)}, bf16[128,512]{1,0:T(8,128)(2,1)S(1)}, u32[]{:S(2)}, u32[]{:S(2)}) collective-permute-start(bf16[128,512]{1,0:T(8,128)(2,1)S(1)} %shard_map.92.half_ref.refs_0_), channel_id=1, source_target_pairs={{0,16},{8,24},{16,0},{24,8},{1,17},{9,25},{17,1},{25,9},{2,18},{10... | collective-permute-start | bytes 393224 | tf_op jit(solution)/shard_map/ppermute | solution.py:64
  50.6 3.8 %collective-permute-start.13 = (bf16[128,512]{1,0:T(8,128)(2,1)S(1)}, bf16[128,512]{1,0:T(8,128)(2,1)S(1)}, u32[]{:S(2)}, u32[]{:S(2)}) collective-permute-start(bf16[128,512]{1,0:T(8,128)(2,1)S(1)} %shard_map.92.half_ref.refs_0_), channel_id=1, source_target_pairs={{0,8},{8,0},{16,24},{24,16},{1,9},{9,1},{17,25},{25,17},{2,10},{10... | collective-permute-start | bytes 393224 | tf_op jit(solution)/shard_map/ppermute | solution.py:64
  50.8 8.7 %collective-permute-start.17 = (bf16[128,512]{1,0:T(8,128)(2,1)S(1)}, bf16[128,512]{1,0:T(8,128)(2,1)S(1)}, u32[]{:S(2)}, u32[]{:S(2)}) collective-permute-start(bf16[128,512]{1,0:T(8,128)(2,1)S(1)} %shard_map.92.half_ref.refs_0_), channel_id=1, source_target_pairs={{0,6},{1,7},{2,4},{3,5},{4,2},{5,3},{6,0},{7,1},{8,14},{9,15},{10,... | collective-permute-start | bytes 393224 | tf_op jit(solution)/shard_map/ppermute | solution.py:64
  54.1 10.6 %collective-permute-start.16 = (bf16[128,512]{1,0:T(8,128)(2,1)S(1)}, bf16[128,512]{1,0:T(8,128)(2,1)S(1)}, u32[]{:S(2)}, u32[]{:S(2)}) collective-permute-start(bf16[128,512]{1,0:T(8,128)(2,1)S(1)} %shard_map.92.half_ref.refs_0_), channel_id=1, source_target_pairs={{0,4},{1,5},{2,6},{3,7},{4,0},{5,1},{6,2},{7,3},{8,12},{9,13},{10,... | collective-permute-start | bytes 393224 | tf_op jit(solution)/shard_map/ppermute | solution.py:64
  54.4 11.7 %collective-permute-start.15 = (bf16[128,512]{1,0:T(8,128)(2,1)S(1)}, bf16[128,512]{1,0:T(8,128)(2,1)S(1)}, u32[]{:S(2)}, u32[]{:S(2)}) collective-permute-start(bf16[128,512]{1,0:T(8,128)(2,1)S(1)} %shard_map.92.half_ref.refs_0_), channel_id=1, source_target_pairs={{0,2},{1,3},{2,0},{3,1},{4,6},{5,7},{6,4},{7,5},{8,10},{9,11},{10,... | collective-permute-start | bytes 393224 | tf_op jit(solution)/shard_map/ppermute | solution.py:64
  54.8 11.3 %collective-permute-start.12 = (bf16[128,512]{1,0:T(8,128)(2,1)S(1)}, bf16[128,512]{1,0:T(8,128)(2,1)S(1)}, u32[]{:S(2)}, u32[]{:S(2)}) collective-permute-start(bf16[128,512]{1,0:T(8,128)(2,1)S(1)} %shard_map.92.half_ref.refs_0_), channel_id=1, source_target_pairs={{0,24},{8,16},{16,8},{24,0},{1,25},{9,17},{17,9},{25,1},{2,26},{10... | collective-permute-start | bytes 393224 | tf_op jit(solution)/shard_map/ppermute | solution.py:64
  56.6 10.5 %collective-permute-start.18 = (bf16[128,512]{1,0:T(8,128)(2,1)S(1)}, bf16[128,512]{1,0:T(8,128)(2,1)S(1)}, u32[]{:S(2)}, u32[]{:S(2)}) collective-permute-start(bf16[128,512]{1,0:T(8,128)(2,1)S(1)} %shard_map.92.half_ref.refs_0_), channel_id=1, source_target_pairs={{0,1},{1,0},{2,3},{3,2},{4,5},{5,4},{6,7},{7,6},{8,9},{9,8},{10,11... | collective-permute-start | bytes 393224 | tf_op jit(solution)/shard_map/ppermute | solution.py:64
  59.5 6.6 %collective-permute-start.21 = (bf16[128,512]{1,0:T(8,128)(2,1)S(1)}, bf16[128,512]{1,0:T(8,128)(2,1)S(1)}, u32[]{:S(2)}, u32[]{:S(2)}) collective-permute-start(bf16[128,512]{1,0:T(8,128)(2,1)S(1)} %collective-permute-done.17.refs_3_), channel_id=1, source_target_pairs={{0,1},{1,0},{2,3},{3,2},{4,5},{5,4},{6,7},{7,6},{8,9},{9,8},{10,11... | collective-permute-start | bytes 393224 | tf_op jit(solution)/shard_map/ppermute | solution.py:64
  64.7 2.4 %collective-permute-start.20 = (bf16[128,512]{1,0:T(8,128)(2,1)S(1)}, bf16[128,512]{1,0:T(8,128)(2,1)S(1)}, u32[]{:S(2)}, u32[]{:S(2)}) collective-permute-start(bf16[128,512]{1,0:T(8,128)(2,1)S(1)} %collective-permute-done.16.refs_2_), channel_id=1, source_target_pairs={{0,1},{1,0},{2,3},{3,2},{4,5},{5,4},{6,7},{7,6},{8,9},{9,8},{10,11... | collective-permute-start | bytes 393224 | tf_op jit(solution)/shard_map/ppermute | solution.py:64
  66.1 1.3 %collective-permute-start.19 = (bf16[128,512]{1,0:T(8,128)(2,1)S(1)}, bf16[128,512]{1,0:T(8,128)(2,1)S(1)}, u32[]{:S(2)}, u32[]{:S(2)}) collective-permute-start(bf16[128,512]{1,0:T(8,128)(2,1)S(1)} %collective-permute-done.15.refs_1_), channel_id=1, source_target_pairs={{0,1},{1,0},{2,3},{3,2},{4,5},{5,4},{6,7},{7,6},{8,9},{9,8},{10,11... | collective-permute-start | bytes 393224 | tf_op jit(solution)/shard_map/ppermute | solution.py:64
  67.4 25.5 %slice-start.1 = ((s8[6291456]{0:T(1024)(128)(4,1)}), s8[2097152]{0:T(1024)(128)(4,1)S(1)}, s32[]{:S(2)}) async-start(s8[6291456]{0:T(1024)(128)(4,1)} %bitcast.7), calls=%async_computation.1 | async-start | bytes 4194304
  68.4 7.3 %collective-permute-start.31 = (bf16[384,256]{1,0:T(8,128)(2,1)S(1)}, bf16[384,256]{1,0:T(8,128)(2,1)S(1)}, u32[]{:S(2)}, u32[]{:S(2)}) collective-permute-start(bf16[384,256]{1,0:T(8,128)(2,1)S(1)} %shard_map.94.a_ref), channel_id=1, source_target_pairs={{0,24},{8,16},{16,8},{24,0},{1,25},{9,17},{17,9},{25,1},{2,26},{10... | collective-permute-start | bytes 589832 | tf_op jit(solution)/shard_map/ppermute | solution.py:64
  70.6 9.8 %collective-permute-start.30 = (bf16[384,256]{1,0:T(8,128)(2,1)S(1)}, bf16[384,256]{1,0:T(8,128)(2,1)S(1)}, u32[]{:S(2)}, u32[]{:S(2)}) collective-permute-start(bf16[384,256]{1,0:T(8,128)(2,1)S(1)} %shard_map.94.a_ref), channel_id=1, source_target_pairs={{0,16},{8,24},{16,0},{24,8},{1,17},{9,25},{17,1},{25,9},{2,18},{10... | collective-permute-start | bytes 589832 | tf_op jit(solution)/shard_map/ppermute | solution.py:64
  70.9 10.2 %collective-permute-start.29 = (bf16[384,256]{1,0:T(8,128)(2,1)S(1)}, bf16[384,256]{1,0:T(8,128)(2,1)S(1)}, u32[]{:S(2)}, u32[]{:S(2)}) collective-permute-start(bf16[384,256]{1,0:T(8,128)(2,1)S(1)} %shard_map.94.a_ref), channel_id=1, source_target_pairs={{0,8},{8,0},{16,24},{24,16},{1,9},{9,1},{17,25},{25,17},{2,10},{10... | collective-permute-start | bytes 589832 | tf_op jit(solution)/shard_map/ppermute | solution.py:64
  72.1 10.9 %collective-permute-start.24 = (bf16[128,512]{1,0:T(8,128)(2,1)S(1)}, bf16[128,512]{1,0:T(8,128)(2,1)S(1)}, u32[]{:S(2)}, u32[]{:S(2)}) collective-permute-start(bf16[128,512]{1,0:T(8,128)(2,1)S(1)} %shard_map.93), channel_id=1, source_target_pairs={{0,6},{1,7},{2,4},{3,5},{4,2},{5,3},{6,0},{7,1},{8,14},{9,15},{10,... | collective-permute-start | bytes 393224 | tf_op jit(solution)/shard_map/ppermute | solution.py:64
  74.5 10.7 %collective-permute-start.23 = (bf16[128,512]{1,0:T(8,128)(2,1)S(1)}, bf16[128,512]{1,0:T(8,128)(2,1)S(1)}, u32[]{:S(2)}, u32[]{:S(2)}) collective-permute-start(bf16[128,512]{1,0:T(8,128)(2,1)S(1)} %shard_map.93), channel_id=1, source_target_pairs={{0,4},{1,5},{2,6},{3,7},{4,0},{5,1},{6,2},{7,3},{8,12},{9,13},{10,... | collective-permute-start | bytes 393224 | tf_op jit(solution)/shard_map/ppermute | solution.py:64
  75.7 9.5 %collective-permute-start.22 = (bf16[128,512]{1,0:T(8,128)(2,1)S(1)}, bf16[128,512]{1,0:T(8,128)(2,1)S(1)}, u32[]{:S(2)}, u32[]{:S(2)}) collective-permute-start(bf16[128,512]{1,0:T(8,128)(2,1)S(1)} %shard_map.93), channel_id=1, source_target_pairs={{0,2},{1,3},{2,0},{3,1},{4,6},{5,7},{6,4},{7,5},{8,10},{9,11},{10,... | collective-permute-start | bytes 393224 | tf_op jit(solution)/shard_map/ppermute | solution.py:64
  80.4 12.5 %collective-permute-start.28 = (bf16[4,128,512]{2,1,0:T(8,128)(2,1)S(1)}, bf16[4,128,512]{2,1,0:T(8,128)(2,1)S(1)}, u32[]{:S(2)}, u32[]{:S(2)}) collective-permute-start(bf16[4,128,512]{2,1,0:T(8,128)(2,1)S(1)} %get-tuple-element.75.refs_0_), channel_id=1, source_target_pairs={{0,1},{1,0},{2,3},{3,2},{4,5},{5,4},{6,7},{7,6},{8,9},{9,8},{10,11... | collective-permute-start | bytes 1572872 | tf_op jit(solution)/shard_map/ppermute | solution.py:64
  82.8 5.1 %collective-permute-start.32 = (f32[384,128]{1,0:T(8,128)S(1)}, f32[384,128]{1,0:T(8,128)S(1)}, u32[]{:S(2)}, u32[]{:S(2)}) collective-permute-start(f32[384,128]{1,0:T(8,128)S(1)} %get-tuple-element.77), channel_id=1, source_target_pairs={{0,1},{1,0},{2,3},{3,2},{4,5},{5,4},{6,7},{7,6},{8,9},{9,8},{10,11... | collective-permute-start | bytes 589832 | tf_op jit(solution)/shard_map/ppermute | solution.py:64
  85.3 12.8 %collective-permute-start.27 = (bf16[3,128,512]{2,1,0:T(8,128)(2,1)S(1)}, bf16[3,128,512]{2,1,0:T(8,128)(2,1)S(1)}, u32[]{:S(2)}, u32[]{:S(2)}) collective-permute-start(bf16[3,128,512]{2,1,0:T(8,128)(2,1)S(1)} %pad_maximum_fusion.1.refs_0_), channel_id=1, source_target_pairs={{0,24},{8,16},{16,8},{24,0},{1,25},{9,17},{17,9},{25,1},{2,26},{10... | collective-permute-start | bytes 1179656 | tf_op jit(solution)/shard_map/ppermute | solution.py:64
  87.5 18.2 %collective-permute-start.26 = (bf16[3,128,512]{2,1,0:T(8,128)(2,1)S(1)}, bf16[3,128,512]{2,1,0:T(8,128)(2,1)S(1)}, u32[]{:S(2)}, u32[]{:S(2)}) collective-permute-start(bf16[3,128,512]{2,1,0:T(8,128)(2,1)S(1)} %pad_maximum_fusion.1.refs_0_), channel_id=1, source_target_pairs={{0,16},{8,24},{16,0},{24,8},{1,17},{9,25},{17,1},{25,9},{2,18},{10... | collective-permute-start | bytes 1179656 | tf_op jit(solution)/shard_map/ppermute | solution.py:64
  87.7 18.0 %collective-permute-start.25 = (bf16[3,128,512]{2,1,0:T(8,128)(2,1)S(1)}, bf16[3,128,512]{2,1,0:T(8,128)(2,1)S(1)}, u32[]{:S(2)}, u32[]{:S(2)}) collective-permute-start(bf16[3,128,512]{2,1,0:T(8,128)(2,1)S(1)} %pad_maximum_fusion.1.refs_0_), channel_id=1, source_target_pairs={{0,8},{8,0},{16,24},{24,16},{1,9},{9,1},{17,25},{25,17},{2,10},{10... | collective-permute-start | bytes 1179656 | tf_op jit(solution)/shard_map/ppermute | solution.py:64
  88.0 3.8 %collective-permute-start.33 = (bf16[384,128]{1,0:T(8,128)(2,1)S(1)}, bf16[384,128]{1,0:T(8,128)(2,1)S(1)}, u32[]{:S(2)}, u32[]{:S(2)}) collective-permute-start(bf16[384,128]{1,0:T(8,128)(2,1)S(1)} %get-tuple-element.79), channel_id=1, source_target_pairs={{0,2},{1,3},{2,0},{3,1},{4,6},{5,7},{6,4},{7,5},{8,10},{9,11},{10,... | collective-permute-start | bytes 294920 | tf_op jit(solution)/shard_map/ppermute | solution.py:64
  91.9 5.6 %collective-permute-start.34 = (bf16[384,128]{1,0:T(8,128)(2,1)S(1)}, bf16[384,128]{1,0:T(8,128)(2,1)S(1)}, u32[]{:S(2)}, u32[]{:S(2)}) collective-permute-start(bf16[384,128]{1,0:T(8,128)(2,1)S(1)} %get-tuple-element.81), channel_id=1, source_target_pairs={{0,4},{1,5},{2,6},{3,7},{4,0},{5,1},{6,2},{7,3},{8,12},{9,13},{10,... | collective-permute-start | bytes 294920 | tf_op jit(solution)/shard_map/ppermute | solution.py:64
  105.7 7.4 %collective-permute-start.35 = (bf16[3,128,512]{2,1,0:T(8,128)(2,1)S(1)}, bf16[3,128,512]{2,1,0:T(8,128)(2,1)S(1)}, u32[]{:S(2)}, u32[]{:S(2)}) collective-permute-start(bf16[3,128,512]{2,1,0:T(8,128)(2,1)S(1)} %pad_maximum_fusion.1.refs_0_), channel_id=1, source_target_pairs={{0,1},{1,0},{2,3},{3,2},{4,5},{5,4},{6,7},{7,6},{8,9},{9,8},{10,11... | collective-permute-start | bytes 1179656 | tf_op jit(solution)/shard_map/ppermute | solution.py:64
  106.3 6.9 %collective-permute-start.36 = (bf16[3,128,512]{2,1,0:T(8,128)(2,1)S(1)}, bf16[3,128,512]{2,1,0:T(8,128)(2,1)S(1)}, u32[]{:S(2)}, u32[]{:S(2)}) collective-permute-start(bf16[3,128,512]{2,1,0:T(8,128)(2,1)S(1)} %collective-permute-done.25.refs_1_), channel_id=1, source_target_pairs={{0,1},{1,0},{2,3},{3,2},{4,5},{5,4},{6,7},{7,6},{8,9},{9,8},{10,11... | collective-permute-start | bytes 1179656 | tf_op jit(solution)/shard_map/ppermute | solution.py:64
  106.3 6.9 %collective-permute-start.37 = (bf16[3,128,512]{2,1,0:T(8,128)(2,1)S(1)}, bf16[3,128,512]{2,1,0:T(8,128)(2,1)S(1)}, u32[]{:S(2)}, u32[]{:S(2)}) collective-permute-start(bf16[3,128,512]{2,1,0:T(8,128)(2,1)S(1)} %collective-permute-done.26.refs_2_), channel_id=1, source_target_pairs={{0,1},{1,0},{2,3},{3,2},{4,5},{5,4},{6,7},{7,6},{8,9},{9,8},{10,11... | collective-permute-start | bytes 1179656 | tf_op jit(solution)/shard_map/ppermute | solution.py:64
  106.8 6.4 %collective-permute-start.38 = (bf16[3,128,512]{2,1,0:T(8,128)(2,1)S(1)}, bf16[3,128,512]{2,1,0:T(8,128)(2,1)S(1)}, u32[]{:S(2)}, u32[]{:S(2)}) collective-permute-start(bf16[3,128,512]{2,1,0:T(8,128)(2,1)S(1)} %collective-permute-done.27.refs_3_), channel_id=1, source_target_pairs={{0,1},{1,0},{2,3},{3,2},{4,5},{5,4},{6,7},{7,6},{8,9},{9,8},{10,11... | collective-permute-start | bytes 1179656 | tf_op jit(solution)/shard_map/ppermute | solution.py:64
  106.8 3.8 %collective-permute-start.39 = (f32[384,128]{1,0:T(8,128)S(1)}, f32[384,128]{1,0:T(8,128)S(1)}, u32[]{:S(2)}, u32[]{:S(2)}) collective-permute-start(f32[384,128]{1,0:T(8,128)S(1)} %get-tuple-element.82.own_ref), channel_id=1, source_target_pairs={{0,1},{1,0},{2,3},{3,2},{4,5},{5,4},{6,7},{7,6},{8,9},{9,8},{10,11... | collective-permute-start | bytes 589832 | tf_op jit(solution)/shard_map/ppermute | solution.py:64

commit v5 on v4

--- a/solution.py
+++ b/solution.py
@@ -404,6 +404,7 @@
 
     new_one, new_two, local = moments(place, gathered, moment_one, moment_two)
 
+    halves[3] = after(halves[3], mine)
     halves += [far_half] + [core(h) for h in halves[1:]]
     halves[0] = after(halves[0], gathered[3])
     part = span(gradient_high, gradient_low, halves)

time: 117 us -> 116 us (level)
  no operation moved by 1% of the time
where the time goes in v5:
time: 116 us; the launch traced here: 115 us
  waiting for transfers between devices  47.4 us (41%)
  starting transfers between devices  38.5 us (33%)
  Pallas kernels  27.4 us (24%)
    ppermute x40, waiting for transfers between devices, swap(): return lax.ppermute(x, axis, [(i, i ^ bit) for i in range(size)])  47.4 us
    ppermute x40, starting transfers between devices, swap(): return lax.ppermute(x, axis, [(i, i ^ bit) for i in range(size)])  38.5 us
    pallas_call x3, Pallas kernels, update(): pl.pallas_call(body, grid_spec=pltpu.PrefetchScalarGridSpec(num_scalar_pr...  9.09 us
    pallas_call x2, Pallas kernels, pack(): pl.pallas_call(body, grid_spec=pltpu.PrefetchScalarGridSpec(num_scalar_pr...  6.59 us
    pallas_call x13, Pallas kernels, call(): pl.pallas_call(body, in_specs=[SMEM] * len(scalars) + [VMEM] * len(args),...  5.63 us
    pallas_call x1, Pallas kernels, moments(): pl.pallas_call(body, in_specs=[SMEM] + [VMEM] * 6, out_specs=(VMEM,) * 3,...  3.54 us
    pallas_call x1, Pallas kernels, polish(): pl.pallas_call(body, in_specs=[SMEM] + [VMEM] * 3, out_specs=VMEM, out_sh...  2.5 us
  transfers between devices with their start and end apart: 40, of which 21 were waited for; matrix products, arithmetic and copies ran while one was open for 1% of the time, Pallas kernels for 17%

profile of v5, /device:TPU:1, one launch (start us, length us, event | category | flops | bytes accessed | tf_op | source)
XLA Modules:
  0.0 115.5 jit_solution(7730391177028125345)
XLA Ops:
  0.7 3.3 %shard_map.84 = (bf16[2,2,384,128]{3,2,1,0:T(8,128)(2,1)S(1)}, bf16[2,2,384,128]{3,2,1,0:T(8,128)(2,1)S(1)}, bf16[2,2,384,128]{3,2,1,0:T(8,128)(2,1)S(1)}, bf16[2,2,384,128]{3,2,1,0:T(8,128)(2,1)S(1)}) custom-call(s32[3]{0:T(128)S(1)} %pad_add_fusion.place_ref, bf16[192,2,4096]{2,1,0:T(2,128)(2,1)} %bitcast.9), custom_call_target="tpu_custom_call" | custom-call | bytes 11550000 | tf_op jit(solution)/shard_map/pallas_call | solution.py:118
  4.0 2.1 %collective-permute-start = (bf16[2,2,384,128]{3,2,1,0:T(8,128)(2,1)S(1)}, bf16[2,2,384,128]{3,2,1,0:T(8,128)(2,1)S(1)}, u32[]{:S(2)}, u32[]{:S(2)}) collective-permute-start(bf16[2,2,384,128]{3,2,1,0:T(8,128)(2,1)S(1)} %get-tuple-element.48), channel_id=1, source_target_pairs={{0,8},{8,0},{16,24},{24,16},{1,9},{9,1},{17,25},{25,17},{2,10},{10... | collective-permute-start | bytes 1179656 | tf_op jit(solution)/shard_map/ppermute | solution.py:64
  6.1 1.2 %collective-permute-start.1 = (bf16[2,2,384,128]{3,2,1,0:T(8,128)(2,1)S(1)}, bf16[2,2,384,128]{3,2,1,0:T(8,128)(2,1)S(1)}, u32[]{:S(2)}, u32[]{:S(2)}) collective-permute-start(bf16[2,2,384,128]{3,2,1,0:T(8,128)(2,1)S(1)} %get-tuple-element.49), channel_id=1, source_target_pairs={{0,16},{8,24},{16,0},{24,8},{1,17},{9,25},{17,1},{25,9},{2,18},{10... | collective-permute-start | bytes 1179656 | tf_op jit(solution)/shard_map/ppermute | solution.py:64
  7.4 1.0 reshape.11
  8.4 3.3 %shard_map.85 = (bf16[2,2,384,128]{3,2,1,0:T(8,128)(2,1)S(1)}, bf16[2,2,384,128]{3,2,1,0:T(8,128)(2,1)S(1)}, bf16[2,2,384,128]{3,2,1,0:T(8,128)(2,1)S(1)}, bf16[2,2,384,128]{3,2,1,0:T(8,128)(2,1)S(1)}) custom-call(s32[3]{0:T(128)S(1)} %pad_add_fusion.place_ref, bf16[192,2,4096]{2,1,0:T(2,128)(2,1)} %bitcast.10), custom_call_target="tpu_custom_call" | custom-call | bytes 11550000 | tf_op jit(solution)/shard_map/pallas_call | solution.py:118
  11.7 3.2 %collective-permute-done.came_x_ref.refs_1_ = bf16[2,2,384,128]{3,2,1,0:T(8,128)(2,1)S(1)} collective-permute-done((bf16[2,2,384,128]{3,2,1,0:T(8,128)(2,1)S(1)}, bf16[2,2,384,128]{3,2,1,0:T(8,128)(2,1)S(1)}, u32[]{:S(2)}, u32[]{:S(2)}) %collective-permute-start) | collective-permute-done | bytes 393248 | tf_op jit(solution)/shard_map/ppermute | solution.py:64
  15.0 0.8 collective-permute-done.1.came_y_ref.refs_4_
  15.9 1.3 %collective-permute-start.6 = (bf16[2,384,128]{2,1,0:T(8,128)(2,1)S(1)}, bf16[2,384,128]{2,1,0:T(8,128)(2,1)S(1)}, u32[]{:S(2)}, u32[]{:S(2)}) collective-permute-start(bf16[2,384,128]{2,1,0:T(8,128)(2,1)S(1)} %get-tuple-element.64), channel_id=1, source_target_pairs={{0,16},{8,24},{16,0},{24,8},{1,17},{9,25},{17,1},{25,9},{2,18},{10... | collective-permute-start | bytes 589832 | tf_op jit(solution)/shard_map/ppermute | solution.py:64
  17.7 1.2 %collective-permute-start.2 = (bf16[2,2,384,128]{3,2,1,0:T(8,128)(2,1)S(1)}, bf16[2,2,384,128]{3,2,1,0:T(8,128)(2,1)S(1)}, u32[]{:S(2)}, u32[]{:S(2)}) collective-permute-start(bf16[2,2,384,128]{3,2,1,0:T(8,128)(2,1)S(1)} %get-tuple-element.56), channel_id=1, source_target_pairs={{0,8},{8,0},{16,24},{24,16},{1,9},{9,1},{17,25},{25,17},{2,10},{10... | collective-permute-start | bytes 1179656 | tf_op jit(solution)/shard_map/ppermute | solution.py:64
  19.2 1.3 %collective-permute-done.6.refs_2_ = bf16[2,384,128]{2,1,0:T(8,128)(2,1)S(1)} collective-permute-done((bf16[2,384,128]{2,1,0:T(8,128)(2,1)S(1)}, bf16[2,384,128]{2,1,0:T(8,128)(2,1)S(1)}, u32[]{:S(2)}, u32[]{:S(2)}) %collective-permute-start.6) | collective-permute-done | bytes 196640 | tf_op jit(solution)/shard_map/ppermute | solution.py:64
  20.5 1.5 %collective-permute-done.7.refs_5_ = bf16[2,384,128]{2,1,0:T(8,128)(2,1)S(1)} collective-permute-done((bf16[2,384,128]{2,1,0:T(8,128)(2,1)S(1)}, bf16[2,384,128]{2,1,0:T(8,128)(2,1)S(1)}, u32[]{:S(2)}, u32[]{:S(2)}) %collective-permute-start.7) | collective-permute-done | bytes 196640 | tf_op jit(solution)/shard_map/ppermute | solution.py:64
  22.5 5.2 %collective-permute-start.8 = (bf16[2,128,512]{2,1,0:T(8,128)(2,1)S(1)}, bf16[2,128,512]{2,1,0:T(8,128)(2,1)S(1)}, u32[]{:S(2)}, u32[]{:S(2)}) collective-permute-start(bf16[2,128,512]{2,1,0:T(8,128)(2,1)S(1)} %get-tuple-element.67), channel_id=1, source_target_pairs={{0,1},{1,0},{2,3},{3,2},{4,5},{5,4},{6,7},{7,6},{8,9},{9,8},{10,11... | collective-permute-start | bytes 786440 | tf_op jit(solution)/shard_map/ppermute | solution.py:64
  27.7 1.2 %collective-permute-done.8.came_ref = bf16[2,128,512]{2,1,0:T(8,128)(2,1)S(1)} collective-permute-done((bf16[2,128,512]{2,1,0:T(8,128)(2,1)S(1)}, bf16[2,128,512]{2,1,0:T(8,128)(2,1)S(1)}, u32[]{:S(2)}, u32[]{:S(2)}) %collective-permute-start.8) | collective-permute-done | bytes 262176 | tf_op jit(solution)/shard_map/ppermute | solution.py:64
  28.9 2.4 %collective-permute-start.9 = (bf16[2,128,512]{2,1,0:T(8,128)(2,1)S(1)}, bf16[2,128,512]{2,1,0:T(8,128)(2,1)S(1)}, u32[]{:S(2)}, u32[]{:S(2)}) collective-permute-start(bf16[2,128,512]{2,1,0:T(8,128)(2,1)S(1)} %shard_map.90), channel_id=1, source_target_pairs={{0,4},{1,5},{2,6},{3,7},{4,0},{5,1},{6,2},{7,3},{8,12},{9,13},{10,... | collective-permute-start | bytes 786440 | tf_op jit(solution)/shard_map/ppermute | solution.py:64
  32.0 4.3 %collective-permute-done.4.refs_2_ = bf16[2,384,128]{2,1,0:T(8,128)(2,1)S(1)} collective-permute-done((bf16[2,384,128]{2,1,0:T(8,128)(2,1)S(1)}, bf16[2,384,128]{2,1,0:T(8,128)(2,1)S(1)}, u32[]{:S(2)}, u32[]{:S(2)}) %collective-permute-start.4) | collective-permute-done | bytes 196640 | tf_op jit(solution)/shard_map/ppermute | solution.py:64
  37.0 6.0 %collective-permute-done.9.chips_ref = bf16[2,128,512]{2,1,0:T(8,128)(2,1)S(1)} collective-permute-done((bf16[2,128,512]{2,1,0:T(8,128)(2,1)S(1)}, bf16[2,128,512]{2,1,0:T(8,128)(2,1)S(1)}, u32[]{:S(2)}, u32[]{:S(2)}) %collective-permute-start.9) | collective-permute-done | bytes 262176 | tf_op jit(solution)/shard_map/ppermute | solution.py:64
  43.0 1.2 %collective-permute-start.10 = (bf16[2,128,512]{2,1,0:T(8,128)(2,1)S(1)}, bf16[2,128,512]{2,1,0:T(8,128)(2,1)S(1)}, u32[]{:S(2)}, u32[]{:S(2)}) collective-permute-start(bf16[2,128,512]{2,1,0:T(8,128)(2,1)S(1)} %get-tuple-element.68), channel_id=1, source_target_pairs={{0,1},{1,0},{2,3},{3,2},{4,5},{5,4},{6,7},{7,6},{8,9},{9,8},{10,11... | collective-permute-start | bytes 786440 | tf_op jit(solution)/shard_map/ppermute | solution.py:64
  44.2 1.2 %collective-permute-done.10.came_ref = bf16[2,128,512]{2,1,0:T(8,128)(2,1)S(1)} collective-permute-done((bf16[2,128,512]{2,1,0:T(8,128)(2,1)S(1)}, bf16[2,128,512]{2,1,0:T(8,128)(2,1)S(1)}, u32[]{:S(2)}, u32[]{:S(2)}) %collective-permute-start.10) | collective-permute-done | bytes 262176 | tf_op jit(solution)/shard_map/ppermute | solution.py:64
  45.9 4.3 %collective-permute-done.11.came_ref = bf16[128,512]{1,0:T(8,128)(2,1)S(1)} collective-permute-done((bf16[128,512]{1,0:T(8,128)(2,1)S(1)}, bf16[128,512]{1,0:T(8,128)(2,1)S(1)}, u32[]{:S(2)}, u32[]{:S(2)}) %collective-permute-start.11) | collective-permute-done | bytes 131104 | tf_op jit(solution)/shard_map/ppermute | solution.py:64
  50.8 3.3 %collective-permute-start.17 = (bf16[128,512]{1,0:T(8,128)(2,1)S(1)}, bf16[128,512]{1,0:T(8,128)(2,1)S(1)}, u32[]{:S(2)}, u32[]{:S(2)}) collective-permute-start(bf16[128,512]{1,0:T(8,128)(2,1)S(1)} %shard_map.92.half_ref.refs_0_), channel_id=1, source_target_pairs={{0,6},{1,7},{2,4},{3,5},{4,2},{5,3},{6,0},{7,1},{8,14},{9,15},{10,... | collective-permute-start | bytes 393224 | tf_op jit(solution)/shard_map/ppermute | solution.py:64
  54.8 1.8 %collective-permute-start.12 = (bf16[128,512]{1,0:T(8,128)(2,1)S(1)}, bf16[128,512]{1,0:T(8,128)(2,1)S(1)}, u32[]{:S(2)}, u32[]{:S(2)}) collective-permute-start(bf16[128,512]{1,0:T(8,128)(2,1)S(1)} %shard_map.92.half_ref.refs_0_), channel_id=1, source_target_pairs={{0,24},{8,16},{16,8},{24,0},{1,25},{9,17},{17,9},{25,1},{2,26},{10... | collective-permute-start | bytes 393224 | tf_op jit(solution)/shard_map/ppermute | solution.py:64
  56.6 0.9 shard_map.93
  57.5 2.9 %collective-permute-start.18 = (bf16[128,512]{1,0:T(8,128)(2,1)S(1)}, bf16[128,512]{1,0:T(8,128)(2,1)S(1)}, u32[]{:S(2)}, u32[]{:S(2)}) collective-permute-start(bf16[128,512]{1,0:T(8,128)(2,1)S(1)} %shard_map.92.half_ref.refs_0_), channel_id=1, source_target_pairs={{0,1},{1,0},{2,3},{3,2},{4,5},{5,4},{6,7},{7,6},{8,9},{9,8},{10,11... | collective-permute-start | bytes 393224 | tf_op jit(solution)/shard_map/ppermute | solution.py:64
  60.5 4.1 %collective-permute-done.16.refs_2_ = bf16[128,512]{1,0:T(8,128)(2,1)S(1)} collective-permute-done((bf16[128,512]{1,0:T(8,128)(2,1)S(1)}, bf16[128,512]{1,0:T(8,128)(2,1)S(1)}, u32[]{:S(2)}, u32[]{:S(2)}) %collective-permute-start.16) | collective-permute-done | bytes 131104 | tf_op jit(solution)/shard_map/ppermute | solution.py:64
  64.7 1.4 %collective-permute-start.20 = (bf16[128,512]{1,0:T(8,128)(2,1)S(1)}, bf16[128,512]{1,0:T(8,128)(2,1)S(1)}, u32[]{:S(2)}, u32[]{:S(2)}) collective-permute-start(bf16[128,512]{1,0:T(8,128)(2,1)S(1)} %collective-permute-done.16.refs_2_), channel_id=1, source_target_pairs={{0,1},{1,0},{2,3},{3,2},{4,5},{5,4},{6,7},{7,6},{8,9},{9,8},{10,11... | collective-permute-start | bytes 393224 | tf_op jit(solution)/shard_map/ppermute | solution.py:64
  66.1 1.0 collective-permute-done.20.refs_6_
  67.4 1.0 shard_map.94.a_ref
  68.4 2.2 %collective-permute-start.31 = (bf16[384,256]{1,0:T(8,128)(2,1)S(1)}, bf16[384,256]{1,0:T(8,128)(2,1)S(1)}, u32[]{:S(2)}, u32[]{:S(2)}) collective-permute-start(bf16[384,256]{1,0:T(8,128)(2,1)S(1)} %shard_map.94.a_ref), channel_id=1, source_target_pairs={{0,24},{8,16},{16,8},{24,0},{1,25},{9,17},{17,9},{25,1},{2,26},{10... | collective-permute-start | bytes 589832 | tf_op jit(solution)/shard_map/ppermute | solution.py:64
  71.1 2.4 %collective-permute-start.24 = (bf16[128,512]{1,0:T(8,128)(2,1)S(1)}, bf16[128,512]{1,0:T(8,128)(2,1)S(1)}, u32[]{:S(2)}, u32[]{:S(2)}) collective-permute-start(bf16[128,512]{1,0:T(8,128)(2,1)S(1)} %shard_map.93), channel_id=1, source_target_pairs={{0,6},{1,7},{2,4},{3,5},{4,2},{5,3},{6,0},{7,1},{8,14},{9,15},{10,... | collective-permute-start | bytes 393224 | tf_op jit(solution)/shard_map/ppermute | solution.py:64
  73.5 2.3 %collective-permute-done.31.d_ref = bf16[384,256]{1,0:T(8,128)(2,1)S(1)} collective-permute-done((bf16[384,256]{1,0:T(8,128)(2,1)S(1)}, bf16[384,256]{1,0:T(8,128)(2,1)S(1)}, u32[]{:S(2)}, u32[]{:S(2)}) %collective-permute-start.31) | collective-permute-done | bytes 196640 | tf_op jit(solution)/shard_map/ppermute | solution.py:64
  75.7 3.5 %shard_map.95 = (f32[512,2,256]{2,1,0:T(2,128)}, f32[512,2,256]{2,1,0:T(2,128)}, bf16[4,128,512]{2,1,0:T(8,128)(2,1)S(1)}) custom-call(s32[3]{0:T(128)S(1)} %pad_add_fusion.place_ref, bf16[128,512]{1,0:T(8,128)(2,1)S(1)} %shard_map.92.half_ref.refs_0_, bf16[128,512]{1,0:T(8,128)(2,1)S(1)} %collective-permute-done.13.refs_1_, ...), custom_call_target="tpu_custom_call" | custom-call | bytes 12250000 | tf_op jit(solution)/shard_map/pallas_call | solution.py:217
  79.3 1.1 collective-permute-done.30.c_ref
  80.4 0.5 collective-permute-start.28
  80.9 1.8 %shard_map.97 = (f32[384,256]{1,0:T(8,128)S(1)}, f32[384,128]{1,0:T(8,128)S(1)}, f32[384,128]{1,0:T(8,128)S(1)}) custom-call(s32[3]{0:T(128)S(1)} %pad_add_fusion.place_ref, bf16[384,256]{1,0:T(8,128)(2,1)S(1)} %shard_map.94.a_ref, bf16[384,256]{1,0:T(8,128)(2,1)S(1)} %collective-permute-done.29.b_ref, bf16[384,256]{1,0:T(8,128)(2,1)S(1)} %collective-permute-done.30.c_ref, ...), custom_call_target="tpu_custom_call" | custom-call | bytes 6300000 | tf_op jit(solution)/shard_map/pallas_call | solution.py:83
  82.8 1.4 %collective-permute-done.23 = bf16[128,512]{1,0:T(8,128)(2,1)S(1)} collective-permute-done((bf16[128,512]{1,0:T(8,128)(2,1)S(1)}, bf16[128,512]{1,0:T(8,128)(2,1)S(1)}, u32[]{:S(2)}, u32[]{:S(2)}) %collective-permute-start.23) | collective-permute-done | bytes 131104 | tf_op jit(solution)/shard_map/ppermute | solution.py:64
  84.3 2.2 %collective-permute-start.27 = (bf16[3,128,512]{2,1,0:T(8,128)(2,1)S(1)}, bf16[3,128,512]{2,1,0:T(8,128)(2,1)S(1)}, u32[]{:S(2)}, u32[]{:S(2)}) collective-permute-start(bf16[3,128,512]{2,1,0:T(8,128)(2,1)S(1)} %pad_maximum_fusion.1.refs_0_), channel_id=1, source_target_pairs={{0,24},{8,16},{16,8},{24,0},{1,25},{9,17},{17,9},{25,1},{2,26},{10... | collective-permute-start | bytes 1179656 | tf_op jit(solution)/shard_map/ppermute | solution.py:64
  87.3 3.5 %collective-permute-done.33.came_ref = bf16[384,128]{1,0:T(8,128)(2,1)S(1)} collective-permute-done((bf16[384,128]{1,0:T(8,128)(2,1)S(1)}, bf16[384,128]{1,0:T(8,128)(2,1)S(1)}, u32[]{:S(2)}, u32[]{:S(2)}) %collective-permute-start.33) | collective-permute-done | bytes 98336 | tf_op jit(solution)/shard_map/ppermute | solution.py:64
  90.9 1.5 %collective-permute-start.34 = (bf16[384,128]{1,0:T(8,128)(2,1)S(1)}, bf16[384,128]{1,0:T(8,128)(2,1)S(1)}, u32[]{:S(2)}, u32[]{:S(2)}) collective-permute-start(bf16[384,128]{1,0:T(8,128)(2,1)S(1)} %get-tuple-element.83), channel_id=1, source_target_pairs={{0,4},{1,5},{2,6},{3,7},{4,0},{5,1},{6,2},{7,3},{8,12},{9,13},{10,... | collective-permute-start | bytes 294920 | tf_op jit(solution)/shard_map/ppermute | solution.py:64
  92.4 2.4 %shard_map.96.refs_4_ = f32[192,2,4096]{2,1,0:T(2,128)} custom-call(s32[3]{0:T(128)S(1)} %pad_add_fusion.place_ref, f32[192,2,4096]{2,1,0:T(2,128)S(1)} %bitcast.8, bf16[384,512]{1,0:T(8,128)(2,1)S(1)} %pad_maximum_fusion.refs_6_.s_ref, bf16[4,128,512]{2,1,0:T(8,128)(2,1)S(1)} %get-tuple-element.77.refs_0_, ...), custom_call_target="tpu_custom_call" | custom-call | bytes 8750000 | tf_op jit(solution)/shard_map/pallas_call | solution.py:346
  94.8 1.8 %collective-permute-done.34.came_ref = bf16[384,128]{1,0:T(8,128)(2,1)S(1)} collective-permute-done((bf16[384,128]{1,0:T(8,128)(2,1)S(1)}, bf16[384,128]{1,0:T(8,128)(2,1)S(1)}, u32[]{:S(2)}, u32[]{:S(2)}) %collective-permute-start.34) | collective-permute-done | bytes 98336 | tf_op jit(solution)/shard_map/ppermute | solution.py:64
  96.6 0.7 shard_map.100
  97.3 7.4 %collective-permute-done.26.refs_2_ = bf16[3,128,512]{2,1,0:T(8,128)(2,1)S(1)} collective-permute-done((bf16[3,128,512]{2,1,0:T(8,128)(2,1)S(1)}, bf16[3,128,512]{2,1,0:T(8,128)(2,1)S(1)}, u32[]{:S(2)}, u32[]{:S(2)}) %collective-permute-start.26) | collective-permute-done | bytes 393248 | tf_op jit(solution)/shard_map/ppermute | solution.py:64
  104.7 0.6 collective-permute-start.35
  105.3 0.5 collective-permute-start.37
  105.8 0.5 collective-permute-start.39
  106.3 3.3 %shard_map.101.refs_4_ = f32[192,2,4096]{2,1,0:T(2,128)} custom-call(s32[3]{0:T(128)S(1)} %pad_add_fusion.place_ref, f32[192,2,4096]{2,1,0:T(2,128)S(1)} %bitcast.8, bf16[384,512]{1,0:T(8,128)(2,1)S(1)} %pad_maximum_fusion.refs_6_.s_ref, bf16[3,128,512]{2,1,0:T(8,128)(2,1)S(1)} %pad_maximum_fusion.1.refs_0_, ...), custom_call_target="tpu_custom_call", output_to_operand_aliasing={{}: (7, {})} | custom-call | bytes 12250000 | tf_op jit(solution)/shard_map/pallas_call | solution.py:346
  109.6 2.5 %shard_map.103 = bf16[192,2,256]{2,1,0:T(2,128)(2,1)} custom-call(s32[3]{0:T(128)S(1)} %pad_add_fusion.place_ref, f32[384,256]{1,0:T(8,128)S(1)} %get-tuple-element.91.spanned_ref, f32[384,128]{1,0:T(8,128)S(1)} %get-tuple-element.84.own_ref, f32[384,128]{1,0:T(8,128)S(1)} %collective-permute-done.39.other_ref), custom_call_target="tpu_custom_call" | custom-call | bytes 6300000 | tf_op jit(solution)/shard_map/pallas_call | solution.py:309
  112.1 3.3 %shard_map.102 = f32[192,2,4096]{2,1,0:T(2,128)} custom-call(s32[3]{0:T(128)S(1)} %pad_add_fusion.place_ref, f32[192,2,4096]{2,1,0:T(2,128)S(1)} %bitcast.8, bf16[384,512]{1,0:T(8,128)(2,1)S(1)} %pad_maximum_fusion.refs_6_.s_ref, bf16[3,128,512]{2,1,0:T(8,128)(2,1)S(1)} %collective-permute-done.35.refs_0_, ...), custom_call_target="tpu_custom_call", output_to_operand_aliasing={{}: (7, {})} | custom-call | bytes 12250000 | tf_op jit(solution)/shard_map/pallas_call | solution.py:346
  (68 shorter events, 6.7 us)
Async XLA Ops:
  4.0 10.9 %collective-permute-start = (bf16[2,2,384,128]{3,2,1,0:T(8,128)(2,1)S(1)}, bf16[2,2,384,128]{3,2,1,0:T(8,128)(2,1)S(1)}, u32[]{:S(2)}, u32[]{:S(2)}) collective-permute-start(bf16[2,2,384,128]{3,2,1,0:T(8,128)(2,1)S(1)} %get-tuple-element.48), channel_id=1, source_target_pairs={{0,8},{8,0},{16,24},{24,16},{1,9},{9,1},{17,25},{25,17},{2,10},{10... | collective-permute-start | bytes 1179656 | tf_op jit(solution)/shard_map/ppermute | solution.py:64
  6.1 9.7 %collective-permute-start.1 = (bf16[2,2,384,128]{3,2,1,0:T(8,128)(2,1)S(1)}, bf16[2,2,384,128]{3,2,1,0:T(8,128)(2,1)S(1)}, u32[]{:S(2)}, u32[]{:S(2)}) collective-permute-start(bf16[2,2,384,128]{3,2,1,0:T(8,128)(2,1)S(1)} %get-tuple-element.49), channel_id=1, source_target_pairs={{0,16},{8,24},{16,0},{24,8},{1,17},{9,25},{17,1},{25,9},{2,18},{10... | collective-permute-start | bytes 1179656 | tf_op jit(solution)/shard_map/ppermute | solution.py:64
  11.7 44.9 %copy-start = (f32[512,2,256]{2,1,0:T(2,128)S(1)}, f32[512,2,256]{2,1,0:T(2,128)}, u32[]{:S(2)}) copy-start(f32[512,2,256]{2,1,0:T(2,128)} %refs_4_.1) | copy-start | bytes 3145732
  11.7 44.9 %copy-start.1 = (f32[512,2,256]{2,1,0:T(2,128)S(1)}, f32[512,2,256]{2,1,0:T(2,128)}, u32[]{:S(2)}) copy-start(f32[512,2,256]{2,1,0:T(2,128)} %refs_5_.1) | copy-start | bytes 3145732
  15.9 4.6 %collective-permute-start.6 = (bf16[2,384,128]{2,1,0:T(8,128)(2,1)S(1)}, bf16[2,384,128]{2,1,0:T(8,128)(2,1)S(1)}, u32[]{:S(2)}, u32[]{:S(2)}) collective-permute-start(bf16[2,384,128]{2,1,0:T(8,128)(2,1)S(1)} %get-tuple-element.64), channel_id=1, source_target_pairs={{0,16},{8,24},{16,0},{24,8},{1,17},{9,25},{17,1},{25,9},{2,18},{10... | collective-permute-start | bytes 589832 | tf_op jit(solution)/shard_map/ppermute | solution.py:64
  17.2 4.8 %collective-permute-start.7 = (bf16[2,384,128]{2,1,0:T(8,128)(2,1)S(1)}, bf16[2,384,128]{2,1,0:T(8,128)(2,1)S(1)}, u32[]{:S(2)}, u32[]{:S(2)}) collective-permute-start(bf16[2,384,128]{2,1,0:T(8,128)(2,1)S(1)} %get-tuple-element.65), channel_id=1, source_target_pairs={{0,8},{8,0},{16,24},{24,16},{1,9},{9,1},{17,25},{25,17},{2,10},{10... | collective-permute-start | bytes 589832 | tf_op jit(solution)/shard_map/ppermute | solution.py:64
  17.7 13.6 %collective-permute-start.2 = (bf16[2,2,384,128]{3,2,1,0:T(8,128)(2,1)S(1)}, bf16[2,2,384,128]{3,2,1,0:T(8,128)(2,1)S(1)}, u32[]{:S(2)}, u32[]{:S(2)}) collective-permute-start(bf16[2,2,384,128]{3,2,1,0:T(8,128)(2,1)S(1)} %get-tuple-element.56), channel_id=1, source_target_pairs={{0,8},{8,0},{16,24},{24,16},{1,9},{9,1},{17,25},{25,17},{2,10},{10... | collective-permute-start | bytes 1179656 | tf_op jit(solution)/shard_map/ppermute | solution.py:64
  18.9 12.4 %collective-permute-start.3 = (bf16[2,2,384,128]{3,2,1,0:T(8,128)(2,1)S(1)}, bf16[2,2,384,128]{3,2,1,0:T(8,128)(2,1)S(1)}, u32[]{:S(2)}, u32[]{:S(2)}) collective-permute-start(bf16[2,2,384,128]{3,2,1,0:T(8,128)(2,1)S(1)} %get-tuple-element.58), channel_id=1, source_target_pairs={{0,16},{8,24},{16,0},{24,8},{1,17},{9,25},{17,1},{25,9},{2,18},{10... | collective-permute-start | bytes 1179656 | tf_op jit(solution)/shard_map/ppermute | solution.py:64
  22.5 6.4 %collective-permute-start.8 = (bf16[2,128,512]{2,1,0:T(8,128)(2,1)S(1)}, bf16[2,128,512]{2,1,0:T(8,128)(2,1)S(1)}, u32[]{:S(2)}, u32[]{:S(2)}) collective-permute-start(bf16[2,128,512]{2,1,0:T(8,128)(2,1)S(1)} %get-tuple-element.67), channel_id=1, source_target_pairs={{0,1},{1,0},{2,3},{3,2},{4,5},{5,4},{6,7},{7,6},{8,9},{9,8},{10,11... | collective-permute-start | bytes 786440 | tf_op jit(solution)/shard_map/ppermute | solution.py:64
  28.9 14.1 %collective-permute-start.9 = (bf16[2,128,512]{2,1,0:T(8,128)(2,1)S(1)}, bf16[2,128,512]{2,1,0:T(8,128)(2,1)S(1)}, u32[]{:S(2)}, u32[]{:S(2)}) collective-permute-start(bf16[2,128,512]{2,1,0:T(8,128)(2,1)S(1)} %shard_map.90), channel_id=1, source_target_pairs={{0,4},{1,5},{2,6},{3,7},{4,0},{5,1},{6,2},{7,3},{8,12},{9,13},{10,... | collective-permute-start | bytes 786440 | tf_op jit(solution)/shard_map/ppermute | solution.py:64
  31.3 61.1 %slice-start = ((s8[6291456]{0:T(1024)(128)(4,1)}), s8[4194304]{0:T(1024)(128)(4,1)S(1)}, s32[]{:S(2)}) async-start(s8[6291456]{0:T(1024)(128)(4,1)} %bitcast.7), calls=%async_computation | async-start | bytes 8388608
  31.4 4.9 %collective-permute-start.4 = (bf16[2,384,128]{2,1,0:T(8,128)(2,1)S(1)}, bf16[2,384,128]{2,1,0:T(8,128)(2,1)S(1)}, u32[]{:S(2)}, u32[]{:S(2)}) collective-permute-start(bf16[2,384,128]{2,1,0:T(8,128)(2,1)S(1)} %get-tuple-element.59), channel_id=1, source_target_pairs={{0,16},{8,24},{16,0},{24,8},{1,17},{9,25},{17,1},{25,9},{2,18},{10... | collective-permute-start | bytes 589832 | tf_op jit(solution)/shard_map/ppermute | solution.py:64
  31.7 4.8 %collective-permute-start.5 = (bf16[2,384,128]{2,1,0:T(8,128)(2,1)S(1)}, bf16[2,384,128]{2,1,0:T(8,128)(2,1)S(1)}, u32[]{:S(2)}, u32[]{:S(2)}) collective-permute-start(bf16[2,384,128]{2,1,0:T(8,128)(2,1)S(1)} %get-tuple-element.60), channel_id=1, source_target_pairs={{0,8},{8,0},{16,24},{24,16},{1,9},{9,1},{17,25},{25,17},{2,10},{10... | collective-permute-start | bytes 589832 | tf_op jit(solution)/shard_map/ppermute | solution.py:64
  43.0 2.4 %collective-permute-start.10 = (bf16[2,128,512]{2,1,0:T(8,128)(2,1)S(1)}, bf16[2,128,512]{2,1,0:T(8,128)(2,1)S(1)}, u32[]{:S(2)}, u32[]{:S(2)}) collective-permute-start(bf16[2,128,512]{2,1,0:T(8,128)(2,1)S(1)} %get-tuple-element.68), channel_id=1, source_target_pairs={{0,1},{1,0},{2,3},{3,2},{4,5},{5,4},{6,7},{7,6},{8,9},{9,8},{10,11... | collective-permute-start | bytes 786440 | tf_op jit(solution)/shard_map/ppermute | solution.py:64
  45.5 4.8 %collective-permute-start.11 = (bf16[128,512]{1,0:T(8,128)(2,1)S(1)}, bf16[128,512]{1,0:T(8,128)(2,1)S(1)}, u32[]{:S(2)}, u32[]{:S(2)}) collective-permute-start(bf16[128,512]{1,0:T(8,128)(2,1)S(1)} %get-tuple-element.70), channel_id=1, source_target_pairs={{0,2},{1,3},{2,0},{3,1},{4,6},{5,7},{6,4},{7,5},{8,10},{9,11},{10,... | collective-permute-start | bytes 393224 | tf_op jit(solution)/shard_map/ppermute | solution.py:64
  50.3 42.1 %slice-start.1 = ((s8[6291456]{0:T(1024)(128)(4,1)}), s8[2097152]{0:T(1024)(128)(4,1)S(1)}, s32[]{:S(2)}) async-start(s8[6291456]{0:T(1024)(128)(4,1)} %bitcast.7), calls=%async_computation.1 | async-start | bytes 4194304
  50.3 3.9 %collective-permute-start.14 = (bf16[128,512]{1,0:T(8,128)(2,1)S(1)}, bf16[128,512]{1,0:T(8,128)(2,1)S(1)}, u32[]{:S(2)}, u32[]{:S(2)}) collective-permute-start(bf16[128,512]{1,0:T(8,128)(2,1)S(1)} %shard_map.92.half_ref.refs_0_), channel_id=1, source_target_pairs={{0,16},{8,24},{16,0},{24,8},{1,17},{9,25},{17,1},{25,9},{2,18},{10... | collective-permute-start | bytes 393224 | tf_op jit(solution)/shard_map/ppermute | solution.py:64
  50.6 3.8 %collective-permute-start.13 = (bf16[128,512]{1,0:T(8,128)(2,1)S(1)}, bf16[128,512]{1,0:T(8,128)(2,1)S(1)}, u32[]{:S(2)}, u32[]{:S(2)}) collective-permute-start(bf16[128,512]{1,0:T(8,128)(2,1)S(1)} %shard_map.92.half_ref.refs_0_), channel_id=1, source_target_pairs={{0,8},{8,0},{16,24},{24,16},{1,9},{9,1},{17,25},{25,17},{2,10},{10... | collective-permute-start | bytes 393224 | tf_op jit(solution)/shard_map/ppermute | solution.py:64
  50.8 9.7 %collective-permute-start.17 = (bf16[128,512]{1,0:T(8,128)(2,1)S(1)}, bf16[128,512]{1,0:T(8,128)(2,1)S(1)}, u32[]{:S(2)}, u32[]{:S(2)}) collective-permute-start(bf16[128,512]{1,0:T(8,128)(2,1)S(1)} %shard_map.92.half_ref.refs_0_), channel_id=1, source_target_pairs={{0,6},{1,7},{2,4},{3,5},{4,2},{5,3},{6,0},{7,1},{8,14},{9,15},{10,... | collective-permute-start | bytes 393224 | tf_op jit(solution)/shard_map/ppermute | solution.py:64
  54.1 10.6 %collective-permute-start.16 = (bf16[128,512]{1,0:T(8,128)(2,1)S(1)}, bf16[128,512]{1,0:T(8,128)(2,1)S(1)}, u32[]{:S(2)}, u32[]{:S(2)}) collective-permute-start(bf16[128,512]{1,0:T(8,128)(2,1)S(1)} %shard_map.92.half_ref.refs_0_), channel_id=1, source_target_pairs={{0,4},{1,5},{2,6},{3,7},{4,0},{5,1},{6,2},{7,3},{8,12},{9,13},{10,... | collective-permute-start | bytes 393224 | tf_op jit(solution)/shard_map/ppermute | solution.py:64
  54.4 11.7 %collective-permute-start.15 = (bf16[128,512]{1,0:T(8,128)(2,1)S(1)}, bf16[128,512]{1,0:T(8,128)(2,1)S(1)}, u32[]{:S(2)}, u32[]{:S(2)}) collective-permute-start(bf16[128,512]{1,0:T(8,128)(2,1)S(1)} %shard_map.92.half_ref.refs_0_), channel_id=1, source_target_pairs={{0,2},{1,3},{2,0},{3,1},{4,6},{5,7},{6,4},{7,5},{8,10},{9,11},{10,... | collective-permute-start | bytes 393224 | tf_op jit(solution)/shard_map/ppermute | solution.py:64
  54.8 11.3 %collective-permute-start.12 = (bf16[128,512]{1,0:T(8,128)(2,1)S(1)}, bf16[128,512]{1,0:T(8,128)(2,1)S(1)}, u32[]{:S(2)}, u32[]{:S(2)}) collective-permute-start(bf16[128,512]{1,0:T(8,128)(2,1)S(1)} %shard_map.92.half_ref.refs_0_), channel_id=1, source_target_pairs={{0,24},{8,16},{16,8},{24,0},{1,25},{9,17},{17,9},{25,1},{2,26},{10... | collective-permute-start | bytes 393224 | tf_op jit(solution)/shard_map/ppermute | solution.py:64
  57.5 9.6 %collective-permute-start.18 = (bf16[128,512]{1,0:T(8,128)(2,1)S(1)}, bf16[128,512]{1,0:T(8,128)(2,1)S(1)}, u32[]{:S(2)}, u32[]{:S(2)}) collective-permute-start(bf16[128,512]{1,0:T(8,128)(2,1)S(1)} %shard_map.92.half_ref.refs_0_), channel_id=1, source_target_pairs={{0,1},{1,0},{2,3},{3,2},{4,5},{5,4},{6,7},{7,6},{8,9},{9,8},{10,11... | collective-permute-start | bytes 393224 | tf_op jit(solution)/shard_map/ppermute | solution.py:64
  60.5 5.6 %collective-permute-start.21 = (bf16[128,512]{1,0:T(8,128)(2,1)S(1)}, bf16[128,512]{1,0:T(8,128)(2,1)S(1)}, u32[]{:S(2)}, u32[]{:S(2)}) collective-permute-start(bf16[128,512]{1,0:T(8,128)(2,1)S(1)} %collective-permute-done.17.refs_3_), channel_id=1, source_target_pairs={{0,1},{1,0},{2,3},{3,2},{4,5},{5,4},{6,7},{7,6},{8,9},{9,8},{10,11... | collective-permute-start | bytes 393224 | tf_op jit(solution)/shard_map/ppermute | solution.py:64
  64.7 2.4 %collective-permute-start.20 = (bf16[128,512]{1,0:T(8,128)(2,1)S(1)}, bf16[128,512]{1,0:T(8,128)(2,1)S(1)}, u32[]{:S(2)}, u32[]{:S(2)}) collective-permute-start(bf16[128,512]{1,0:T(8,128)(2,1)S(1)} %collective-permute-done.16.refs_2_), channel_id=1, source_target_pairs={{0,1},{1,0},{2,3},{3,2},{4,5},{5,4},{6,7},{7,6},{8,9},{9,8},{10,11... | collective-permute-start | bytes 393224 | tf_op jit(solution)/shard_map/ppermute | solution.py:64
  66.1 1.3 %collective-permute-start.19 = (bf16[128,512]{1,0:T(8,128)(2,1)S(1)}, bf16[128,512]{1,0:T(8,128)(2,1)S(1)}, u32[]{:S(2)}, u32[]{:S(2)}) collective-permute-start(bf16[128,512]{1,0:T(8,128)(2,1)S(1)} %collective-permute-done.15.refs_1_), channel_id=1, source_target_pairs={{0,1},{1,0},{2,3},{3,2},{4,5},{5,4},{6,7},{7,6},{8,9},{9,8},{10,11... | collective-permute-start | bytes 393224 | tf_op jit(solution)/shard_map/ppermute | solution.py:64
  68.4 7.3 %collective-permute-start.31 = (bf16[384,256]{1,0:T(8,128)(2,1)S(1)}, bf16[384,256]{1,0:T(8,128)(2,1)S(1)}, u32[]{:S(2)}, u32[]{:S(2)}) collective-permute-start(bf16[384,256]{1,0:T(8,128)(2,1)S(1)} %shard_map.94.a_ref), channel_id=1, source_target_pairs={{0,24},{8,16},{16,8},{24,0},{1,25},{9,17},{17,9},{25,1},{2,26},{10... | collective-permute-start | bytes 589832 | tf_op jit(solution)/shard_map/ppermute | solution.py:64
  70.6 9.8 %collective-permute-start.30 = (bf16[384,256]{1,0:T(8,128)(2,1)S(1)}, bf16[384,256]{1,0:T(8,128)(2,1)S(1)}, u32[]{:S(2)}, u32[]{:S(2)}) collective-permute-start(bf16[384,256]{1,0:T(8,128)(2,1)S(1)} %shard_map.94.a_ref), channel_id=1, source_target_pairs={{0,16},{8,24},{16,0},{24,8},{1,17},{9,25},{17,1},{25,9},{2,18},{10... | collective-permute-start | bytes 589832 | tf_op jit(solution)/shard_map/ppermute | solution.py:64
  70.8 10.0 %collective-permute-start.29 = (bf16[384,256]{1,0:T(8,128)(2,1)S(1)}, bf16[384,256]{1,0:T(8,128)(2,1)S(1)}, u32[]{:S(2)}, u32[]{:S(2)}) collective-permute-start(bf16[384,256]{1,0:T(8,128)(2,1)S(1)} %shard_map.94.a_ref), channel_id=1, source_target_pairs={{0,8},{8,0},{16,24},{24,16},{1,9},{9,1},{17,25},{25,17},{2,10},{10... | collective-permute-start | bytes 589832 | tf_op jit(solution)/shard_map/ppermute | solution.py:64
  71.1 11.7 %collective-permute-start.24 = (bf16[128,512]{1,0:T(8,128)(2,1)S(1)}, bf16[128,512]{1,0:T(8,128)(2,1)S(1)}, u32[]{:S(2)}, u32[]{:S(2)}) collective-permute-start(bf16[128,512]{1,0:T(8,128)(2,1)S(1)} %shard_map.93), channel_id=1, source_target_pairs={{0,6},{1,7},{2,4},{3,5},{4,2},{5,3},{6,0},{7,1},{8,14},{9,15},{10,... | collective-permute-start | bytes 393224 | tf_op jit(solution)/shard_map/ppermute | solution.py:64
  73.5 10.7 %collective-permute-start.23 = (bf16[128,512]{1,0:T(8,128)(2,1)S(1)}, bf16[128,512]{1,0:T(8,128)(2,1)S(1)}, u32[]{:S(2)}, u32[]{:S(2)}) collective-permute-start(bf16[128,512]{1,0:T(8,128)(2,1)S(1)} %shard_map.93), channel_id=1, source_target_pairs={{0,4},{1,5},{2,6},{3,7},{4,0},{5,1},{6,2},{7,3},{8,12},{9,13},{10,... | collective-permute-start | bytes 393224 | tf_op jit(solution)/shard_map/ppermute | solution.py:64
  75.7 8.5 %collective-permute-start.22 = (bf16[128,512]{1,0:T(8,128)(2,1)S(1)}, bf16[128,512]{1,0:T(8,128)(2,1)S(1)}, u32[]{:S(2)}, u32[]{:S(2)}) collective-permute-start(bf16[128,512]{1,0:T(8,128)(2,1)S(1)} %shard_map.93), channel_id=1, source_target_pairs={{0,2},{1,3},{2,0},{3,1},{4,6},{5,7},{6,4},{7,5},{8,10},{9,11},{10,... | collective-permute-start | bytes 393224 | tf_op jit(solution)/shard_map/ppermute | solution.py:64
  80.4 12.0 %collective-permute-start.28 = (bf16[4,128,512]{2,1,0:T(8,128)(2,1)S(1)}, bf16[4,128,512]{2,1,0:T(8,128)(2,1)S(1)}, u32[]{:S(2)}, u32[]{:S(2)}) collective-permute-start(bf16[4,128,512]{2,1,0:T(8,128)(2,1)S(1)} %get-tuple-element.77.refs_0_), channel_id=1, source_target_pairs={{0,1},{1,0},{2,3},{3,2},{4,5},{5,4},{6,7},{7,6},{8,9},{9,8},{10,11... | collective-permute-start | bytes 1572872 | tf_op jit(solution)/shard_map/ppermute | solution.py:64
  82.6 4.3 %collective-permute-start.32 = (f32[384,128]{1,0:T(8,128)S(1)}, f32[384,128]{1,0:T(8,128)S(1)}, u32[]{:S(2)}, u32[]{:S(2)}) collective-permute-start(f32[384,128]{1,0:T(8,128)S(1)} %get-tuple-element.79), channel_id=1, source_target_pairs={{0,1},{1,0},{2,3},{3,2},{4,5},{5,4},{6,7},{7,6},{8,9},{9,8},{10,11... | collective-permute-start | bytes 589832 | tf_op jit(solution)/shard_map/ppermute | solution.py:64
  84.3 13.0 %collective-permute-start.27 = (bf16[3,128,512]{2,1,0:T(8,128)(2,1)S(1)}, bf16[3,128,512]{2,1,0:T(8,128)(2,1)S(1)}, u32[]{:S(2)}, u32[]{:S(2)}) collective-permute-start(bf16[3,128,512]{2,1,0:T(8,128)(2,1)S(1)} %pad_maximum_fusion.1.refs_0_), channel_id=1, source_target_pairs={{0,24},{8,16},{16,8},{24,0},{1,25},{9,17},{17,9},{25,1},{2,26},{10... | collective-permute-start | bytes 1179656 | tf_op jit(solution)/shard_map/ppermute | solution.py:64
  86.5 18.2 %collective-permute-start.26 = (bf16[3,128,512]{2,1,0:T(8,128)(2,1)S(1)}, bf16[3,128,512]{2,1,0:T(8,128)(2,1)S(1)}, u32[]{:S(2)}, u32[]{:S(2)}) collective-permute-start(bf16[3,128,512]{2,1,0:T(8,128)(2,1)S(1)} %pad_maximum_fusion.1.refs_0_), channel_id=1, source_target_pairs={{0,16},{8,24},{16,0},{24,8},{1,17},{9,25},{17,1},{25,9},{2,18},{10... | collective-permute-start | bytes 1179656 | tf_op jit(solution)/shard_map/ppermute | solution.py:64
  86.7 18.0 %collective-permute-start.25 = (bf16[3,128,512]{2,1,0:T(8,128)(2,1)S(1)}, bf16[3,128,512]{2,1,0:T(8,128)(2,1)S(1)}, u32[]{:S(2)}, u32[]{:S(2)}) collective-permute-start(bf16[3,128,512]{2,1,0:T(8,128)(2,1)S(1)} %pad_maximum_fusion.1.refs_0_), channel_id=1, source_target_pairs={{0,8},{8,0},{16,24},{24,16},{1,9},{9,1},{17,25},{25,17},{2,10},{10... | collective-permute-start | bytes 1179656 | tf_op jit(solution)/shard_map/ppermute | solution.py:64
  87.0 3.8 %collective-permute-start.33 = (bf16[384,128]{1,0:T(8,128)(2,1)S(1)}, bf16[384,128]{1,0:T(8,128)(2,1)S(1)}, u32[]{:S(2)}, u32[]{:S(2)}) collective-permute-start(bf16[384,128]{1,0:T(8,128)(2,1)S(1)} %get-tuple-element.81), channel_id=1, source_target_pairs={{0,2},{1,3},{2,0},{3,1},{4,6},{5,7},{6,4},{7,5},{8,10},{9,11},{10,... | collective-permute-start | bytes 294920 | tf_op jit(solution)/shard_map/ppermute | solution.py:64
  90.9 5.8 %collective-permute-start.34 = (bf16[384,128]{1,0:T(8,128)(2,1)S(1)}, bf16[384,128]{1,0:T(8,128)(2,1)S(1)}, u32[]{:S(2)}, u32[]{:S(2)}) collective-permute-start(bf16[384,128]{1,0:T(8,128)(2,1)S(1)} %get-tuple-element.83), channel_id=1, source_target_pairs={{0,4},{1,5},{2,6},{3,7},{4,0},{5,1},{6,2},{7,3},{8,12},{9,13},{10,... | collective-permute-start | bytes 294920 | tf_op jit(solution)/shard_map/ppermute | solution.py:64
  104.7 7.4 %collective-permute-start.35 = (bf16[3,128,512]{2,1,0:T(8,128)(2,1)S(1)}, bf16[3,128,512]{2,1,0:T(8,128)(2,1)S(1)}, u32[]{:S(2)}, u32[]{:S(2)}) collective-permute-start(bf16[3,128,512]{2,1,0:T(8,128)(2,1)S(1)} %pad_maximum_fusion.1.refs_0_), channel_id=1, source_target_pairs={{0,1},{1,0},{2,3},{3,2},{4,5},{5,4},{6,7},{7,6},{8,9},{9,8},{10,11... | collective-permute-start | bytes 1179656 | tf_op jit(solution)/shard_map/ppermute | solution.py:64
  105.3 6.9 %collective-permute-start.36 = (bf16[3,128,512]{2,1,0:T(8,128)(2,1)S(1)}, bf16[3,128,512]{2,1,0:T(8,128)(2,1)S(1)}, u32[]{:S(2)}, u32[]{:S(2)}) collective-permute-start(bf16[3,128,512]{2,1,0:T(8,128)(2,1)S(1)} %collective-permute-done.25.refs_1_), channel_id=1, source_target_pairs={{0,1},{1,0},{2,3},{3,2},{4,5},{5,4},{6,7},{7,6},{8,9},{9,8},{10,11... | collective-permute-start | bytes 1179656 | tf_op jit(solution)/shard_map/ppermute | solution.py:64
  105.3 6.9 %collective-permute-start.37 = (bf16[3,128,512]{2,1,0:T(8,128)(2,1)S(1)}, bf16[3,128,512]{2,1,0:T(8,128)(2,1)S(1)}, u32[]{:S(2)}, u32[]{:S(2)}) collective-permute-start(bf16[3,128,512]{2,1,0:T(8,128)(2,1)S(1)} %collective-permute-done.26.refs_2_), channel_id=1, source_target_pairs={{0,1},{1,0},{2,3},{3,2},{4,5},{5,4},{6,7},{7,6},{8,9},{9,8},{10,11... | collective-permute-start | bytes 1179656 | tf_op jit(solution)/shard_map/ppermute | solution.py:64
  105.8 6.4 %collective-permute-start.38 = (bf16[3,128,512]{2,1,0:T(8,128)(2,1)S(1)}, bf16[3,128,512]{2,1,0:T(8,128)(2,1)S(1)}, u32[]{:S(2)}, u32[]{:S(2)}) collective-permute-start(bf16[3,128,512]{2,1,0:T(8,128)(2,1)S(1)} %collective-permute-done.27.refs_3_), channel_id=1, source_target_pairs={{0,1},{1,0},{2,3},{3,2},{4,5},{5,4},{6,7},{7,6},{8,9},{9,8},{10,11... | collective-permute-start | bytes 1179656 | tf_op jit(solution)/shard_map/ppermute | solution.py:64
  105.8 3.8 %collective-permute-start.39 = (f32[384,128]{1,0:T(8,128)S(1)}, f32[384,128]{1,0:T(8,128)S(1)}, u32[]{:S(2)}, u32[]{:S(2)}) collective-permute-start(f32[384,128]{1,0:T(8,128)S(1)} %get-tuple-element.84.own_ref), channel_id=1, source_target_pairs={{0,1},{1,0},{2,3},{3,2},{4,5},{5,4},{6,7},{7,6},{8,9},{9,8},{10,11... | collective-permute-start | bytes 589832 | tf_op jit(solution)/shard_map/ppermute | solution.py:64

commit v6 on v5

--- a/solution.py
+++ b/solution.py
@@ -397,7 +397,7 @@
     half = finish(own, chip(following, 1))
 
     gathered = [half] + [group(half, a) for a in (1, 2, 3)]
-    late = after(half, gathered[1], gathered[2])
+    late = after(half, gathered[1])
     halves = [half] + [chip(late if k == 1 else half, k) for k in (1, 2, 3)]
     far_half = core(late)
     mine = own_direction(place, half, moment_one, moment_two)
@@ -406,7 +406,7 @@
 
     halves[3] = after(halves[3], mine)
     halves += [far_half] + [core(h) for h in halves[1:]]
-    halves[0] = after(halves[0], gathered[3])
+    halves[0] = after(halves[0], gathered[2], gathered[3])
     part = span(gradient_high, gradient_low, halves)
     parts = [part] + [group(part, a) for a in (1, 2, 3)]
     mine = after(mine, part)

time: 116 us -> 116 us (level)
  waiting for transfers between devices: 47.4 us -> 46.1 us
    ppermute x40, waiting for transfers between devices: 47.4 us -> 46.1 us  [swap(): return lax.ppermute(x, axis, [(i, i ^ bit) for i in range(size)])]
  transfers between devices with their start and end apart: 40 -> 40, of which waited for: 21 -> 20; matrix products, arithmetic and copies ran while one was open for 1% -> 1% of each run, Pallas kernels for 17% -> 17%
where the time goes in v6:
time: 116 us; the launch traced here: 115 us
  waiting for transfers between devices  46.1 us (40%)
  starting transfers between devices  39.6 us (34%)
  Pallas kernels  27.4 us (24%)
    ppermute x40, waiting for transfers between devices, swap(): return lax.ppermute(x, axis, [(i, i ^ bit) for i in range(size)])  46.1 us
    ppermute x40, starting transfers between devices, swap(): return lax.ppermute(x, axis, [(i, i ^ bit) for i in range(size)])  39.6 us
    pallas_call x3, Pallas kernels, update(): pl.pallas_call(body, grid_spec=pltpu.PrefetchScalarGridSpec(num_scalar_pr...  9.09 us
    pallas_call x2, Pallas kernels, pack(): pl.pallas_call(body, grid_spec=pltpu.PrefetchScalarGridSpec(num_scalar_pr...  6.59 us
    pallas_call x13, Pallas kernels, call(): pl.pallas_call(body, in_specs=[SMEM] * len(scalars) + [VMEM] * len(args),...  5.63 us
    pallas_call x1, Pallas kernels, moments(): pl.pallas_call(body, in_specs=[SMEM] + [VMEM] * 6, out_specs=(VMEM,) * 3,...  3.54 us
    pallas_call x1, Pallas kernels, polish(): pl.pallas_call(body, in_specs=[SMEM] + [VMEM] * 3, out_specs=VMEM, out_sh...  2.5 us
  transfers between devices with their start and end apart: 40, of which 20 were waited for; matrix products, arithmetic and copies ran while one was open for 1% of the time, Pallas kernels for 17%

profile of v6, /device:TPU:1, one launch (start us, length us, event | category | flops | bytes accessed | tf_op | source)
XLA Modules:
  0.0 115.3 jit_solution(6896271512161436022)
XLA Ops:
  0.7 3.3 %shard_map.84 = (bf16[2,2,384,128]{3,2,1,0:T(8,128)(2,1)S(1)}, bf16[2,2,384,128]{3,2,1,0:T(8,128)(2,1)S(1)}, bf16[2,2,384,128]{3,2,1,0:T(8,128)(2,1)S(1)}, bf16[2,2,384,128]{3,2,1,0:T(8,128)(2,1)S(1)}) custom-call(s32[3]{0:T(128)S(1)} %pad_add_fusion.place_ref, bf16[192,2,4096]{2,1,0:T(2,128)(2,1)} %bitcast.9), custom_call_target="tpu_custom_call" | custom-call | bytes 11550000 | tf_op jit(solution)/shard_map/pallas_call | solution.py:118
  4.0 2.1 %collective-permute-start = (bf16[2,2,384,128]{3,2,1,0:T(8,128)(2,1)S(1)}, bf16[2,2,384,128]{3,2,1,0:T(8,128)(2,1)S(1)}, u32[]{:S(2)}, u32[]{:S(2)}) collective-permute-start(bf16[2,2,384,128]{3,2,1,0:T(8,128)(2,1)S(1)} %get-tuple-element.48), channel_id=1, source_target_pairs={{0,8},{8,0},{16,24},{24,16},{1,9},{9,1},{17,25},{25,17},{2,10},{10... | collective-permute-start | bytes 1179656 | tf_op jit(solution)/shard_map/ppermute | solution.py:64
  6.1 1.2 %collective-permute-start.1 = (bf16[2,2,384,128]{3,2,1,0:T(8,128)(2,1)S(1)}, bf16[2,2,384,128]{3,2,1,0:T(8,128)(2,1)S(1)}, u32[]{:S(2)}, u32[]{:S(2)}) collective-permute-start(bf16[2,2,384,128]{3,2,1,0:T(8,128)(2,1)S(1)} %get-tuple-element.49), channel_id=1, source_target_pairs={{0,16},{8,24},{16,0},{24,8},{1,17},{9,25},{17,1},{25,9},{2,18},{10... | collective-permute-start | bytes 1179656 | tf_op jit(solution)/shard_map/ppermute | solution.py:64
  7.4 1.0 reshape.11
  8.4 3.3 %shard_map.85 = (bf16[2,2,384,128]{3,2,1,0:T(8,128)(2,1)S(1)}, bf16[2,2,384,128]{3,2,1,0:T(8,128)(2,1)S(1)}, bf16[2,2,384,128]{3,2,1,0:T(8,128)(2,1)S(1)}, bf16[2,2,384,128]{3,2,1,0:T(8,128)(2,1)S(1)}) custom-call(s32[3]{0:T(128)S(1)} %pad_add_fusion.place_ref, bf16[192,2,4096]{2,1,0:T(2,128)(2,1)} %bitcast.10), custom_call_target="tpu_custom_call" | custom-call | bytes 11550000 | tf_op jit(solution)/shard_map/pallas_call | solution.py:118
  11.7 3.2 %collective-permute-done.came_x_ref.refs_1_ = bf16[2,2,384,128]{3,2,1,0:T(8,128)(2,1)S(1)} collective-permute-done((bf16[2,2,384,128]{3,2,1,0:T(8,128)(2,1)S(1)}, bf16[2,2,384,128]{3,2,1,0:T(8,128)(2,1)S(1)}, u32[]{:S(2)}, u32[]{:S(2)}) %collective-permute-start) | collective-permute-done | bytes 393248 | tf_op jit(solution)/shard_map/ppermute | solution.py:64
  15.0 0.8 collective-permute-done.1.came_y_ref.refs_4_
  15.9 1.3 %collective-permute-start.6 = (bf16[2,384,128]{2,1,0:T(8,128)(2,1)S(1)}, bf16[2,384,128]{2,1,0:T(8,128)(2,1)S(1)}, u32[]{:S(2)}, u32[]{:S(2)}) collective-permute-start(bf16[2,384,128]{2,1,0:T(8,128)(2,1)S(1)} %get-tuple-element.64), channel_id=1, source_target_pairs={{0,16},{8,24},{16,0},{24,8},{1,17},{9,25},{17,1},{25,9},{2,18},{10... | collective-permute-start | bytes 589832 | tf_op jit(solution)/shard_map/ppermute | solution.py:64
  17.7 1.2 %collective-permute-start.2 = (bf16[2,2,384,128]{3,2,1,0:T(8,128)(2,1)S(1)}, bf16[2,2,384,128]{3,2,1,0:T(8,128)(2,1)S(1)}, u32[]{:S(2)}, u32[]{:S(2)}) collective-permute-start(bf16[2,2,384,128]{3,2,1,0:T(8,128)(2,1)S(1)} %get-tuple-element.56), channel_id=1, source_target_pairs={{0,8},{8,0},{16,24},{24,16},{1,9},{9,1},{17,25},{25,17},{2,10},{10... | collective-permute-start | bytes 1179656 | tf_op jit(solution)/shard_map/ppermute | solution.py:64
  19.2 1.3 %collective-permute-done.6.refs_2_ = bf16[2,384,128]{2,1,0:T(8,128)(2,1)S(1)} collective-permute-done((bf16[2,384,128]{2,1,0:T(8,128)(2,1)S(1)}, bf16[2,384,128]{2,1,0:T(8,128)(2,1)S(1)}, u32[]{:S(2)}, u32[]{:S(2)}) %collective-permute-start.6) | collective-permute-done | bytes 196640 | tf_op jit(solution)/shard_map/ppermute | solution.py:64
  20.5 1.5 %collective-permute-done.7.refs_5_ = bf16[2,384,128]{2,1,0:T(8,128)(2,1)S(1)} collective-permute-done((bf16[2,384,128]{2,1,0:T(8,128)(2,1)S(1)}, bf16[2,384,128]{2,1,0:T(8,128)(2,1)S(1)}, u32[]{:S(2)}, u32[]{:S(2)}) %collective-permute-start.7) | collective-permute-done | bytes 196640 | tf_op jit(solution)/shard_map/ppermute | solution.py:64
  22.5 5.2 %collective-permute-start.8 = (bf16[2,128,512]{2,1,0:T(8,128)(2,1)S(1)}, bf16[2,128,512]{2,1,0:T(8,128)(2,1)S(1)}, u32[]{:S(2)}, u32[]{:S(2)}) collective-permute-start(bf16[2,128,512]{2,1,0:T(8,128)(2,1)S(1)} %get-tuple-element.67), channel_id=1, source_target_pairs={{0,1},{1,0},{2,3},{3,2},{4,5},{5,4},{6,7},{7,6},{8,9},{9,8},{10,11... | collective-permute-start | bytes 786440 | tf_op jit(solution)/shard_map/ppermute | solution.py:64
  27.7 1.2 %collective-permute-done.8.came_ref = bf16[2,128,512]{2,1,0:T(8,128)(2,1)S(1)} collective-permute-done((bf16[2,128,512]{2,1,0:T(8,128)(2,1)S(1)}, bf16[2,128,512]{2,1,0:T(8,128)(2,1)S(1)}, u32[]{:S(2)}, u32[]{:S(2)}) %collective-permute-start.8) | collective-permute-done | bytes 262176 | tf_op jit(solution)/shard_map/ppermute | solution.py:64
  28.9 2.4 %collective-permute-start.9 = (bf16[2,128,512]{2,1,0:T(8,128)(2,1)S(1)}, bf16[2,128,512]{2,1,0:T(8,128)(2,1)S(1)}, u32[]{:S(2)}, u32[]{:S(2)}) collective-permute-start(bf16[2,128,512]{2,1,0:T(8,128)(2,1)S(1)} %shard_map.90), channel_id=1, source_target_pairs={{0,4},{1,5},{2,6},{3,7},{4,0},{5,1},{6,2},{7,3},{8,12},{9,13},{10,... | collective-permute-start | bytes 786440 | tf_op jit(solution)/shard_map/ppermute | solution.py:64
  32.0 4.3 %collective-permute-done.4.refs_2_ = bf16[2,384,128]{2,1,0:T(8,128)(2,1)S(1)} collective-permute-done((bf16[2,384,128]{2,1,0:T(8,128)(2,1)S(1)}, bf16[2,384,128]{2,1,0:T(8,128)(2,1)S(1)}, u32[]{:S(2)}, u32[]{:S(2)}) %collective-permute-start.4) | collective-permute-done | bytes 196640 | tf_op jit(solution)/shard_map/ppermute | solution.py:64
  37.0 6.0 %collective-permute-done.9.chips_ref = bf16[2,128,512]{2,1,0:T(8,128)(2,1)S(1)} collective-permute-done((bf16[2,128,512]{2,1,0:T(8,128)(2,1)S(1)}, bf16[2,128,512]{2,1,0:T(8,128)(2,1)S(1)}, u32[]{:S(2)}, u32[]{:S(2)}) %collective-permute-start.9) | collective-permute-done | bytes 262176 | tf_op jit(solution)/shard_map/ppermute | solution.py:64
  43.0 1.2 %collective-permute-start.10 = (bf16[2,128,512]{2,1,0:T(8,128)(2,1)S(1)}, bf16[2,128,512]{2,1,0:T(8,128)(2,1)S(1)}, u32[]{:S(2)}, u32[]{:S(2)}) collective-permute-start(bf16[2,128,512]{2,1,0:T(8,128)(2,1)S(1)} %get-tuple-element.68), channel_id=1, source_target_pairs={{0,1},{1,0},{2,3},{3,2},{4,5},{5,4},{6,7},{7,6},{8,9},{9,8},{10,11... | collective-permute-start | bytes 786440 | tf_op jit(solution)/shard_map/ppermute | solution.py:64
  44.2 1.2 %collective-permute-done.10.came_ref = bf16[2,128,512]{2,1,0:T(8,128)(2,1)S(1)} collective-permute-done((bf16[2,128,512]{2,1,0:T(8,128)(2,1)S(1)}, bf16[2,128,512]{2,1,0:T(8,128)(2,1)S(1)}, u32[]{:S(2)}, u32[]{:S(2)}) %collective-permute-start.10) | collective-permute-done | bytes 262176 | tf_op jit(solution)/shard_map/ppermute | solution.py:64
  45.9 4.3 %collective-permute-done.11.came_ref = bf16[128,512]{1,0:T(8,128)(2,1)S(1)} collective-permute-done((bf16[128,512]{1,0:T(8,128)(2,1)S(1)}, bf16[128,512]{1,0:T(8,128)(2,1)S(1)}, u32[]{:S(2)}, u32[]{:S(2)}) %collective-permute-start.11) | collective-permute-done | bytes 131104 | tf_op jit(solution)/shard_map/ppermute | solution.py:64
  50.6 3.2 %collective-permute-start.17 = (bf16[128,512]{1,0:T(8,128)(2,1)S(1)}, bf16[128,512]{1,0:T(8,128)(2,1)S(1)}, u32[]{:S(2)}, u32[]{:S(2)}) collective-permute-start(bf16[128,512]{1,0:T(8,128)(2,1)S(1)} %shard_map.92.half_ref.refs_0_), channel_id=1, source_target_pairs={{0,6},{1,7},{2,4},{3,5},{4,2},{5,3},{6,0},{7,1},{8,14},{9,15},{10,... | collective-permute-start | bytes 393224 | tf_op jit(solution)/shard_map/ppermute | solution.py:64
  53.8 1.2 collective-permute-start.13
  55.3 1.2 %collective-permute-start.12 = (bf16[128,512]{1,0:T(8,128)(2,1)S(1)}, bf16[128,512]{1,0:T(8,128)(2,1)S(1)}, u32[]{:S(2)}, u32[]{:S(2)}) collective-permute-start(bf16[128,512]{1,0:T(8,128)(2,1)S(1)} %shard_map.92.half_ref.refs_0_), channel_id=1, source_target_pairs={{0,16},{8,24},{16,0},{24,8},{1,17},{9,25},{17,1},{25,9},{2,18},{10... | collective-permute-start | bytes 393224 | tf_op jit(solution)/shard_map/ppermute | solution.py:64
  56.6 0.9 shard_map.93
  57.5 2.9 %collective-permute-start.18 = (bf16[128,512]{1,0:T(8,128)(2,1)S(1)}, bf16[128,512]{1,0:T(8,128)(2,1)S(1)}, u32[]{:S(2)}, u32[]{:S(2)}) collective-permute-start(bf16[128,512]{1,0:T(8,128)(2,1)S(1)} %shard_map.92.half_ref.refs_0_), channel_id=1, source_target_pairs={{0,1},{1,0},{2,3},{3,2},{4,5},{5,4},{6,7},{7,6},{8,9},{9,8},{10,11... | collective-permute-start | bytes 393224 | tf_op jit(solution)/shard_map/ppermute | solution.py:64
  60.5 3.9 %collective-permute-done.16.refs_2_ = bf16[128,512]{1,0:T(8,128)(2,1)S(1)} collective-permute-done((bf16[128,512]{1,0:T(8,128)(2,1)S(1)}, bf16[128,512]{1,0:T(8,128)(2,1)S(1)}, u32[]{:S(2)}, u32[]{:S(2)}) %collective-permute-start.16) | collective-permute-done | bytes 131104 | tf_op jit(solution)/shard_map/ppermute | solution.py:64
  64.4 1.4 %collective-permute-start.21 = (bf16[128,512]{1,0:T(8,128)(2,1)S(1)}, bf16[128,512]{1,0:T(8,128)(2,1)S(1)}, u32[]{:S(2)}, u32[]{:S(2)}) collective-permute-start(bf16[128,512]{1,0:T(8,128)(2,1)S(1)} %collective-permute-done.17.refs_3_), channel_id=1, source_target_pairs={{0,1},{1,0},{2,3},{3,2},{4,5},{5,4},{6,7},{7,6},{8,9},{9,8},{10,11... | collective-permute-start | bytes 393224 | tf_op jit(solution)/shard_map/ppermute | solution.py:64
  65.9 0.5 collective-permute-start.19
  67.4 0.9 shard_map.94.a_ref
  68.3 1.2 %collective-permute-start.31 = (bf16[384,256]{1,0:T(8,128)(2,1)S(1)}, bf16[384,256]{1,0:T(8,128)(2,1)S(1)}, u32[]{:S(2)}, u32[]{:S(2)}) collective-permute-start(bf16[384,256]{1,0:T(8,128)(2,1)S(1)} %shard_map.94.a_ref), channel_id=1, source_target_pairs={{0,24},{8,16},{16,8},{24,0},{1,25},{9,17},{17,9},{25,1},{2,26},{10... | collective-permute-start | bytes 589832 | tf_op jit(solution)/shard_map/ppermute | solution.py:64
  69.6 1.2 %collective-permute-start.30 = (bf16[384,256]{1,0:T(8,128)(2,1)S(1)}, bf16[384,256]{1,0:T(8,128)(2,1)S(1)}, u32[]{:S(2)}, u32[]{:S(2)}) collective-permute-start(bf16[384,256]{1,0:T(8,128)(2,1)S(1)} %shard_map.94.a_ref), channel_id=1, source_target_pairs={{0,16},{8,24},{16,0},{24,8},{1,17},{9,25},{17,1},{25,9},{2,18},{10... | collective-permute-start | bytes 589832 | tf_op jit(solution)/shard_map/ppermute | solution.py:64
  71.1 2.4 %collective-permute-start.24 = (bf16[128,512]{1,0:T(8,128)(2,1)S(1)}, bf16[128,512]{1,0:T(8,128)(2,1)S(1)}, u32[]{:S(2)}, u32[]{:S(2)}) collective-permute-start(bf16[128,512]{1,0:T(8,128)(2,1)S(1)} %shard_map.93), channel_id=1, source_target_pairs={{0,6},{1,7},{2,4},{3,5},{4,2},{5,3},{6,0},{7,1},{8,14},{9,15},{10,... | collective-permute-start | bytes 393224 | tf_op jit(solution)/shard_map/ppermute | solution.py:64
  73.4 2.1 %collective-permute-done.31.d_ref = bf16[384,256]{1,0:T(8,128)(2,1)S(1)} collective-permute-done((bf16[384,256]{1,0:T(8,128)(2,1)S(1)}, bf16[384,256]{1,0:T(8,128)(2,1)S(1)}, u32[]{:S(2)}, u32[]{:S(2)}) %collective-permute-start.31) | collective-permute-done | bytes 196640 | tf_op jit(solution)/shard_map/ppermute | solution.py:64
  75.5 3.5 %shard_map.95 = (f32[512,2,256]{2,1,0:T(2,128)}, f32[512,2,256]{2,1,0:T(2,128)}, bf16[4,128,512]{2,1,0:T(8,128)(2,1)S(1)}) custom-call(s32[3]{0:T(128)S(1)} %pad_add_fusion.place_ref, bf16[128,512]{1,0:T(8,128)(2,1)S(1)} %shard_map.92.half_ref.refs_0_, bf16[128,512]{1,0:T(8,128)(2,1)S(1)} %collective-permute-done.14.refs_1_, ...), custom_call_target="tpu_custom_call" | custom-call | bytes 12250000 | tf_op jit(solution)/shard_map/pallas_call | solution.py:217
  79.1 1.3 %collective-permute-done.30.c_ref = bf16[384,256]{1,0:T(8,128)(2,1)S(1)} collective-permute-done((bf16[384,256]{1,0:T(8,128)(2,1)S(1)}, bf16[384,256]{1,0:T(8,128)(2,1)S(1)}, u32[]{:S(2)}, u32[]{:S(2)}) %collective-permute-start.30) | collective-permute-done | bytes 196640 | tf_op jit(solution)/shard_map/ppermute | solution.py:64
  80.3 0.6 collective-permute-start.28
  81.0 1.8 %shard_map.97 = (f32[384,256]{1,0:T(8,128)S(1)}, f32[384,128]{1,0:T(8,128)S(1)}, f32[384,128]{1,0:T(8,128)S(1)}) custom-call(s32[3]{0:T(128)S(1)} %pad_add_fusion.place_ref, bf16[384,256]{1,0:T(8,128)(2,1)S(1)} %shard_map.94.a_ref, bf16[384,256]{1,0:T(8,128)(2,1)S(1)} %collective-permute-done.29.b_ref, bf16[384,256]{1,0:T(8,128)(2,1)S(1)} %collective-permute-done.30.c_ref, ...), custom_call_target="tpu_custom_call" | custom-call | bytes 6300000 | tf_op jit(solution)/shard_map/pallas_call | solution.py:83
  82.8 1.3 %collective-permute-done.23 = bf16[128,512]{1,0:T(8,128)(2,1)S(1)} collective-permute-done((bf16[128,512]{1,0:T(8,128)(2,1)S(1)}, bf16[128,512]{1,0:T(8,128)(2,1)S(1)}, u32[]{:S(2)}, u32[]{:S(2)}) %collective-permute-start.23) | collective-permute-done | bytes 131104 | tf_op jit(solution)/shard_map/ppermute | solution.py:64
  84.2 1.2 %collective-permute-start.27 = (bf16[3,128,512]{2,1,0:T(8,128)(2,1)S(1)}, bf16[3,128,512]{2,1,0:T(8,128)(2,1)S(1)}, u32[]{:S(2)}, u32[]{:S(2)}) collective-permute-start(bf16[3,128,512]{2,1,0:T(8,128)(2,1)S(1)} %pad_maximum_fusion.1.refs_0_), channel_id=1, source_target_pairs={{0,24},{8,16},{16,8},{24,0},{1,25},{9,17},{17,9},{25,1},{2,26},{10... | collective-permute-start | bytes 1179656 | tf_op jit(solution)/shard_map/ppermute | solution.py:64
  85.4 1.2 %collective-permute-start.26 = (bf16[3,128,512]{2,1,0:T(8,128)(2,1)S(1)}, bf16[3,128,512]{2,1,0:T(8,128)(2,1)S(1)}, u32[]{:S(2)}, u32[]{:S(2)}) collective-permute-start(bf16[3,128,512]{2,1,0:T(8,128)(2,1)S(1)} %pad_maximum_fusion.1.refs_0_), channel_id=1, source_target_pairs={{0,16},{8,24},{16,0},{24,8},{1,17},{9,25},{17,1},{25,9},{2,18},{10... | collective-permute-start | bytes 1179656 | tf_op jit(solution)/shard_map/ppermute | solution.py:64
  87.5 3.3 %collective-permute-done.33.came_ref = bf16[384,128]{1,0:T(8,128)(2,1)S(1)} collective-permute-done((bf16[384,128]{1,0:T(8,128)(2,1)S(1)}, bf16[384,128]{1,0:T(8,128)(2,1)S(1)}, u32[]{:S(2)}, u32[]{:S(2)}) %collective-permute-start.33) | collective-permute-done | bytes 98336 | tf_op jit(solution)/shard_map/ppermute | solution.py:64
  90.8 1.7 %collective-permute-start.34 = (bf16[384,128]{1,0:T(8,128)(2,1)S(1)}, bf16[384,128]{1,0:T(8,128)(2,1)S(1)}, u32[]{:S(2)}, u32[]{:S(2)}) collective-permute-start(bf16[384,128]{1,0:T(8,128)(2,1)S(1)} %get-tuple-element.83), channel_id=1, source_target_pairs={{0,4},{1,5},{2,6},{3,7},{4,0},{5,1},{6,2},{7,3},{8,12},{9,13},{10,... | collective-permute-start | bytes 294920 | tf_op jit(solution)/shard_map/ppermute | solution.py:64
  92.5 2.4 %shard_map.96.refs_4_ = f32[192,2,4096]{2,1,0:T(2,128)} custom-call(s32[3]{0:T(128)S(1)} %pad_add_fusion.place_ref, f32[192,2,4096]{2,1,0:T(2,128)S(1)} %bitcast.8, bf16[384,512]{1,0:T(8,128)(2,1)S(1)} %pad_maximum_fusion.refs_6_.s_ref, bf16[4,128,512]{2,1,0:T(8,128)(2,1)S(1)} %get-tuple-element.77.refs_0_, ...), custom_call_target="tpu_custom_call" | custom-call | bytes 8750000 | tf_op jit(solution)/shard_map/pallas_call | solution.py:346
  95.0 1.6 %collective-permute-done.34.came_ref = bf16[384,128]{1,0:T(8,128)(2,1)S(1)} collective-permute-done((bf16[384,128]{1,0:T(8,128)(2,1)S(1)}, bf16[384,128]{1,0:T(8,128)(2,1)S(1)}, u32[]{:S(2)}, u32[]{:S(2)}) %collective-permute-start.34) | collective-permute-done | bytes 98336 | tf_op jit(solution)/shard_map/ppermute | solution.py:64
  96.6 0.7 shard_map.100
  97.3 7.4 %collective-permute-done.26.refs_2_ = bf16[3,128,512]{2,1,0:T(8,128)(2,1)S(1)} collective-permute-done((bf16[3,128,512]{2,1,0:T(8,128)(2,1)S(1)}, bf16[3,128,512]{2,1,0:T(8,128)(2,1)S(1)}, u32[]{:S(2)}, u32[]{:S(2)}) %collective-permute-start.26) | collective-permute-done | bytes 393248 | tf_op jit(solution)/shard_map/ppermute | solution.py:64
  106.2 3.3 %shard_map.101.refs_4_ = f32[192,2,4096]{2,1,0:T(2,128)} custom-call(s32[3]{0:T(128)S(1)} %pad_add_fusion.place_ref, f32[192,2,4096]{2,1,0:T(2,128)S(1)} %bitcast.8, bf16[384,512]{1,0:T(8,128)(2,1)S(1)} %pad_maximum_fusion.refs_6_.s_ref, bf16[3,128,512]{2,1,0:T(8,128)(2,1)S(1)} %pad_maximum_fusion.1.refs_0_, ...), custom_call_target="tpu_custom_call", output_to_operand_aliasing={{}: (7, {})} | custom-call | bytes 12250000 | tf_op jit(solution)/shard_map/pallas_call | solution.py:346
  109.5 2.5 %shard_map.103 = bf16[192,2,256]{2,1,0:T(2,128)(2,1)} custom-call(s32[3]{0:T(128)S(1)} %pad_add_fusion.place_ref, f32[384,256]{1,0:T(8,128)S(1)} %get-tuple-element.91.spanned_ref, f32[384,128]{1,0:T(8,128)S(1)} %get-tuple-element.84.own_ref, f32[384,128]{1,0:T(8,128)S(1)} %collective-permute-done.39.other_ref), custom_call_target="tpu_custom_call" | custom-call | bytes 6300000 | tf_op jit(solution)/shard_map/pallas_call | solution.py:309
  112.0 3.3 %shard_map.102 = f32[192,2,4096]{2,1,0:T(2,128)} custom-call(s32[3]{0:T(128)S(1)} %pad_add_fusion.place_ref, f32[192,2,4096]{2,1,0:T(2,128)S(1)} %bitcast.8, bf16[384,512]{1,0:T(8,128)(2,1)S(1)} %pad_maximum_fusion.refs_6_.s_ref, bf16[3,128,512]{2,1,0:T(8,128)(2,1)S(1)} %collective-permute-done.35.refs_0_, ...), custom_call_target="tpu_custom_call", output_to_operand_aliasing={{}: (7, {})} | custom-call | bytes 12250000 | tf_op jit(solution)/shard_map/pallas_call | solution.py:346
  (68 shorter events, 7.8 us)
Async XLA Ops:
  4.0 10.9 %collective-permute-start = (bf16[2,2,384,128]{3,2,1,0:T(8,128)(2,1)S(1)}, bf16[2,2,384,128]{3,2,1,0:T(8,128)(2,1)S(1)}, u32[]{:S(2)}, u32[]{:S(2)}) collective-permute-start(bf16[2,2,384,128]{3,2,1,0:T(8,128)(2,1)S(1)} %get-tuple-element.48), channel_id=1, source_target_pairs={{0,8},{8,0},{16,24},{24,16},{1,9},{9,1},{17,25},{25,17},{2,10},{10... | collective-permute-start | bytes 1179656 | tf_op jit(solution)/shard_map/ppermute | solution.py:64
  6.1 9.7 %collective-permute-start.1 = (bf16[2,2,384,128]{3,2,1,0:T(8,128)(2,1)S(1)}, bf16[2,2,384,128]{3,2,1,0:T(8,128)(2,1)S(1)}, u32[]{:S(2)}, u32[]{:S(2)}) collective-permute-start(bf16[2,2,384,128]{3,2,1,0:T(8,128)(2,1)S(1)} %get-tuple-element.49), channel_id=1, source_target_pairs={{0,16},{8,24},{16,0},{24,8},{1,17},{9,25},{17,1},{25,9},{2,18},{10... | collective-permute-start | bytes 1179656 | tf_op jit(solution)/shard_map/ppermute | solution.py:64
  11.7 44.9 %copy-start = (f32[512,2,256]{2,1,0:T(2,128)S(1)}, f32[512,2,256]{2,1,0:T(2,128)}, u32[]{:S(2)}) copy-start(f32[512,2,256]{2,1,0:T(2,128)} %refs_4_.1) | copy-start | bytes 3145732
  11.7 44.9 %copy-start.1 = (f32[512,2,256]{2,1,0:T(2,128)S(1)}, f32[512,2,256]{2,1,0:T(2,128)}, u32[]{:S(2)}) copy-start(f32[512,2,256]{2,1,0:T(2,128)} %refs_5_.1) | copy-start | bytes 3145732
  15.9 4.6 %collective-permute-start.6 = (bf16[2,384,128]{2,1,0:T(8,128)(2,1)S(1)}, bf16[2,384,128]{2,1,0:T(8,128)(2,1)S(1)}, u32[]{:S(2)}, u32[]{:S(2)}) collective-permute-start(bf16[2,384,128]{2,1,0:T(8,128)(2,1)S(1)} %get-tuple-element.64), channel_id=1, source_target_pairs={{0,16},{8,24},{16,0},{24,8},{1,17},{9,25},{17,1},{25,9},{2,18},{10... | collective-permute-start | bytes 589832 | tf_op jit(solution)/shard_map/ppermute | solution.py:64
  17.2 4.8 %collective-permute-start.7 = (bf16[2,384,128]{2,1,0:T(8,128)(2,1)S(1)}, bf16[2,384,128]{2,1,0:T(8,128)(2,1)S(1)}, u32[]{:S(2)}, u32[]{:S(2)}) collective-permute-start(bf16[2,384,128]{2,1,0:T(8,128)(2,1)S(1)} %get-tuple-element.65), channel_id=1, source_target_pairs={{0,8},{8,0},{16,24},{24,16},{1,9},{9,1},{17,25},{25,17},{2,10},{10... | collective-permute-start | bytes 589832 | tf_op jit(solution)/shard_map/ppermute | solution.py:64
  17.7 13.6 %collective-permute-start.2 = (bf16[2,2,384,128]{3,2,1,0:T(8,128)(2,1)S(1)}, bf16[2,2,384,128]{3,2,1,0:T(8,128)(2,1)S(1)}, u32[]{:S(2)}, u32[]{:S(2)}) collective-permute-start(bf16[2,2,384,128]{3,2,1,0:T(8,128)(2,1)S(1)} %get-tuple-element.56), channel_id=1, source_target_pairs={{0,8},{8,0},{16,24},{24,16},{1,9},{9,1},{17,25},{25,17},{2,10},{10... | collective-permute-start | bytes 1179656 | tf_op jit(solution)/shard_map/ppermute | solution.py:64
  18.9 12.4 %collective-permute-start.3 = (bf16[2,2,384,128]{3,2,1,0:T(8,128)(2,1)S(1)}, bf16[2,2,384,128]{3,2,1,0:T(8,128)(2,1)S(1)}, u32[]{:S(2)}, u32[]{:S(2)}) collective-permute-start(bf16[2,2,384,128]{3,2,1,0:T(8,128)(2,1)S(1)} %get-tuple-element.58), channel_id=1, source_target_pairs={{0,16},{8,24},{16,0},{24,8},{1,17},{9,25},{17,1},{25,9},{2,18},{10... | collective-permute-start | bytes 1179656 | tf_op jit(solution)/shard_map/ppermute | solution.py:64
  22.5 6.4 %collective-permute-start.8 = (bf16[2,128,512]{2,1,0:T(8,128)(2,1)S(1)}, bf16[2,128,512]{2,1,0:T(8,128)(2,1)S(1)}, u32[]{:S(2)}, u32[]{:S(2)}) collective-permute-start(bf16[2,128,512]{2,1,0:T(8,128)(2,1)S(1)} %get-tuple-element.67), channel_id=1, source_target_pairs={{0,1},{1,0},{2,3},{3,2},{4,5},{5,4},{6,7},{7,6},{8,9},{9,8},{10,11... | collective-permute-start | bytes 786440 | tf_op jit(solution)/shard_map/ppermute | solution.py:64
  28.9 14.1 %collective-permute-start.9 = (bf16[2,128,512]{2,1,0:T(8,128)(2,1)S(1)}, bf16[2,128,512]{2,1,0:T(8,128)(2,1)S(1)}, u32[]{:S(2)}, u32[]{:S(2)}) collective-permute-start(bf16[2,128,512]{2,1,0:T(8,128)(2,1)S(1)} %shard_map.90), channel_id=1, source_target_pairs={{0,4},{1,5},{2,6},{3,7},{4,0},{5,1},{6,2},{7,3},{8,12},{9,13},{10,... | collective-permute-start | bytes 786440 | tf_op jit(solution)/shard_map/ppermute | solution.py:64
  31.3 61.2 %slice-start = ((s8[6291456]{0:T(1024)(128)(4,1)}), s8[4194304]{0:T(1024)(128)(4,1)S(1)}, s32[]{:S(2)}) async-start(s8[6291456]{0:T(1024)(128)(4,1)} %bitcast.7), calls=%async_computation | async-start | bytes 8388608
  31.4 4.9 %collective-permute-start.4 = (bf16[2,384,128]{2,1,0:T(8,128)(2,1)S(1)}, bf16[2,384,128]{2,1,0:T(8,128)(2,1)S(1)}, u32[]{:S(2)}, u32[]{:S(2)}) collective-permute-start(bf16[2,384,128]{2,1,0:T(8,128)(2,1)S(1)} %get-tuple-element.59), channel_id=1, source_target_pairs={{0,16},{8,24},{16,0},{24,8},{1,17},{9,25},{17,1},{25,9},{2,18},{10... | collective-permute-start | bytes 589832 | tf_op jit(solution)/shard_map/ppermute | solution.py:64
  31.7 4.8 %collective-permute-start.5 = (bf16[2,384,128]{2,1,0:T(8,128)(2,1)S(1)}, bf16[2,384,128]{2,1,0:T(8,128)(2,1)S(1)}, u32[]{:S(2)}, u32[]{:S(2)}) collective-permute-start(bf16[2,384,128]{2,1,0:T(8,128)(2,1)S(1)} %get-tuple-element.60), channel_id=1, source_target_pairs={{0,8},{8,0},{16,24},{24,16},{1,9},{9,1},{17,25},{25,17},{2,10},{10... | collective-permute-start | bytes 589832 | tf_op jit(solution)/shard_map/ppermute | solution.py:64
  43.0 2.4 %collective-permute-start.10 = (bf16[2,128,512]{2,1,0:T(8,128)(2,1)S(1)}, bf16[2,128,512]{2,1,0:T(8,128)(2,1)S(1)}, u32[]{:S(2)}, u32[]{:S(2)}) collective-permute-start(bf16[2,128,512]{2,1,0:T(8,128)(2,1)S(1)} %get-tuple-element.68), channel_id=1, source_target_pairs={{0,1},{1,0},{2,3},{3,2},{4,5},{5,4},{6,7},{7,6},{8,9},{9,8},{10,11... | collective-permute-start | bytes 786440 | tf_op jit(solution)/shard_map/ppermute | solution.py:64
  45.5 4.8 %collective-permute-start.11 = (bf16[128,512]{1,0:T(8,128)(2,1)S(1)}, bf16[128,512]{1,0:T(8,128)(2,1)S(1)}, u32[]{:S(2)}, u32[]{:S(2)}) collective-permute-start(bf16[128,512]{1,0:T(8,128)(2,1)S(1)} %get-tuple-element.70), channel_id=1, source_target_pairs={{0,2},{1,3},{2,0},{3,1},{4,6},{5,7},{6,4},{7,5},{8,10},{9,11},{10,... | collective-permute-start | bytes 393224 | tf_op jit(solution)/shard_map/ppermute | solution.py:64
  50.3 42.2 %slice-start.1 = ((s8[6291456]{0:T(1024)(128)(4,1)}), s8[2097152]{0:T(1024)(128)(4,1)S(1)}, s32[]{:S(2)}) async-start(s8[6291456]{0:T(1024)(128)(4,1)} %bitcast.7), calls=%async_computation.1 | async-start | bytes 4194304
  50.3 4.7 %collective-permute-start.14 = (bf16[128,512]{1,0:T(8,128)(2,1)S(1)}, bf16[128,512]{1,0:T(8,128)(2,1)S(1)}, u32[]{:S(2)}, u32[]{:S(2)}) collective-permute-start(bf16[128,512]{1,0:T(8,128)(2,1)S(1)} %shard_map.92.half_ref.refs_0_), channel_id=1, source_target_pairs={{0,8},{8,0},{16,24},{24,16},{1,9},{9,1},{17,25},{25,17},{2,10},{10... | collective-permute-start | bytes 393224 | tf_op jit(solution)/shard_map/ppermute | solution.py:64
  50.6 6.9 %collective-permute-start.17 = (bf16[128,512]{1,0:T(8,128)(2,1)S(1)}, bf16[128,512]{1,0:T(8,128)(2,1)S(1)}, u32[]{:S(2)}, u32[]{:S(2)}) collective-permute-start(bf16[128,512]{1,0:T(8,128)(2,1)S(1)} %shard_map.92.half_ref.refs_0_), channel_id=1, source_target_pairs={{0,6},{1,7},{2,4},{3,5},{4,2},{5,3},{6,0},{7,1},{8,14},{9,15},{10,... | collective-permute-start | bytes 393224 | tf_op jit(solution)/shard_map/ppermute | solution.py:64
  53.8 10.6 %collective-permute-start.16 = (bf16[128,512]{1,0:T(8,128)(2,1)S(1)}, bf16[128,512]{1,0:T(8,128)(2,1)S(1)}, u32[]{:S(2)}, u32[]{:S(2)}) collective-permute-start(bf16[128,512]{1,0:T(8,128)(2,1)S(1)} %shard_map.92.half_ref.refs_0_), channel_id=1, source_target_pairs={{0,4},{1,5},{2,6},{3,7},{4,0},{5,1},{6,2},{7,3},{8,12},{9,13},{10,... | collective-permute-start | bytes 393224 | tf_op jit(solution)/shard_map/ppermute | solution.py:64
  53.8 12.0 %collective-permute-start.13 = (bf16[128,512]{1,0:T(8,128)(2,1)S(1)}, bf16[128,512]{1,0:T(8,128)(2,1)S(1)}, u32[]{:S(2)}, u32[]{:S(2)}) collective-permute-start(bf16[128,512]{1,0:T(8,128)(2,1)S(1)} %shard_map.92.half_ref.refs_0_), channel_id=1, source_target_pairs={{0,24},{8,16},{16,8},{24,0},{1,25},{9,17},{17,9},{25,1},{2,26},{10... | collective-permute-start | bytes 393224 | tf_op jit(solution)/shard_map/ppermute | solution.py:64
  55.0 10.9 %collective-permute-start.15 = (bf16[128,512]{1,0:T(8,128)(2,1)S(1)}, bf16[128,512]{1,0:T(8,128)(2,1)S(1)}, u32[]{:S(2)}, u32[]{:S(2)}) collective-permute-start(bf16[128,512]{1,0:T(8,128)(2,1)S(1)} %shard_map.92.half_ref.refs_0_), channel_id=1, source_target_pairs={{0,2},{1,3},{2,0},{3,1},{4,6},{5,7},{6,4},{7,5},{8,10},{9,11},{10,... | collective-permute-start | bytes 393224 | tf_op jit(solution)/shard_map/ppermute | solution.py:64
  55.3 11.0 %collective-permute-start.12 = (bf16[128,512]{1,0:T(8,128)(2,1)S(1)}, bf16[128,512]{1,0:T(8,128)(2,1)S(1)}, u32[]{:S(2)}, u32[]{:S(2)}) collective-permute-start(bf16[128,512]{1,0:T(8,128)(2,1)S(1)} %shard_map.92.half_ref.refs_0_), channel_id=1, source_target_pairs={{0,16},{8,24},{16,0},{24,8},{1,17},{9,25},{17,1},{25,9},{2,18},{10... | collective-permute-start | bytes 393224 | tf_op jit(solution)/shard_map/ppermute | solution.py:64
  57.5 9.7 %collective-permute-start.18 = (bf16[128,512]{1,0:T(8,128)(2,1)S(1)}, bf16[128,512]{1,0:T(8,128)(2,1)S(1)}, u32[]{:S(2)}, u32[]{:S(2)}) collective-permute-start(bf16[128,512]{1,0:T(8,128)(2,1)S(1)} %shard_map.92.half_ref.refs_0_), channel_id=1, source_target_pairs={{0,1},{1,0},{2,3},{3,2},{4,5},{5,4},{6,7},{7,6},{8,9},{9,8},{10,11... | collective-permute-start | bytes 393224 | tf_op jit(solution)/shard_map/ppermute | solution.py:64
  64.4 2.4 %collective-permute-start.21 = (bf16[128,512]{1,0:T(8,128)(2,1)S(1)}, bf16[128,512]{1,0:T(8,128)(2,1)S(1)}, u32[]{:S(2)}, u32[]{:S(2)}) collective-permute-start(bf16[128,512]{1,0:T(8,128)(2,1)S(1)} %collective-permute-done.17.refs_3_), channel_id=1, source_target_pairs={{0,1},{1,0},{2,3},{3,2},{4,5},{5,4},{6,7},{7,6},{8,9},{9,8},{10,11... | collective-permute-start | bytes 393224 | tf_op jit(solution)/shard_map/ppermute | solution.py:64
  65.9 1.3 %collective-permute-start.20 = (bf16[128,512]{1,0:T(8,128)(2,1)S(1)}, bf16[128,512]{1,0:T(8,128)(2,1)S(1)}, u32[]{:S(2)}, u32[]{:S(2)}) collective-permute-start(bf16[128,512]{1,0:T(8,128)(2,1)S(1)} %collective-permute-done.16.refs_2_), channel_id=1, source_target_pairs={{0,1},{1,0},{2,3},{3,2},{4,5},{5,4},{6,7},{7,6},{8,9},{9,8},{10,11... | collective-permute-start | bytes 393224 | tf_op jit(solution)/shard_map/ppermute | solution.py:64
  65.9 1.5 %collective-permute-start.19 = (bf16[128,512]{1,0:T(8,128)(2,1)S(1)}, bf16[128,512]{1,0:T(8,128)(2,1)S(1)}, u32[]{:S(2)}, u32[]{:S(2)}) collective-permute-start(bf16[128,512]{1,0:T(8,128)(2,1)S(1)} %collective-permute-done.15.refs_1_), channel_id=1, source_target_pairs={{0,1},{1,0},{2,3},{3,2},{4,5},{5,4},{6,7},{7,6},{8,9},{9,8},{10,11... | collective-permute-start | bytes 393224 | tf_op jit(solution)/shard_map/ppermute | solution.py:64
  68.3 7.2 %collective-permute-start.31 = (bf16[384,256]{1,0:T(8,128)(2,1)S(1)}, bf16[384,256]{1,0:T(8,128)(2,1)S(1)}, u32[]{:S(2)}, u32[]{:S(2)}) collective-permute-start(bf16[384,256]{1,0:T(8,128)(2,1)S(1)} %shard_map.94.a_ref), channel_id=1, source_target_pairs={{0,24},{8,16},{16,8},{24,0},{1,25},{9,17},{17,9},{25,1},{2,26},{10... | collective-permute-start | bytes 589832 | tf_op jit(solution)/shard_map/ppermute | solution.py:64
  69.6 10.8 %collective-permute-start.30 = (bf16[384,256]{1,0:T(8,128)(2,1)S(1)}, bf16[384,256]{1,0:T(8,128)(2,1)S(1)}, u32[]{:S(2)}, u32[]{:S(2)}) collective-permute-start(bf16[384,256]{1,0:T(8,128)(2,1)S(1)} %shard_map.94.a_ref), channel_id=1, source_target_pairs={{0,16},{8,24},{16,0},{24,8},{1,17},{9,25},{17,1},{25,9},{2,18},{10... | collective-permute-start | bytes 589832 | tf_op jit(solution)/shard_map/ppermute | solution.py:64
  70.8 10.2 %collective-permute-start.29 = (bf16[384,256]{1,0:T(8,128)(2,1)S(1)}, bf16[384,256]{1,0:T(8,128)(2,1)S(1)}, u32[]{:S(2)}, u32[]{:S(2)}) collective-permute-start(bf16[384,256]{1,0:T(8,128)(2,1)S(1)} %shard_map.94.a_ref), channel_id=1, source_target_pairs={{0,8},{8,0},{16,24},{24,16},{1,9},{9,1},{17,25},{25,17},{2,10},{10... | collective-permute-start | bytes 589832 | tf_op jit(solution)/shard_map/ppermute | solution.py:64
  71.1 11.8 %collective-permute-start.24 = (bf16[128,512]{1,0:T(8,128)(2,1)S(1)}, bf16[128,512]{1,0:T(8,128)(2,1)S(1)}, u32[]{:S(2)}, u32[]{:S(2)}) collective-permute-start(bf16[128,512]{1,0:T(8,128)(2,1)S(1)} %shard_map.93), channel_id=1, source_target_pairs={{0,6},{1,7},{2,4},{3,5},{4,2},{5,3},{6,0},{7,1},{8,14},{9,15},{10,... | collective-permute-start | bytes 393224 | tf_op jit(solution)/shard_map/ppermute | solution.py:64
  73.4 10.7 %collective-permute-start.23 = (bf16[128,512]{1,0:T(8,128)(2,1)S(1)}, bf16[128,512]{1,0:T(8,128)(2,1)S(1)}, u32[]{:S(2)}, u32[]{:S(2)}) collective-permute-start(bf16[128,512]{1,0:T(8,128)(2,1)S(1)} %shard_map.93), channel_id=1, source_target_pairs={{0,4},{1,5},{2,6},{3,7},{4,0},{5,1},{6,2},{7,3},{8,12},{9,13},{10,... | collective-permute-start | bytes 393224 | tf_op jit(solution)/shard_map/ppermute | solution.py:64
  75.5 8.6 %collective-permute-start.22 = (bf16[128,512]{1,0:T(8,128)(2,1)S(1)}, bf16[128,512]{1,0:T(8,128)(2,1)S(1)}, u32[]{:S(2)}, u32[]{:S(2)}) collective-permute-start(bf16[128,512]{1,0:T(8,128)(2,1)S(1)} %shard_map.93), channel_id=1, source_target_pairs={{0,2},{1,3},{2,0},{3,1},{4,6},{5,7},{6,4},{7,5},{8,10},{9,11},{10,... | collective-permute-start | bytes 393224 | tf_op jit(solution)/shard_map/ppermute | solution.py:64
  80.3 12.2 %collective-permute-start.28 = (bf16[4,128,512]{2,1,0:T(8,128)(2,1)S(1)}, bf16[4,128,512]{2,1,0:T(8,128)(2,1)S(1)}, u32[]{:S(2)}, u32[]{:S(2)}) collective-permute-start(bf16[4,128,512]{2,1,0:T(8,128)(2,1)S(1)} %get-tuple-element.77.refs_0_), channel_id=1, source_target_pairs={{0,1},{1,0},{2,3},{3,2},{4,5},{5,4},{6,7},{7,6},{8,9},{9,8},{10,11... | collective-permute-start | bytes 1572872 | tf_op jit(solution)/shard_map/ppermute | solution.py:64
  82.7 4.2 %collective-permute-start.32 = (f32[384,128]{1,0:T(8,128)S(1)}, f32[384,128]{1,0:T(8,128)S(1)}, u32[]{:S(2)}, u32[]{:S(2)}) collective-permute-start(f32[384,128]{1,0:T(8,128)S(1)} %get-tuple-element.79), channel_id=1, source_target_pairs={{0,1},{1,0},{2,3},{3,2},{4,5},{5,4},{6,7},{7,6},{8,9},{9,8},{10,11... | collective-permute-start | bytes 589832 | tf_op jit(solution)/shard_map/ppermute | solution.py:64
  84.2 13.1 %collective-permute-start.27 = (bf16[3,128,512]{2,1,0:T(8,128)(2,1)S(1)}, bf16[3,128,512]{2,1,0:T(8,128)(2,1)S(1)}, u32[]{:S(2)}, u32[]{:S(2)}) collective-permute-start(bf16[3,128,512]{2,1,0:T(8,128)(2,1)S(1)} %pad_maximum_fusion.1.refs_0_), channel_id=1, source_target_pairs={{0,24},{8,16},{16,8},{24,0},{1,25},{9,17},{17,9},{25,1},{2,26},{10... | collective-permute-start | bytes 1179656 | tf_op jit(solution)/shard_map/ppermute | solution.py:64
  85.4 19.2 %collective-permute-start.26 = (bf16[3,128,512]{2,1,0:T(8,128)(2,1)S(1)}, bf16[3,128,512]{2,1,0:T(8,128)(2,1)S(1)}, u32[]{:S(2)}, u32[]{:S(2)}) collective-permute-start(bf16[3,128,512]{2,1,0:T(8,128)(2,1)S(1)} %pad_maximum_fusion.1.refs_0_), channel_id=1, source_target_pairs={{0,16},{8,24},{16,0},{24,8},{1,17},{9,25},{17,1},{25,9},{2,18},{10... | collective-permute-start | bytes 1179656 | tf_op jit(solution)/shard_map/ppermute | solution.py:64
  86.7 18.0 %collective-permute-start.25 = (bf16[3,128,512]{2,1,0:T(8,128)(2,1)S(1)}, bf16[3,128,512]{2,1,0:T(8,128)(2,1)S(1)}, u32[]{:S(2)}, u32[]{:S(2)}) collective-permute-start(bf16[3,128,512]{2,1,0:T(8,128)(2,1)S(1)} %pad_maximum_fusion.1.refs_0_), channel_id=1, source_target_pairs={{0,8},{8,0},{16,24},{24,16},{1,9},{9,1},{17,25},{25,17},{2,10},{10... | collective-permute-start | bytes 1179656 | tf_op jit(solution)/shard_map/ppermute | solution.py:64
  87.0 3.8 %collective-permute-start.33 = (bf16[384,128]{1,0:T(8,128)(2,1)S(1)}, bf16[384,128]{1,0:T(8,128)(2,1)S(1)}, u32[]{:S(2)}, u32[]{:S(2)}) collective-permute-start(bf16[384,128]{1,0:T(8,128)(2,1)S(1)} %get-tuple-element.81), channel_id=1, source_target_pairs={{0,2},{1,3},{2,0},{3,1},{4,6},{5,7},{6,4},{7,5},{8,10},{9,11},{10,... | collective-permute-start | bytes 294920 | tf_op jit(solution)/shard_map/ppermute | solution.py:64
  90.8 5.8 %collective-permute-start.34 = (bf16[384,128]{1,0:T(8,128)(2,1)S(1)}, bf16[384,128]{1,0:T(8,128)(2,1)S(1)}, u32[]{:S(2)}, u32[]{:S(2)}) collective-permute-start(bf16[384,128]{1,0:T(8,128)(2,1)S(1)} %get-tuple-element.83), channel_id=1, source_target_pairs={{0,4},{1,5},{2,6},{3,7},{4,0},{5,1},{6,2},{7,3},{8,12},{9,13},{10,... | collective-permute-start | bytes 294920 | tf_op jit(solution)/shard_map/ppermute | solution.py:64
  104.6 7.4 %collective-permute-start.35 = (bf16[3,128,512]{2,1,0:T(8,128)(2,1)S(1)}, bf16[3,128,512]{2,1,0:T(8,128)(2,1)S(1)}, u32[]{:S(2)}, u32[]{:S(2)}) collective-permute-start(bf16[3,128,512]{2,1,0:T(8,128)(2,1)S(1)} %pad_maximum_fusion.1.refs_0_), channel_id=1, source_target_pairs={{0,1},{1,0},{2,3},{3,2},{4,5},{5,4},{6,7},{7,6},{8,9},{9,8},{10,11... | collective-permute-start | bytes 1179656 | tf_op jit(solution)/shard_map/ppermute | solution.py:64
  105.1 6.9 %collective-permute-start.36 = (bf16[3,128,512]{2,1,0:T(8,128)(2,1)S(1)}, bf16[3,128,512]{2,1,0:T(8,128)(2,1)S(1)}, u32[]{:S(2)}, u32[]{:S(2)}) collective-permute-start(bf16[3,128,512]{2,1,0:T(8,128)(2,1)S(1)} %collective-permute-done.25.refs_1_), channel_id=1, source_target_pairs={{0,1},{1,0},{2,3},{3,2},{4,5},{5,4},{6,7},{7,6},{8,9},{9,8},{10,11... | collective-permute-start | bytes 1179656 | tf_op jit(solution)/shard_map/ppermute | solution.py:64
  105.2 6.8 %collective-permute-start.37 = (bf16[3,128,512]{2,1,0:T(8,128)(2,1)S(1)}, bf16[3,128,512]{2,1,0:T(8,128)(2,1)S(1)}, u32[]{:S(2)}, u32[]{:S(2)}) collective-permute-start(bf16[3,128,512]{2,1,0:T(8,128)(2,1)S(1)} %collective-permute-done.26.refs_2_), channel_id=1, source_target_pairs={{0,1},{1,0},{2,3},{3,2},{4,5},{5,4},{6,7},{7,6},{8,9},{9,8},{10,11... | collective-permute-start | bytes 1179656 | tf_op jit(solution)/shard_map/ppermute | solution.py:64
  105.6 6.4 %collective-permute-start.38 = (bf16[3,128,512]{2,1,0:T(8,128)(2,1)S(1)}, bf16[3,128,512]{2,1,0:T(8,128)(2,1)S(1)}, u32[]{:S(2)}, u32[]{:S(2)}) collective-permute-start(bf16[3,128,512]{2,1,0:T(8,128)(2,1)S(1)} %collective-permute-done.27.refs_3_), channel_id=1, source_target_pairs={{0,1},{1,0},{2,3},{3,2},{4,5},{5,4},{6,7},{7,6},{8,9},{9,8},{10,11... | collective-permute-start | bytes 1179656 | tf_op jit(solution)/shard_map/ppermute | solution.py:64
  105.7 3.8 %collective-permute-start.39 = (f32[384,128]{1,0:T(8,128)S(1)}, f32[384,128]{1,0:T(8,128)S(1)}, u32[]{:S(2)}, u32[]{:S(2)}) collective-permute-start(f32[384,128]{1,0:T(8,128)S(1)} %get-tuple-element.84.own_ref), channel_id=1, source_target_pairs={{0,1},{1,0},{2,3},{3,2},{4,5},{5,4},{6,7},{7,6},{8,9},{9,8},{10,11... | collective-permute-start | bytes 589832 | tf_op jit(solution)/shard_map/ppermute | solution.py:64
